TPU v7x, 32 devices: a whole 2x2x4 slice. The times are simulated.
32 devices in a mesh: seq: 8 (over z, y), exp: 4 (over x, core).
Axes of the slice: x: 2, y: 2, z: 4, core: 2. Of those that a mesh axis runs over, the one named last changes fastest.
Arguments:
- tokens: bfloat16 [32, 1024, 768], P('exp', 'seq'), may hold values from -6 to 6
- segment_ids: int32 [32, 1024], P('exp', 'seq'), may hold values from 0 to 3, never falling along the last dimension, each value on 1 to 512 neighbouring positions
- routes: int32 [32, 1024], P('exp', 'seq'), may hold values from 0 to 3, as said below
- slot_index: int32 [32, 1024], P('exp', 'seq'), may hold values from 0 to 320, as said below
- norm_gain: bfloat16 [768], P('exp'), may hold values from 0.5 to 1.5
- in_proj: bfloat16 [768, 3072], P(None, 'exp'), may hold values from -0.21875 to 0.21875
- conv_weight: bfloat16 [4, 1536], P(None, 'exp'), may hold values from -3 to 3
- conv_bias: bfloat16 [1536], P('exp'), may hold values from -3 to 3
- x_proj: bfloat16 [1536, 80], P('exp'), may hold values from -0.15625 to 0.15625
- dt_proj: bfloat16 [48, 1536], P(None, 'exp'), may hold values from -0.875 to 0.875
- dt_bias: bfloat16 [1536], P('exp'), may hold values from -4.5 to -2.5
- a_log: bfloat16 [1536, 16], P('exp'), may hold values from -9 to 1.5
- d_skip: bfloat16 [1536], P('exp'), may hold values from 0.5 to 1.5
- out_proj: bfloat16 [1536, 768], P('exp'), may hold values from -0.3125 to 0.3125
- moe_gain: bfloat16 [768], P('exp'), may hold values from 0.5 to 1.5
- router: bfloat16 [768, 4], P('exp'), may hold values from -0.15625 to 0.15625
- expert_up: bfloat16 [4, 768, 3072], P('exp'), may hold values from -0.21875 to 0.21875
- expert_down: bfloat16 [4, 3072, 768], P('exp'), may hold values from -0.625 to 0.625
- cotangent: bfloat16 [32, 1024, 768], P('exp', 'seq'), may hold values from -6 to 6
Outputs:
- block_out: bfloat16 [32, 1024, 768], P('exp', 'seq')
- tokens_grad: float32 [32, 1024, 768], P('exp', 'seq')
- norm_gain_grad: float32 [768], P('exp')
- in_proj_grad: float32 [768, 3072], P(None, 'exp')
- conv_weight_grad: float32 [4, 1536], P(None, 'exp')
- conv_bias_grad: float32 [1536], P('exp')
- x_proj_grad: float32 [1536, 80], P('exp')
- dt_proj_grad: float32 [48, 1536], P(None, 'exp')
- dt_bias_grad: float32 [1536], P('exp')
- a_log_grad: float32 [1536, 16], P('exp')
- d_skip_grad: float32 [1536], P('exp')
- out_proj_grad: float32 [1536, 768], P('exp')
- moe_gain_grad: float32 [768], P('exp')
- router_grad: float32 [768, 4], P('exp')
- expert_up_grad: float32 [4, 768, 3072], P('exp')
- expert_down_grad: float32 [4, 3072, 768], P('exp')
Inputs may be any that keep to these rules, and one draw needn't show every extreme that they name: `routes`: the expert that each token goes to. `slot_index`: the rank of the token, counted in order of sequence and then position, among the tokens of its device's block of 8 sequences by 128 positions that go to the same expert; 320 where that rank is 320 or more, and the token is dropped.
All inputs are finite; a program needn't handle non-finite values.
Results may differ from a plain program's by a relative error of at most 0.02.
Values may be sent and summed in bfloat16 or wider, within the bound.
A program may use at most 384 MiB of HBM per device.

v0:
```python
import jax
import jax.numpy as jnp
from jax import lax
from jax.sharding import PartitionSpec as P

epsilon = 1e-05
highest = lax.Precision.HIGHEST
block_len = 8


def passed_along(value, axis, steps):
    count = lax.axis_size(axis)
    initial, last = (max(0, -steps), min(count, count - steps))
    return lax.ppermute(value, axis, [(source, source + steps) for source in range(initial, last)])


def carried_in(x, axis, combine, identity):
    peers, position = (lax.axis_size(axis), lax.axis_index(axis))
    everything = jax.tree.map(
        lambda part, kind: lax.all_gather(part.astype(kind), axis), x, (jnp.bfloat16, jnp.bfloat16)
    )
    start = jax.tree.map(
        lambda part, zero: jnp.broadcast_to(jnp.asarray(zero, part.dtype), part.shape), x, identity
    )

    def carried_hop(k, before):
        reached = k < position
        new = combine(
            before, jax.tree.map(lambda part, own: part[k].astype(own.dtype), everything, x)
        )
        return jax.tree.map(lambda a, b: jnp.where(reached, a, b), new, before)

    return lax.fori_loop(0, peers, carried_hop, start)


def entering(x, axis, combine, identity):
    peers, position = (lax.axis_size(axis), lax.axis_index(axis))
    everything = jax.tree.map(
        lambda part, kind: lax.all_gather(part.astype(kind), axis),
        x,
        jax.tree.map(lambda a: jnp.bfloat16 if a.dtype == jnp.float32 else a.dtype, x),
    )
    start = jax.tree.map(
        lambda part, zero: jnp.broadcast_to(jnp.asarray(zero, part.dtype), part.shape), x, identity
    )

    def entering_hop(k, before):
        at = peers - 1 - k
        reached = at > position
        new = combine(
            before, jax.tree.map(lambda part, own: part[at].astype(own.dtype), everything, x)
        )
        return jax.tree.map(lambda a, b: jnp.where(reached, a, b), new, before)

    return lax.fori_loop(0, peers, entering_hop, start)


def rms_norm(values, gain):
    return values * lax.rsqrt(jnp.mean(values * values, -1, keepdims=True) + epsilon) * gain


def conv_piece(ext_rows, kernel, shift_bias, ext_ids):
    kernel_len = kernel.shape[0]
    span_len = ext_rows.shape[1] - kernel_len + 1
    current = ext_ids[:, kernel_len - 1 :]
    total = shift_bias + jnp.zeros_like(ext_rows[:, kernel_len - 1 :])
    for offset in range(kernel_len):
        match = (ext_ids[:, offset : offset + span_len] == current).astype(jnp.float32)
        total = total + kernel[offset] * ext_rows[:, offset : offset + span_len] * match[:, :, None]
    return jax.nn.silu(total)


def rate_piece(rate_pre, rate_bias, log_decay):
    return (jax.nn.softplus(rate_pre + rate_bias), -jnp.exp(log_decay))


def tail_piece(scan_rows, conv_rows, gate_pre, skip_gain):
    return (scan_rows + skip_gain * conv_rows) * jax.nn.silu(gate_pre)


def scan_step(state, item, a_mat):
    step_t, b_t, c_t, x_t, keep_t = item
    decay = jnp.exp(step_t[:, :, None] * a_mat) * keep_t[:, None, None]
    state = decay * state + (step_t * x_t)[:, :, None] * b_t[:, None, :]
    return (state, jnp.sum(state * c_t[:, None, :], -1))


def local_scan(start_state, step_vals, b_vals, c_vals, conv_vals, keep_mask, a_mat):
    part_len = step_vals.shape[1]

    def to_blocks(values):
        values = jnp.moveaxis(values, 1, 0)
        return values.reshape((part_len // block_len, block_len) + values.shape[1:])

    items = tuple((to_blocks(v) for v in (step_vals, b_vals, c_vals, conv_vals, keep_mask)))

    def run_block(carry, item):
        results = []
        for position in range(block_len):
            carry, y_step = scan_step(carry, tuple((v[position] for v in item)), a_mat)
            results.append(y_step)
        return (carry, jnp.stack(results))

    end_state, outputs = lax.scan(jax.checkpoint(run_block), start_state, items)
    return (jnp.moveaxis(outputs.reshape((part_len,) + outputs.shape[2:]), 0, 1), end_state)


def chain_combine(earlier, later):
    return (earlier[0] * later[0], later[0] * earlier[1] + later[1])


def local(
    tokens,
    segment_ids,
    routes,
    slot_index,
    norm_gain,
    in_proj,
    conv_weight,
    conv_bias,
    x_proj,
    dt_proj,
    dt_bias,
    a_log,
    d_skip,
    out_proj,
    moe_gain,
    router,
    expert_up,
    expert_down,
    cotangent,
):
    gathered = (
        lax.all_gather(norm_gain, "exp", axis=0, tiled=True),
        lax.all_gather(in_proj, "exp", axis=1, tiled=True),
        lax.all_gather(conv_weight, "exp", axis=1, tiled=True),
        lax.all_gather(conv_bias, "exp", axis=0, tiled=True),
        lax.all_gather(x_proj, "exp", axis=0, tiled=True),
        lax.all_gather(dt_proj, "exp", axis=1, tiled=True),
        lax.all_gather(dt_bias, "exp", axis=0, tiled=True),
        lax.all_gather(a_log, "exp", axis=0, tiled=True),
        lax.all_gather(d_skip, "exp", axis=0, tiled=True),
        lax.all_gather(out_proj, "exp", axis=0, tiled=True),
        lax.all_gather(moe_gain, "exp", axis=0, tiled=True),
        lax.all_gather(router, "exp", axis=0, tiled=True),
    )
    (
        gain_one,
        w_in,
        w_conv,
        b_conv,
        w_x,
        w_dt,
        b_dt,
        log_decay,
        skip_gain,
        w_out,
        gain_two,
        w_router,
    ) = gathered
    seq_count, part_len, width = tokens.shape
    inner_width = w_out.shape[0]
    rank_width = w_dt.shape[0]
    state_width = log_decay.shape[1]
    kernel_len = w_conv.shape[0]
    expert_total = w_router.shape[1]
    local_experts = expert_up.shape[0]
    source_count = expert_total // local_experts
    row_count = seq_count * part_len
    capacity = 5 * row_count // (4 * expert_total)
    token_rows = tokens.reshape(row_count, width).astype(jnp.float32)
    normed, norm_one_back = jax.vjp(rms_norm, token_rows, gain_one.astype(jnp.float32))
    normed_low = normed.astype(jnp.bfloat16)
    projected = jnp.dot(normed_low, w_in, preferred_element_type=jnp.float32)
    conv_input = (
        projected[:, :inner_width].astype(jnp.bfloat16).reshape(seq_count, part_len, inner_width)
    )
    gate_pre = projected[:, inner_width:]
    doc_ids = (segment_ids + 1).astype(jnp.float32)
    edge_start = part_len - kernel_len + 1
    edge_rows, edge_ids = passed_along(
        (conv_input[:, edge_start:], doc_ids[:, edge_start:].astype(jnp.bfloat16)), "seq", 1
    )
    ext_rows = jnp.concatenate([edge_rows, conv_input], 1).astype(jnp.float32)
    ext_ids = jnp.concatenate([edge_ids.astype(jnp.float32), doc_ids], 1)
    keep_mask = (ext_ids[:, kernel_len - 2 : kernel_len - 2 + part_len] == doc_ids).astype(
        jnp.float32
    )
    conv_out, conv_back = jax.vjp(
        lambda rows_in, kernel, shift_bias: conv_piece(rows_in, kernel, shift_bias, ext_ids),
        ext_rows,
        w_conv.astype(jnp.float32),
        b_conv.astype(jnp.float32),
    )
    conv_low = conv_out.astype(jnp.bfloat16).reshape(row_count, inner_width)
    conv_value = conv_low.astype(jnp.float32)
    mixed_proj = jnp.dot(conv_low, w_x, preferred_element_type=jnp.float32)
    rate_low = mixed_proj[:, :rank_width].astype(jnp.bfloat16)
    b_rows = mixed_proj[:, rank_width : rank_width + state_width]
    c_rows = mixed_proj[:, rank_width + state_width :]
    rate_pre = jnp.dot(rate_low, w_dt, preferred_element_type=jnp.float32)
    (step_size, a_mat), rate_back = jax.vjp(
        rate_piece, rate_pre, b_dt.astype(jnp.float32), log_decay.astype(jnp.float32)
    )

    def by_seq(values):
        return values.reshape((seq_count, part_len) + values.shape[1:])

    step_seq = by_seq(step_size)
    b_seq = by_seq(b_rows)
    c_seq = by_seq(c_rows)
    conv_seq = by_seq(conv_value)
    zero_state = jnp.zeros((seq_count, inner_width, state_width), jnp.float32)
    unit_state = jnp.ones_like(zero_state)
    decay_total = (
        jnp.exp(a_mat * jnp.sum(step_seq, 1)[:, :, None]) * jnp.prod(keep_mask, 1)[:, None, None]
    )
    unused_rows, local_end = local_scan(
        zero_state, step_seq, b_seq, c_seq, conv_seq, keep_mask, a_mat
    )
    carried = carried_in((decay_total, local_end), "seq", chain_combine, (unit_state, zero_state))
    (scan_out, state_end), scan_back = jax.vjp(
        lambda start_state, step_vals, b_vals, c_vals, conv_vals, decay_rates: local_scan(
            start_state, step_vals, b_vals, c_vals, conv_vals, keep_mask, decay_rates
        ),
        carried[1],
        step_seq,
        b_seq,
        c_seq,
        conv_seq,
        a_mat,
    )
    mixed_rows, tail_back = jax.vjp(
        tail_piece,
        scan_out.reshape(row_count, inner_width),
        conv_value,
        gate_pre,
        skip_gain.astype(jnp.float32),
    )
    mixed_low = mixed_rows.astype(jnp.bfloat16)
    hidden_one = token_rows + jnp.dot(mixed_low, w_out, preferred_element_type=jnp.float32)
    normed_two, norm_two_back = jax.vjp(rms_norm, hidden_one, gain_two.astype(jnp.float32))
    moe_low = normed_two.astype(jnp.bfloat16)
    logits = jnp.dot(moe_low, w_router, preferred_element_type=jnp.float32)
    router_prob = jax.nn.softmax(logits, -1)
    route_rows = routes.reshape(row_count)
    onehot = (route_rows[:, None] == jnp.arange(expert_total)[None, :]).astype(jnp.float32)
    gate_prob = jnp.sum(router_prob * onehot, -1)
    slot_rows = slot_index.reshape(row_count)
    target = jnp.where(
        slot_rows < capacity, route_rows * capacity + slot_rows, expert_total * capacity
    )
    send_buffer = (
        jnp.zeros((expert_total * capacity, width), jnp.bfloat16)
        .at[target]
        .set(moe_low, mode="drop")
        .reshape(expert_total, capacity, width)
    )
    received = lax.all_to_all(send_buffer, "exp", split_axis=0, concat_axis=0, tiled=True)
    slot_len = received.shape[1]
    grouped = received.reshape(source_count, local_experts, slot_len, width)
    pre_act = jnp.einsum("sjcd,jdf->sjcf", grouped, expert_up, preferred_element_type=jnp.float32)
    active = jax.nn.gelu(pre_act, approximate=False).astype(jnp.bfloat16)
    result = jnp.einsum(
        "sjcf,jfd->sjcd", active, expert_down, preferred_element_type=jnp.float32
    ).astype(jnp.bfloat16)
    expert_out = result.reshape(received.shape)
    pre_kept = pre_act.reshape(expert_total, slot_len, -1)
    returned = lax.all_to_all(expert_out, "exp", split_axis=0, concat_axis=0, tiled=True)
    expert_tok = jnp.take(
        returned.reshape(expert_total * capacity, width), target, axis=0, mode="fill", fill_value=0
    ).astype(jnp.float32)
    block_out = (
        (hidden_one + gate_prob[:, None] * expert_tok).astype(jnp.bfloat16).reshape(tokens.shape)
    )
    grad_rows = cotangent.reshape(row_count, width).astype(jnp.float32)
    gate_grad = jnp.sum(grad_rows * expert_tok, -1)
    out_grad = (gate_prob[:, None] * grad_rows).astype(jnp.bfloat16)
    grad_buffer = (
        jnp.zeros((expert_total * capacity, width), jnp.bfloat16)
        .at[target]
        .set(out_grad, mode="drop")
        .reshape(expert_total, capacity, width)
    )
    grad_recv = lax.all_to_all(grad_buffer, "exp", split_axis=0, concat_axis=0, tiled=True)
    grad_four = grad_recv.reshape(source_count, local_experts, capacity, width)
    pre_four = pre_kept.reshape(source_count, local_experts, capacity, -1)
    rows_four = received.reshape(source_count, local_experts, capacity, width)
    act_grad = jnp.einsum(
        "sjcd,jfd->sjcf", grad_four, expert_down, preferred_element_type=jnp.float32
    )
    active_again, gelu_back = jax.vjp(
        lambda values: jax.nn.gelu(values, approximate=False), pre_four
    )
    pre_grad = gelu_back(act_grad)[0].astype(jnp.bfloat16)
    active_low = active_again.astype(jnp.bfloat16)
    down_grad = jnp.einsum(
        "sjcf,sjcd->jfd", active_low, grad_four, preferred_element_type=jnp.float32
    )
    up_grad = jnp.einsum("sjcd,sjcf->jdf", rows_four, pre_grad, preferred_element_type=jnp.float32)
    rows_grad = (
        jnp.einsum("sjcf,jdf->sjcd", pre_grad, expert_up, preferred_element_type=jnp.float32)
        .astype(jnp.bfloat16)
        .reshape(expert_total, capacity, width)
    )
    rows_back = lax.all_to_all(rows_grad, "exp", split_axis=0, concat_axis=0, tiled=True)
    expert_in_grad = jnp.take(
        rows_back.reshape(expert_total * capacity, width), target, axis=0, mode="fill", fill_value=0
    ).astype(jnp.float32)
    logit_grad = router_prob * (onehot - gate_prob[:, None]) * gate_grad[:, None]
    router_grad = jnp.dot(moe_low.astype(jnp.float32).T, logit_grad, precision=highest)
    moe_in_grad = (
        jnp.dot(logit_grad, w_router.astype(jnp.float32).T, precision=highest) + expert_in_grad
    )
    hidden_part, gain_two_grad = norm_two_back(moe_in_grad)
    hidden_grad = grad_rows + hidden_part
    branch_grad = hidden_grad.astype(jnp.bfloat16)
    out_proj_grad = jnp.dot(mixed_low.T, branch_grad, preferred_element_type=jnp.float32)
    mixed_grad = jnp.dot(branch_grad, w_out.T, preferred_element_type=jnp.float32)
    scan_grad, conv_tail_grad, gate_pre_grad, skip_grad = tail_back(mixed_grad)
    grads_local = scan_back((scan_grad.reshape(seq_count, part_len, inner_width), zero_state))
    carried_back = entering(
        (decay_total, grads_local[0]), "seq", chain_combine, (unit_state, zero_state)
    )
    grads_carry = scan_back((jnp.zeros_like(scan_out), carried_back[1]))
    step_grad = (grads_local[1] + grads_carry[1]).reshape(row_count, inner_width)
    b_grad = (grads_local[2] + grads_carry[2]).reshape(row_count, state_width)
    c_grad = (grads_local[3] + grads_carry[3]).reshape(row_count, state_width)
    conv_scan_grad = (grads_local[4] + grads_carry[4]).reshape(row_count, inner_width)
    a_grad = grads_local[5] + grads_carry[5]
    rate_pre_grad, dt_bias_grad, a_log_grad = rate_back((step_grad, a_grad))
    rate_pre_low = rate_pre_grad.astype(jnp.bfloat16)
    dt_proj_grad = jnp.dot(rate_low.T, rate_pre_low, preferred_element_type=jnp.float32)
    rate_grad = jnp.dot(rate_pre_low, w_dt.T, preferred_element_type=jnp.float32)
    mixed_proj_grad = jnp.concatenate([rate_grad, b_grad, c_grad], -1).astype(jnp.bfloat16)
    x_proj_grad = jnp.dot(conv_low.T, mixed_proj_grad, preferred_element_type=jnp.float32)
    conv_grad = (
        conv_tail_grad
        + conv_scan_grad
        + jnp.dot(mixed_proj_grad, w_x.T, preferred_element_type=jnp.float32)
    )
    ext_grad, conv_weight_grad, conv_bias_grad = conv_back(
        conv_grad.reshape(seq_count, part_len, inner_width)
    )
    edge_back = passed_along(ext_grad[:, : kernel_len - 1].astype(jnp.bfloat16), "seq", -1).astype(
        jnp.float32
    )
    input_grad = ext_grad[:, kernel_len - 1 :]
    input_grad = input_grad.at[:, edge_start:].add(edge_back)
    proj_grad = jnp.concatenate(
        [input_grad.reshape(row_count, inner_width), gate_pre_grad], -1
    ).astype(jnp.bfloat16)
    in_proj_grad = jnp.dot(normed_low.T, proj_grad, preferred_element_type=jnp.float32)
    normed_grad = jnp.dot(proj_grad, w_in.T, preferred_element_type=jnp.float32)
    token_part, gain_one_grad = norm_one_back(normed_grad)
    tokens_grad = (hidden_grad + token_part).reshape(tokens.shape)
    whole = lax.psum(
        (
            gain_one_grad,
            in_proj_grad,
            conv_weight_grad,
            conv_bias_grad,
            x_proj_grad,
            dt_proj_grad,
            dt_bias_grad,
            a_log_grad,
            skip_grad,
            out_proj_grad,
            gain_two_grad,
            router_grad,
        ),
        ("seq", "exp"),
    )
    position = lax.axis_index("exp")
    exp_count = lax.axis_size("exp")

    def own_share(full, axis_dim):
        share_len = full.shape[axis_dim] // exp_count
        return lax.dynamic_slice_in_dim(full, position * share_len, share_len, axis_dim)

    share_dims = (0, 1, 1, 0, 0, 1, 0, 0, 0, 0, 0, 0)
    weight_sums = tuple((own_share(whole[number], share_dims[number]) for number in range(12)))
    expert_sums = (
        lax.psum(up_grad.astype(jnp.bfloat16), "seq").astype(jnp.float32),
        lax.psum(down_grad.astype(jnp.bfloat16), "seq").astype(jnp.float32),
    )
    return (
        block_out,
        tokens_grad,
        weight_sums[0],
        weight_sums[1],
        weight_sums[2],
        weight_sums[3],
        weight_sums[4],
        weight_sums[5],
        weight_sums[6],
        weight_sums[7],
        weight_sums[8],
        weight_sums[9],
        weight_sums[10],
        weight_sums[11],
        expert_sums[0],
        expert_sums[1],
    )


def solution(mesh):
    in_specs = (
        P("exp", "seq", None),
        P("exp", "seq"),
        P("exp", "seq"),
        P("exp", "seq"),
        P("exp"),
        P(None, "exp"),
        P(None, "exp"),
        P("exp"),
        P("exp", None),
        P(None, "exp"),
        P("exp"),
        P("exp", None),
        P("exp"),
        P("exp", None),
        P("exp"),
        P("exp", None),
        P("exp", None, None),
        P("exp", None, None),
        P("exp", "seq", None),
    )
    out_specs = (
        P("exp", "seq", None),
        P("exp", "seq", None),
        P("exp"),
        P(None, "exp"),
        P(None, "exp"),
        P("exp"),
        P("exp", None),
        P(None, "exp"),
        P("exp"),
        P("exp", None),
        P("exp"),
        P("exp", None),
        P("exp"),
        P("exp", None),
        P("exp", None, None),
        P("exp", None, None),
    )
    return jax.shard_map(local, mesh=mesh, in_specs=in_specs, out_specs=out_specs, check_vma=False)
```

profile of v0, /device:TPU:0, one launch (start us, length us, event | category | flops | bytes accessed | tf_op | source)
XLA Modules:
  0.0 2074.4 jit_solution(4944522527399566457)
XLA Ops:
  89.2 8.6 convert_bitcast_fusion
  114.7 9.2 copy.60
  124.0 67.2 %while.108 = (s32[]{:T(128)}, f32[8,1536,16]{1,2,0:T(8,128)S(1)}, f32[16,8,8,1536]{3,2,1,0:T(8,128)}, f32[1536,16]{0,1:T(8,128)S(1)}, f32[16,8,8]{2,1,0:T(8,128)...) while((s32[]{:T(128)}, f32[8,1536,16]{1,2,0:T(8,128)S(1)}, ...), condition=%wide.region_4.5_spmd.clone, body=%wide.region_3.4_spmd.clone.sunk | while | flops 8159242 | bytes 4437591 | solution.py:104
  199.9 54.3 %all-gather.18.cloned.1.call-done = bf16[64,1536,16]{1,2,0:T(8,128)(2,1)} async-done(((bf16[8,1536,16]{1,2,0:T(8,128)(2,1)}), bf16[64,1536,16]{1,2,0:T(8,128)(2,1)}) %all-gather.18.cloned.1.call-update) | async-done | bytes 3145744 | tf_op jit(solution)/shard_map/all_gather | solution.py:20
  254.2 61.9 %all-gather.14.cloned.1.call-done = bf16[8,8,1536,16]{2,3,1,0:T(8,128)(2,1)} async-done(((bf16[1,8,1536,16]{2,3,1,0:T(8,128)(2,1)}), bf16[8,8,1536,16]{2,3,1,0:T(8,128)(2,1)}) %all-gather.14.cloned.1.call-update) | async-done | bytes 3145744 | tf_op jit(solution)/shard_map/all_gather | solution.py:20
  316.1 14.7 while.109
  334.3 145.3 %while.107 = (s32[]{:T(128)}, f32[8,1536,16]{1,2,0:T(8,128)S(1)}, f32[16,8,8,1536]{3,2,1,0:T(8,128)}, f32[16,8,1536,16]{2,3,1,0:T(8,128)}, f32[16,8,8,1536]{3,2,...) while((s32[]{:T(128)}, f32[8,1536,16]{1,2,0:T(8,128)S(1)}, ...), condition=%wide.region_16.17_spmd, body=%wide.region_7.16_spmd.sunk | while | flops 14942217 | bytes 15659749 | solution.py:104
  512.0 25.2 %all-gather.5 = bf16[4,192,4]{1,2,0:T(4,128)(2,1)S(1)} all-gather(bf16[1,192,4]{1,2,0:T(4,128)(2,1)S(1)} %bitcast.1226), channel_id=1, replica_groups=mesh['seq'=8,'exp'=4] {'exp'}, dimensions={0}, use_global_device_ids=true | all-gather | bytes 7680 | tf_op jit(solution)/shard_map/all_gather | solution.py:145
  539.5 7.6 scatter_custom_fusion.1
  550.8 12.2 fusion.118
  563.0 12.1 all-to-all-done.2
  575.1 43.4 %fusion.83 = bf16[4,1,320,3072]{3,2,0,1:T(8,128)(2,1)S(1)} fusion(f32[4,320,3072]{2,1,0:T(8,128)} %fusion.118, bf16[4,320,768]{2,1,0:T(8,128)(2,1)S(1)} %all-to-all-done.2, bf16[1,3072,768]{2,1,0:T(8,128)(2,1)} %param.52), kind=kOutput, calls=%fused_computation.506 | convolution fusion | flops 6322913280 | bytes 30277632 | tf_op jit(solution)/shard_map/sjcd,jfd->sjcf/dot_general | solution.py:289
  621.7 7.5 fusion.140
  633.2 43.5 %fusion.137 = bf16[4,320,768]{2,1,0:T(8,128)(2,1)} fusion(bf16[1,3072,768]{2,1,0:T(8,128)(2,1)} %param.52, f32[4,320,3072]{2,1,0:T(8,128)} %fusion.118), kind=kOutput, calls=%fused_computation.604 | convolution fusion | flops 6296371200 | bytes 22413312 | tf_op jit(solution)/shard_map/sjcf,jfd->sjcd/dot_general | solution.py:264
  686.7 18.8 all-to-all-done.1
  705.6 7.5 gather_fusion
  725.3 10.6 fusion.101
  750.8 311.5 %while.110 = (s32[]{:T(128)}, f32[1536,16]{0,1:T(8,128)S(1)}, f32[8,1536,16]{1,2,0:T(8,128)S(1)}, f32[16,8,8,1536]{3,2,1,0:T(8,128)}, f32[16,8,8,16]{3,2,1,0:T(8...) while((s32[]{:T(128)}, f32[1536,16]{0,1:T(8,128)S(1)}, ...), condition=%wide.region_66.68_spmd.clone, body=%wide.region_25.67_spmd.clone.sunk | while | flops 44863492 | bytes 36012544 | solution.py:104
  1063.2 42.1 %fusion.123 = bf16[1,3072,768]{2,1,0:T(8,128)(2,1)} fusion(bf16[4,320,768]{2,1,0:T(8,128)(2,1)} %copy-done.32, f32[4,320,3072]{2,1,0:T(8,128)} %fusion.118), kind=kOutput, calls=%fused_computation.578 | convolution fusion | flops 6297747456 | bytes 22413312 | tf_op jit(solution)/shard_map/sjcf,sjcd->jfd/dot_general | solution.py:297
  1105.3 9.6 fusion.120
  1115.0 7.7 fusion.158
  1122.7 14.9 while.111
  1144.7 287.1 %while.112 = (s32[]{:T(128)}, f32[1536,16]{0,1:T(8,128)S(1)}, f32[8,1536,16]{1,2,0:T(8,128)S(1)}, f32[16,8,8,1536]{3,2,1,0:T(8,128)}, f32[16,8,8,16]{3,2,1,0:T(8...) while((s32[]{:T(128)}, f32[1536,16]{0,1:T(8,128)S(1)}, ...), condition=%wide.region_110.112_spmd.clone, body=%wide.region_69.111_spmd.clone.sunk | while | flops 44666880 | bytes 34103804 | solution.py:104
  1457.3 8.0 fusion.197
  1471.3 9.6 multiply_reduce_fusion.91
  1480.9 7.7 multiply_multiply_fusion.17
  1488.6 8.2 pad_add_fusion
  1505.0 10.2 fusion.124
  1517.5 10.8 fusion.134
  1528.3 42.8 %all-reduce.74 = (f32[768]{0:T(1024)S(1)}, f32[4,1536]{1,0:T(4,128)S(1)}, f32[1536]{0:T(1024)S(1)}, f32[1536]{0:T(1024)S(1)}, f32[1536]{0:T(1024)S(1)}, /*index=5*/f32[768]{0:T(1024)S(1)}, f32[768,4]{0,1:T(4,128)S(1)}) all-reduce(f32[768]{0:T(1024)S(1)} %get-tuple-element.1280, ...), channel_id=1, replica_groups=mesh['seq'=8,'exp'=4] {'seq','exp'}, use_global_device_ids=true, to_apply=%region_113.115 | all-reduce | flops 15360 | bytes 122880 | tf_op jit(solution)/shard_map/psum | solution.py:357
  1581.0 7.6 convert_element_type.247
  1593.1 464.3 %all-reduce.81.cloned.1.call-done = (f32[768,3072]{1,0:T(8,128)}, f32[1536,80]{0,1:T(8,128)}, f32[48,1536]{1,0:T(8,128)}, f32[1536,16]{0,1:T(8,128)}, f32[1536,768]{1,0:T(8,128)}) async-done(((f32[768,3072]{1,0:T(8,128)}, f32[1536,80]{0,1:T(8,128)}, f32[48,1536]{1,0:T(8,128)}, f32[1536,16]{0,1:T(8,128)}, f32[1536,768]{1,0:T(8,128)}), (f32[768,3072]{1,0:T(8,128)}, f32[1536,80]{0,1:T(8,128)}, ...) | async-done | bytes 15040528 | tf_op jit(solution)/shard_map/psum | solution.py:357
  (1609 shorter events, 1099.2 us)
Async XLA Ops:
  7.2 60.8 %all-gather.12.cloned.1.call-start = ((), (), s32[]{:S(2)}) async-start(), calls=%async_computation.4 | async-start | bytes 5898240 | tf_op jit(solution)/shard_map/all_gather | solution.py:135
  7.9 246.3 %all-gather.18.cloned.1.call-start = ((), (), s32[]{:S(2)}) async-start(), calls=%async_computation.7 | async-start | bytes 3538944 | tf_op jit(solution)/shard_map/all_gather | solution.py:20
  8.7 58.4 %collective-permute-start.1 = (bf16[8,3]{1,0:T(8,128)(2,1)S(1)}, bf16[8,3]{1,0:T(8,128)(2,1)S(1)}, u32[]{:S(2)}, u32[]{:S(2)}) collective-permute-start(bf16[8,3]{1,0:T(8,128)(2,1)S(1)} %slice.1142), channel_id=1, source_target_pairs={{0,4},{4,8},{8,12},{12,16},{16,20},{20,24},{24,28},{1,5},{5,9},{9,... | collective-permute-start | bytes 152 | tf_op jit(solution)/shard_map/ppermute | solution.py:14
  53.7 46.0 %copy-start.35 = (bf16[48,1536]{1,0:T(8,128)(2,1)}, bf16[48,1536]{1,0:T(8,128)(2,1)S(1)}, u32[]{:S(2)}) copy-start(bf16[48,1536]{1,0:T(8,128)(2,1)S(1)} %all_gather.60) | copy-start | bytes 442372
  80.9 6.3 collective-permute-start
  123.9 68.1 %copy-start.76 = (f32[8,1536]{1,0:T(8,128)S(1)}, f32[8,1536]{1,0:T(8,128)}, u32[]{:S(2)}) copy-start(f32[8,1536]{1,0:T(8,128)} %get-tuple-element.1680) | copy-start | bytes 147460
  123.9 68.1 %copy-start.92 = (f32[8]{0:T(128)S(1)}, f32[8]{0:T(128)}, u32[]{:S(2)}) copy-start(f32[8]{0:T(128)} %get-tuple-element.1447) | copy-start | bytes 100
  123.9 69.7 %copy-start.95 = (bf16[384]{0:T(512)(128)(2,1)S(1)}, bf16[384]{0:T(512)(128)(2,1)}, u32[]{:S(2)}) copy-start(bf16[384]{0:T(512)(128)(2,1)} %param.47) | copy-start | bytes 2308
  123.9 74.9 %copy-start.94 = (bf16[768]{0:T(1024)(128)(2,1)S(1)}, bf16[768]{0:T(1024)(128)(2,1)}, u32[]{:S(2)}) copy-start(bf16[768]{0:T(1024)(128)(2,1)} %get-tuple-element.1413) | copy-start | bytes 4612
  123.9 74.9 %copy-start.43 = (s32[8,128]{1,0:T(8,128)S(1)}, s32[8,128]{1,0:T(8,128)}, u32[]{:S(2)}) copy-start(s32[8,128]{1,0:T(8,128)} %param.37) | copy-start | bytes 12292
  123.9 74.9 %copy-start.85 = (s32[8,128]{1,0:T(8,128)S(1)}, s32[8,128]{1,0:T(8,128)}, u32[]{:S(2)}) copy-start(s32[8,128]{1,0:T(8,128)} %param.38) | copy-start | bytes 12292
  123.9 74.9 %copy-start.40 = (f32[2,8,8,128]{3,1,2,0:T(8,128)S(1)}, f32[2,8,8,128]{3,1,2,0:T(8,128)}, u32[]{:S(2)}) copy-start(f32[2,8,8,128]{3,1,2,0:T(8,128)} %get-tuple-element.1672) | copy-start | bytes 196612
  191.2 124.9 %copy-start.1 = (f32[1536,16]{0,1:T(8,128)}, f32[1536,16]{0,1:T(8,128)S(1)}, u32[]{:S(2)}) copy-start(f32[1536,16]{0,1:T(8,128)S(1)} %get-tuple-element.2982) | copy-start | bytes 294916
  192.0 124.1 %all-gather.14.cloned.1.call-start = ((), (), s32[]{:S(2)}) async-start(), calls=%async_computation.5 | async-start | bytes 3538944 | tf_op jit(solution)/shard_map/all_gather | solution.py:20
  193.0 301.5 %all-gather.16.cloned.1.call-start = ((), (), s32[]{:S(2)}) async-start(), calls=%async_computation.6 | async-start | bytes 2949120 | tf_op jit(solution)/shard_map/all_gather | solution.py:143
  198.8 287.5 %copy-start.55 = (f32[1536]{0:T(1024)}, f32[1536]{0:T(1024)S(1)}, u32[]{:S(2)}) copy-start(f32[1536]{0:T(1024)S(1)} %reshape.1721) | copy-start | bytes 18436
  198.8 338.5 %copy-start.51 = (f32[768]{0:T(1024)}, f32[768]{0:T(1024)S(1)}, u32[]{:S(2)}) copy-start(f32[768]{0:T(1024)S(1)} %convert_element_type.228) | copy-start | bytes 9220
  507.5 39.5 %all-to-all-start = ((bf16[4,320,768]{2,1,0:T(8,128)(2,1)}), bf16[4,320,768]{2,1,0:T(8,128)(2,1)}, u32[]{:S(2)}, u32[]{:S(2)}) async-start(bf16[4,320,768]{2,1,0:T(8,128)(2,1)} %bitcast.1168), calls=%async_computation | async-start | bytes 3932160 | tf_op jit(solution)/shard_map/all_to_all | solution.py:259
  547.0 28.1 %all-to-all-start.2 = ((bf16[4,320,768]{2,1,0:T(8,128)(2,1)}), bf16[4,320,768]{2,1,0:T(8,128)(2,1)S(1)}, u32[]{:S(2)}, u32[]{:S(2)}) async-start(bf16[4,320,768]{2,1,0:T(8,128)(2,1)} %bitcast.97), calls=%async_computation.2 | async-start | bytes 3932160 | tf_op jit(solution)/shard_map/all_to_all | solution.py:285
  575.1 43.4 %copy-start.32 = (bf16[4,320,768]{2,1,0:T(8,128)(2,1)}, bf16[4,320,768]{2,1,0:T(8,128)(2,1)S(1)}, u32[]{:S(2)}) copy-start(bf16[4,320,768]{2,1,0:T(8,128)(2,1)S(1)} %all-to-all-done.2) | copy-start | bytes 5898244
  575.1 46.6 %copy-start.96 = (bf16[1,768,3072]{2,1,0:T(8,128)(2,1)S(1)}, bf16[1,768,3072]{2,1,0:T(8,128)(2,1)}, u32[]{:S(2)}) copy-start(bf16[1,768,3072]{2,1,0:T(8,128)(2,1)} %param.51) | copy-start | bytes 14155780
  629.2 47.6 %all-to-all-start.3 = ((bf16[4,320,768]{2,1,0:T(8,128)(2,1)}), bf16[4,320,768]{2,1,0:T(8,128)(2,1)S(1)}, u32[]{:S(2)}, u32[]{:S(2)}) async-start(bf16[4,320,768]{2,1,0:T(8,128)(2,1)} %fusion.140), calls=%async_computation.3 | async-start | bytes 3932160 | tf_op jit(solution)/shard_map/all_to_all | solution.py:306
  633.2 48.1 %copy-start.44 = (s32[8,128]{1,0:T(8,128)S(1)}, s32[8,128]{1,0:T(8,128)}, u32[]{:S(2)}) copy-start(s32[8,128]{1,0:T(8,128)} %param.37) | copy-start | bytes 12292
  633.2 48.1 %copy-start.86 = (s32[8,128]{1,0:T(8,128)S(1)}, s32[8,128]{1,0:T(8,128)}, u32[]{:S(2)}) copy-start(s32[8,128]{1,0:T(8,128)} %param.38) | copy-start | bytes 12292
  676.8 28.8 %all-to-all-start.1 = ((bf16[4,320,768]{2,1,0:T(8,128)(2,1)}), bf16[4,320,768]{2,1,0:T(8,128)(2,1)}, u32[]{:S(2)}, u32[]{:S(2)}) async-start(bf16[4,320,768]{2,1,0:T(8,128)(2,1)} %fusion.137), calls=%async_computation.1 | async-start | bytes 3932160 | tf_op jit(solution)/shard_map/all_to_all | solution.py:269
  681.2 441.5 %all-gather.20.cloned.1.call-start = ((), (), s32[]{:S(2)}) async-start(), calls=%async_computation.8 | async-start | bytes 3538944 | tf_op jit(solution)/shard_map/all_gather | solution.py:39
  1062.3 43.0 %copy-start.22 = (f32[1536,16]{0,1:T(8,128)}, f32[1536,16]{0,1:T(8,128)S(1)}, u32[]{:S(2)}) copy-start(f32[1536,16]{0,1:T(8,128)S(1)} %get-tuple-element.997) | copy-start | bytes 294916
  1063.2 517.8 %all-reduce.83.cloned.1.call-start = ((), (), s32[]{:S(2)}) async-start(), calls=%async_computation.10 | async-start | bytes 18874368 | tf_op jit(solution)/shard_map/psum | solution.py:384
  1063.2 42.1 %copy-start.98 = (bf16[4,1,320,3072]{3,2,0,1:T(8,128)(2,1)S(1)}, bf16[4,1,320,3072]{3,2,0,1:T(8,128)(2,1)}, u32[]{:S(2)}) copy-start(bf16[4,1,320,3072]{3,2,0,1:T(8,128)(2,1)} %copy-done.97) | copy-start | bytes 23592964
  1114.9 942.4 %all-reduce.81.cloned.1.call-start = ((), (), s32[]{:S(2)}) async-start(), calls=%async_computation.9 | async-start | bytes 30081024 | tf_op jit(solution)/shard_map/psum | solution.py:357
  1496.8 6.5 collective-permute-start.2
  1517.5 58.1 %copy-start.84 = (f32[8,128]{1,0:T(8,128)S(1)}, f32[8,128]{1,0:T(8,128)}, u32[]{:S(2)}) copy-start(f32[8,128]{1,0:T(8,128)} %copy-done.83) | copy-start | bytes 12292
  (89 other events, 705.9 us)
Sparse Core Ops, SparseCore 0:
  9.6 40.5 all-gather.11
  192.1 62.0 all-gather.17
  256.9 59.0 all-gather.13
  317.5 22.6 all-gather.15
  1063.3 58.1 all-gather.19
  1125.3 297.4 all-reduce.82
  1515.5 541.8 all-reduce.80
where the time goes:
time: 2100 us; the launch traced here: 2070 us
  other arithmetic  678 us (32%)
  waiting for transfers between devices  614 us (29%)
  local copies, waits for them, and re-layouts  387 us (18%)
  matrix products  230 us (11%)
  blocking collectives  114 us (5%)
  starting transfers between devices  27.2 us (1%)
    psum x1, waiting for transfers between devices, local(): lax.psum((gain_one_grad, in_proj_grad, conv_weight_grad, conv_bias_grad,...  464 us
    reduce_sum x128, other arithmetic, scan_step(): decay = jnp.exp(step_t[:, :, None] * a_mat) * keep_t[:, None, None]  283 us
    squeeze x224, local copies, waits for them, and re-layouts, local_scan(): end_state, outputs = lax.scan(jax.checkpoint(run_block), start_state, items)  192 us
    all_gather x2, waiting for transfers between devices, carried_in(): lax.all_gather(part.astype(kind), axis)  116 us
    reduce_sum x48, other arithmetic, scan_step(): return (state, jnp.sum(state * c_t[:, None, :], -1))  66.1 us
    mul x128, other arithmetic, scan_step(): state = decay * state + (step_t * x_t)[:, :, None] * b_t[:, None, :]  62.3 us
    reduce_sum x32, other arithmetic, scan_step(): state = decay * state + (step_t * x_t)[:, :, None] * b_t[:, None, :]  44.4 us
    dot_general x1, matrix products, local(): jnp.einsum('sjcf,jfd->sjcd', active, expert_down, preferred_element_type=...  43.5 us
  transfers between devices with their start and end apart: 14, of which 7 were waited for; matrix products, arithmetic and copies ran while one was open for 36% of the time, Pallas kernels for 0%

commit v1 on v0

v1 whole, which is shorter than its diff:
```python
import functools

import jax
import jax.numpy as jnp
from jax import lax
from jax.experimental import pallas as pl
from jax.experimental.pallas import tpu as pltpu
from jax.sharding import PartitionSpec as P

f32, bf16 = jnp.float32, jnp.bfloat16
highest = lax.Precision.HIGHEST
LANES = 128
MESH = pl.DeviceIdType.MESH
epsilon = 1e-05
log2e = 1.4426950408889634
cut = 1e8
ln2 = 0.6931471805599453
vmem_cap = 58 << 20


def tree_sum(parts):
    parts = list(parts)
    while len(parts) > 1:
        paired = [parts[i] + parts[i + 1] for i in range(0, len(parts) - 1, 2)]
        parts = paired + parts[len(parts) - len(parts) % 2 :]
    return parts[0]


UN = dict(state=8, scan=8, adj=8, fwd=4, bwd=4)


def spread(rows_ref, pick_ref, outs, states, group):
    steps = rows_ref.shape[0] // group
    chunk = 16
    wide = 2 * LANES

    @pl.loop(0, steps // chunk)
    def _(i):
        rows = rows_ref[pl.ds(pl.multiple_of(i * chunk * group, chunk * group), chunk * group), :]
        for which, out_ref in outs:
            for n in range(0, states, 2):
                at = (which * states + n) * LANES
                part = jnp.dot(rows, pick_ref[:, at : at + wide], preferred_element_type=f32)
                for k in range(2):
                    out_ref[pl.ds(i * chunk, chunk), n + k] = part[:, k * LANES : (k + 1) * LANES].reshape(
                        chunk, group, LANES
                    )


def softplus(v):
    return jnp.maximum(v, 0.0) + jnp.log1p(jnp.exp(-jnp.abs(v)))


class Carry:
    def __init__(self, step, ends, total, a_all, held, got, sent, send_sem, recv_sem):
        self.step, self.ends, self.total, self.a_all = step, ends, total, a_all
        self.held, self.got, self.sent, self.send_sem, self.recv_sem = held, got, sent, send_sem, recv_sem
        self.place, self.peers = lax.axis_index("seq"), lax.axis_size("seq")
        self.rank = self.place if step > 0 else self.peers - 1 - self.place
        self.count, self.states = ends.shape[0], ends.shape[1]
        self.has_before, self.has_after = self.rank > 0, self.rank < self.peers - 1
        self.lag = jnp.minimum(self.rank, self.count)

    def enter(self, devices=1, hosted=None):
        spot = lax.axis_index("exp")
        barrier = pltpu.get_barrier_semaphore()

        @pl.when(self.has_before)
        def _():
            pl.semaphore_signal(barrier, inc=1, device_id={"seq": self.place - self.step}, device_id_type=MESH)

        @pl.when(self.has_after)
        def _():
            pl.semaphore_signal(barrier, inc=1, device_id={"seq": self.place + self.step}, device_id_type=MESH)

        for hop in range(1, devices):
            pl.semaphore_signal(barrier, inc=1, device_id={"exp": lax.rem(spot + hop, devices)}, device_id_type=MESH)
        neighbours = self.has_before.astype(jnp.int32) + self.has_after.astype(jnp.int32)
        extra = devices - 1
        if hosted is not None:
            hosted.enter(barrier)
            extra += 2
        pl.semaphore_wait(barrier, neighbours + extra)

    def hop(self, u):
        return pltpu.make_async_remote_copy(
            src_ref=self.sent.at[u], dst_ref=self.got.at[u], send_sem=self.send_sem.at[u], recv_sem=self.recv_sem.at[u],
            device_id={"seq": self.place + self.step}, device_id_type=MESH,
        )

    def handle(self, at):
        u = at - self.lag

        @pl.when(jnp.logical_and(u >= 0, u < self.count))
        def _():
            @pl.when(self.has_before)
            def _():
                self.hop(u).wait_recv()
                self.held[u] = self.got[u].astype(f32)

            @pl.when(jnp.logical_not(self.has_before))
            def _():
                self.held[u] = jnp.zeros(self.held.shape[1:], f32)

            @pl.when(self.has_after)
            def _():
                for n in range(self.states):
                    decay = jnp.exp2(self.a_all[u, n : n + 1, :] * self.total[u])
                    self.sent[u, n] = (self.ends[u, n] + decay * self.held[u, n]).astype(bf16)
                self.hop(u).start()

    def leave(self):
        @pl.loop(0, self.count)
        def _(u):
            @pl.when(self.has_after)
            def _():
                self.hop(u).wait_send()


def forward_kernel(
    rate_ref, wdt_ref, bias_ref, conv_ref, bc_ref, pick_ref, match_ref, a_all, gate_ref, skip_ref, cot_ref, target_ref,
    step_ref, z_ref, mixed_ref, start_ref, total_ref, cot_out,
    cot_got, kb_ref, b_all, c_all, step_all, ends, staged, cot_send, cot_recv, got, sent, send_sem, recv_sem, *, states, group, devices,
):
    at = pl.program_id(0)
    count = a_all.shape[0]
    j = lax.rem(at, count)
    carry_of = Carry(1, ends, total_ref, a_all, start_ref, got, sent, send_sem, recv_sem)
    rows = conv_ref.shape[0]
    moved = Dispatch(cot_ref, target_ref, cot_got, staged, cot_send, cot_recv, devices)

    @pl.when(at == 0)
    def _():
        carry_of.enter(devices)
        moved.start()
        kb_ref[...] = broad_cut(match_ref)
        spread(bc_ref, pick_ref, ((0, b_all), (1, c_all)), states, group)

    @pl.when(at < count)
    def _():
        pre = jnp.dot(rate_ref[...], wdt_ref[...], preferred_element_type=f32) + bias_ref[...]
        step = softplus(pre)
        step_ref[...] = step
        step_all[j] = step
        a_rows = [jnp.broadcast_to(a_all[j, n : n + 1, :], (group, LANES)) for n in range(states)]
        un = UN["state"]

        def body(i, carry):
            total, state = carry
            base = pl.multiple_of(i * un * group, un * group)
            x_two = conv_ref[pl.ds(base, un * group), :].astype(f32)
            for k in range(un):
                here = pl.ds(pl.multiple_of(base + k * group, group), group)
                dt = step_ref[here, :]
                masked = dt + kb_ref[here, :]
                u = dt * x_two[k * group : (k + 1) * group]
                total = total + masked
                state = [
                    jnp.exp2(masked * a_rows[n]) * state[n] + u * b_all[un * i + k, n] for n in range(states)
                ]
            return total, state

        zero = jnp.zeros((group, LANES), f32)
        total, state = lax.fori_loop(0, rows // (un * group), body, (zero, [zero] * states))
        total_ref[j] = total
        for n in range(states):
            ends[j, n] = state[n]

    carry_of.handle(at)

    @pl.when(at >= count)
    def _():
        a_rows = [jnp.broadcast_to(a_all[j, n : n + 1, :], (group, LANES)) for n in range(states)]
        un = UN["scan"]

        def body(i, state):
            base = pl.multiple_of(i * un * group, un * group)
            x_two = conv_ref[pl.ds(base, un * group), :].astype(f32)
            outs = []
            for k in range(un):
                here = pl.ds(pl.multiple_of(base + k * group, group), group)
                dt = step_all[j, here, :]
                masked = dt + kb_ref[here, :]
                u = dt * x_two[k * group : (k + 1) * group]
                state = [
                    jnp.exp2(masked * a_rows[n]) * state[n] + u * b_all[un * i + k, n] for n in range(states)
                ]
                outs.append(tree_sum(state[n] * c_all[un * i + k, n] for n in range(states)))
            whole = pl.ds(base, un * group)
            gate = gate_ref[whole, :]
            z = jnp.concatenate(outs, 0) + skip_ref[...] * x_two
            z_ref[whole, :] = z
            mixed_ref[whole, :] = (z * (gate * jax.nn.sigmoid(gate))).astype(bf16)
            return state

        lax.fori_loop(0, rows // (un * group), body, [start_ref[j, n] for n in range(states)])

    @pl.when(at == 2 * count - 1)
    def _():
        carry_of.leave()
        moved.wait()
        cot_out[...] = cot_got[...]


def broad_cut(match_ref):
    keep = match_ref[:, match_ref.shape[1] - 1 :]
    return jnp.broadcast_to((1.0 - keep) * cut, (match_ref.shape[0], LANES))


def backward_kernel(
    mg_ref, gate_ref, z_ref, step_ref, conv_ref, bc_ref, pick_ref, match_ref, a_all, total_ref, start_ref, rate_ref, wdt_ref,
    bias_ref, skip_ref, back_ref, *refs, states, group, devices, peers,
):
    sources, refs = refs[:2], refs[2:]
    first_step, spread_steps, _ = hosting_plan(peers, a_all.shape[0])
    opening = None
    if first_step:
        opening, refs = refs[:2], refs[2:]
    gg_ref, low_ref, cg_ref, small_ref, mpg_ref, tok_ref = refs[:6]
    landed, result, buffers, host_sems, spread_pair = refs[6:8], refs[8:10], refs[10:14], refs[14:18], refs[18:20]
    (
        back_send, back_recv, back_own, kb_ref, b_all, c_all, b_acc, c_acc, kept, dt_grad, g_all, rate_acc, ends, last, got, sent, send_sem,
        recv_sem,
    ) = refs[20:]
    at = pl.program_id(0)
    count = a_all.shape[0]
    j = lax.rem(at, count)
    carry_of = Carry(-1, ends, total_ref, a_all, last, got, sent, send_sem, recv_sem)
    steps = conv_ref.shape[0] // group
    rank = rate_ref.shape[1]
    zero = jnp.zeros((group, LANES), f32)
    spot = lax.axis_index("exp")
    shared = HostedSpread(peers, spread_pair, result, 0, spread_steps)
    hosted = HostedSum(
        peers, host_sems, sources, landed, buffers, first_step, peers - 1, opening=opening, spread=shared
    )
    planned = first_step > 0

    def back_copy(hop):
        peer = lax.rem(spot + hop, devices)
        return pltpu.make_async_remote_copy(
            src_ref=back_ref.at[peer], dst_ref=tok_ref.at[spot], send_sem=back_send.at[hop - 1],
            recv_sem=back_recv.at[hop - 1], device_id={"exp": peer}, device_id_type=MESH,
        )

    def own_copy():
        return pltpu.make_async_copy(back_ref.at[spot], tok_ref.at[spot], back_own.at[0])

    @pl.when(at == 0)
    def _():
        carry_of.enter(devices, hosted)
        hosted.open()
        own_copy().start()
        for hop in range(1, devices):
            back_copy(hop).start()
        kb_ref[...] = broad_cut(match_ref)
        spread(bc_ref, pick_ref, ((0, b_all), (1, c_all)), states, group)
        rate_acc[...] = jnp.zeros_like(rate_acc)

        @pl.loop(0, steps)
        def _(t):
            none = jnp.zeros((states, group, LANES), f32)
            b_acc[t] = none
            c_acc[t] = none

    if planned:

        @pl.when(at == 7)
        def _():
            hosted.fetch(jnp.int32(3))

        @pl.when(at == 8)
        def _():
            hosted.add(jnp.int32(3))

        @pl.when(jnp.logical_and(lax.rem(at, 2) == 1, jnp.logical_and(at >= 13, at <= 17)))
        def _():
            hosted.add(lax.div(at - 5, 2))

        @pl.when(at == 19)
        def _():
            shared.hand(jnp.int32(0))

    @pl.when(at < count)
    def _():
        a_rows = [jnp.broadcast_to(a_all[j, n : n + 1, :], (group, LANES)) for n in range(states)]
        un = UN["adj"]

        def body(i, q):
            base = pl.multiple_of((steps // un - 1 - i) * un * group, un * group)
            whole = pl.ds(base, un * group)
            mixed_grad, gate = mg_ref[whole, :], gate_ref[whole, :]
            sig = jax.nn.sigmoid(gate)
            g_rows = mixed_grad * (gate * sig)
            g_all[j, whole, :] = g_rows.astype(bf16)
            gg_ref[whole, :] = (mixed_grad * z_ref[whole, :] * (sig * (1.0 + gate * (1.0 - sig)))).astype(bf16)
            for k in reversed(range(un)):
                t = un * (steps // un - 1 - i) + k
                here = pl.ds(pl.multiple_of(base + k * group, group), group)
                masked = step_ref[here, :] + kb_ref[here, :]
                g = g_rows[k * group : (k + 1) * group]
                q = [jnp.exp2(masked * a_rows[n]) * (c_all[t, n] * g + q[n]) for n in range(states)]
            return q

        q = lax.fori_loop(0, steps // un, body, [zero] * states)
        for n in range(states):
            ends[j, n] = q[n]

    carry_of.handle(at)

    @pl.when(at >= count)
    def _():
        a_rows = [jnp.broadcast_to(a_all[j, n : n + 1, :], (group, LANES)) for n in range(states)]
        fu, bu = UN["fwd"], UN["bwd"]

        def forward(i, state):
            base = pl.multiple_of(i * fu * group, fu * group)
            x_two = conv_ref[pl.ds(base, fu * group), :].astype(f32)
            g_two = g_all[j, pl.ds(base, fu * group), :].astype(f32)
            for k in range(fu):
                t = fu * i + k
                here = pl.ds(pl.multiple_of(base + k * group, group), group)
                dt = step_ref[here, :]
                masked = dt + kb_ref[here, :]
                g = g_two[k * group : (k + 1) * group]
                u = dt * x_two[k * group : (k + 1) * group]
                for n in range(states):
                    kept[t, n] = state[n]
                state = [jnp.exp2(masked * a_rows[n]) * state[n] + u * b_all[t, n] for n in range(states)]
                for n in range(states):
                    c_acc[t, n] += state[n] * g
            return state

        lax.fori_loop(0, steps // fu, forward, [start_ref[0, n] for n in range(states)])
        if planned:
            even = lax.rem(at, 2) == 0

            @pl.when(jnp.logical_and(even, at <= 16))
            def _():
                hosted.fetch(lax.div(at - 4, 2))

            @pl.when(jnp.logical_and(even, at >= 20))
            def _():
                shared.hand(lax.div(at - 18, 2))

        skip = skip_ref[...]

        def backward(i, carry):
            q, a_sum, skip_sum = carry
            base = pl.multiple_of((steps // bu - 1 - i) * bu * group, bu * group)
            x_two = conv_ref[pl.ds(base, bu * group), :].astype(f32)
            g_two = g_all[j, pl.ds(base, bu * group), :].astype(f32)
            for k in reversed(range(bu)):
                t = bu * (steps // bu - 1 - i) + k
                here = pl.ds(pl.multiple_of(base + k * group, group), group)
                dt = step_ref[here, :]
                masked = dt + kb_ref[here, :]
                g = g_two[k * group : (k + 1) * group]
                x = x_two[k * group : (k + 1) * group]
                u = dt * x
                skip_sum = skip_sum + g * x
                lam = [c_all[t, n] * g + q[n] for n in range(states)]
                for n in range(states):
                    b_acc[t, n] += lam[n] * u
                s_one = tree_sum(lam[n] * b_all[t, n] for n in range(states))
                q = [jnp.exp2(masked * a_rows[n]) * lam[n] for n in range(states)]
                w = [q[n] * kept[t, n] for n in range(states)]
                s_two = tree_sum(w[n] * a_rows[n] for n in range(states))
                a_sum = [a_sum[n] + dt * w[n] for n in range(states)]
                cg_ref[here, :] = skip * g + dt * s_one
                dt_grad[here, :] = x * s_one + ln2 * s_two
            return q, a_sum, skip_sum

        q, a_sum, skip_sum = lax.fori_loop(
            0, steps // bu, backward, ([last[j, n] for n in range(states)], [zero] * states, zero)
        )
        pre = jnp.dot(rate_ref[...], wdt_ref[...], preferred_element_type=f32) + bias_ref[...]
        pre_grad = dt_grad[...] * jax.nn.sigmoid(pre)
        low = pre_grad.astype(bf16)
        low_ref[...] = low
        rate_acc[...] += lax.dot_general(low, wdt_ref[...], (((1,), (1,)), ((), ())), preferred_element_type=f32)
        rows_of = [lax.dot_general(rate_ref[...], low, (((0,), (0,)), ((), ())), preferred_element_type=f32)]
        rows_of += [jnp.sum(a_sum[n], 0, keepdims=True) * a_all[j, n : n + 1, :] * ln2 for n in range(states)]
        rows_of += [jnp.sum(pre_grad, 0, keepdims=True), jnp.sum(skip_sum, 0, keepdims=True)]
        spare = small_ref.shape[0] - rank - states - 2
        small_ref[...] = jnp.concatenate(rows_of + [jnp.zeros((spare, LANES), f32)], 0).astype(bf16)

    @pl.when(at == 2 * count - 1)
    def _():
        carry_of.leave()
        if planned:
            shared.hand(jnp.int32(3))
        else:

            @pl.loop(0, peers - 1)
            def _(s):
                hosted.fetch(s)
                hosted.add(s)

            @pl.loop(0, peers - 1)
            def _(s):
                shared.hand(s)

        hosted.finish()
        shared.finish(False)
        own_copy().wait()
        for hop in range(1, devices):
            back_copy(hop).wait()
        mpg_ref[:, :rank] = rate_acc[...].astype(bf16)
        lane = lax.broadcasted_iota(jnp.int32, (LANES, 2 * states), 1)
        total = jnp.zeros((steps * group, 2 * states), f32)
        for n in range(states):
            for column, acc in ((n, b_acc), (states + n, c_acc)):
                rows = acc[:, n].reshape(steps * group, LANES)
                pick = (lane == column).astype(f32)
                total = total + jnp.dot(rows, pick, precision=highest, preferred_element_type=f32)
        mpg_ref[:, rank:] = total.astype(bf16)


def rows_block(rows):
    return pl.BlockSpec((rows, LANES), lambda j: (0, j))


def whole_block(shape):
    return pl.BlockSpec(shape, lambda j: (0,) * len(shape))


def state_block(states, group):
    return pl.BlockSpec((1, states, group, LANES), lambda j: (j, 0, 0, 0))


def shape_of(shape, dtype):
    return jax.ShapeDtypeStruct(shape, dtype)


def params():
    return pltpu.CompilerParams(vmem_limit_bytes=vmem_cap)


def carry_scratch(shape):
    return [
        pltpu.VMEM(shape, bf16), pltpu.VMEM(shape, bf16), pltpu.SemaphoreType.DMA((shape[0],)),
        pltpu.SemaphoreType.DMA((shape[0],)),
    ]


def forward_scan(rate_low, w_dt, bias, conv_low, bc, pick, match, a_blocks, gate, skip, cot, target, capacity, group, devices):
    rows, inner = conv_low.shape
    count, states, _ = a_blocks.shape
    rank = rate_low.shape[1]
    first = lambda at: (0, jnp.minimum(at, count - 1))
    both = lambda at: (0, lax.rem(at, count))
    second = lambda at: (0, jnp.maximum(at - count, 0))
    shape = (count, states, group, LANES)
    big = pltpu.VMEM((rows // group, states, group, LANES), f32)
    return pl.pallas_call(
        functools.partial(forward_kernel, states=states, group=group, devices=devices),
        grid=(2 * count,),
        in_specs=[
            whole_block((rows, rank)), pl.BlockSpec((rank, LANES), first), pl.BlockSpec((1, LANES), first),
            pl.BlockSpec((rows, LANES), both), whole_block(bc.shape), whole_block(pick.shape),
            whole_block(match.shape), whole_block(a_blocks.shape), pl.BlockSpec((rows, LANES), second),
            pl.BlockSpec((1, LANES), second), whole_block(cot.shape), whole_block((1, rows)),
        ],
        out_specs=[
            pl.BlockSpec((rows, LANES), first), pl.BlockSpec((rows, LANES), second), pl.BlockSpec((rows, LANES), second),
            whole_block(shape), whole_block((count, group, LANES)), whole_block((devices, capacity, cot.shape[1])),
        ],
        out_shape=[
            shape_of((rows, inner), f32), shape_of((rows, inner), f32), shape_of((rows, inner), bf16),
            shape_of(shape, f32), shape_of((count, group, LANES), f32), shape_of((devices, capacity, cot.shape[1]), bf16),
        ],
        scratch_shapes=[pltpu.VMEM((devices, capacity, cot.shape[1]), bf16), pltpu.VMEM((rows, LANES), f32), big, big]
        + [pltpu.VMEM((count, rows, LANES), f32), pltpu.VMEM(shape, f32)]
        + [pltpu.VMEM((devices - 1, capacity, cot.shape[1]), bf16)]
        + [pltpu.SemaphoreType.DMA((devices - 1,)), pltpu.SemaphoreType.DMA((devices - 1,))] + carry_scratch(shape),
        compiler_params=pltpu.CompilerParams(collective_id=0, has_side_effects=True, vmem_limit_bytes=vmem_cap),
        name="forward_scan",
    )(rate_low, w_dt, bias, conv_low, bc, pick, match, a_blocks, gate, skip, cot, target[None, :])


def backward_scan(mixed_grad, gate, z, step, conv_low, bc, pick, match, a_blocks, total, start, rate_low, w_dt, bias, skip, back, sources, partial, group, devices):
    rows, inner = conv_low.shape
    count, states, _ = a_blocks.shape
    rank = rate_low.shape[1]
    small_rows = -(-(rank + states + 2) // 16) * 16
    peers, pieces = sources[0].shape[1], [v.shape[2:] for v in sources]
    first_step, spread_steps, _ = hosting_plan(peers, count)
    dma = pltpu.SemaphoreType.DMA
    extra = list(sources) + (list(partial) if first_step else [])
    first = lambda at: (0, jnp.minimum(at, count - 1))
    both = lambda at: (0, lax.rem(at, count))
    second = lambda at: (0, jnp.maximum(at - count, 0))
    shape = (count, states, group, LANES)
    big = pltpu.VMEM((rows // group, states, group, LANES), f32)
    return pl.pallas_call(
        functools.partial(backward_kernel, states=states, group=group, devices=devices, peers=peers),
        grid=(2 * count,),
        in_specs=[
            pl.BlockSpec((rows, LANES), first), pl.BlockSpec((rows, LANES), first), pl.BlockSpec((rows, LANES), first),
            pl.BlockSpec((rows, LANES), both), pl.BlockSpec((rows, LANES), second), whole_block(bc.shape),
            whole_block(pick.shape), whole_block(match.shape), whole_block(a_blocks.shape), whole_block(total.shape),
            pl.BlockSpec((1, states, group, LANES), lambda at: (jnp.maximum(at - count, 0), 0, 0, 0)),
            whole_block((rows, rank)), pl.BlockSpec((rank, LANES), second), pl.BlockSpec((1, LANES), second),
            pl.BlockSpec((1, LANES), second), pl.BlockSpec(memory_space=pl.ANY),
        ]
        + any_specs(len(extra)),
        out_specs=[
            pl.BlockSpec((rows, LANES), lambda at: (0, jnp.minimum(at, count - 1) + count)),
            pl.BlockSpec((rows, LANES), second), pl.BlockSpec((rows, LANES), second),
            pl.BlockSpec((small_rows, LANES), second), whole_block((rows, rank + 2 * states)),
        ]
        + any_specs(5),
        out_shape=[
            shape_of((rows, 2 * inner), bf16), shape_of((rows, inner), bf16), shape_of((rows, inner), f32),
            shape_of((small_rows, inner), bf16), shape_of((rows, rank + 2 * states), bf16), shape_of(back.shape, bf16),
        ]
        + [shape_of((2, peers - 1 - first_step) + p, bf16) for p in pieces]
        + [shape_of(v.shape, bf16) for v in sources],
        scratch_shapes=sum_buffers(pieces) + sum_sems(peers - 1 - first_step) + spread_sems(spread_steps)
        + [dma((devices - 1,)), dma((devices - 1,)), dma((1,))]
        + [pltpu.VMEM((rows, LANES), f32), big, big, big, big, big]
        + [pltpu.VMEM((rows, LANES), f32), pltpu.VMEM((count, rows, LANES), bf16)]
        + [pltpu.VMEM((rows, rank), f32), pltpu.VMEM(shape, f32), pltpu.VMEM(shape, f32)] + carry_scratch(shape),
        compiler_params=pltpu.CompilerParams(collective_id=1, has_side_effects=True, vmem_limit_bytes=64 << 20),
        name="backward_scan",
    )(mixed_grad, gate, z, step, conv_low, bc, pick, match, a_blocks, total, start, rate_low, w_dt, bias, skip, back, *extra)


def split_three(v):
    high = v.astype(bf16)
    rest = v - high.astype(f32)
    mid = rest.astype(bf16)
    low = (rest - mid.astype(f32)).astype(bf16)
    return jnp.concatenate([high, mid, low], -1)


def pick_matrix(columns):
    eye = (jnp.arange(columns)[:, None] == jnp.arange(columns * LANES)[None, :] // LANES).astype(bf16)
    return jnp.concatenate([eye] * 3, 0)

def broad_match(match_ref, wide):
    @pl.when(pl.program_id(0) == 0)
    def _():
        for k in range(match_ref.shape[1]):
            wide[k] = jnp.broadcast_to(match_ref[:, k : k + 1], wide.shape[1:])


def front_kernel(
    token_ref, before_ref, gain_ref, wc_ref, wg_ref, cw_ref, cb_ref, compact_ref, wx_ref, ci_ref, low_ref, gate_ref, mixed_ref,
    normed_ref, rows_f, match_ref, *, halo, group,
):
    rows = low_ref.shape[0]
    broad_match(compact_ref, match_ref)

    @pl.when(pl.program_id(0) == 0)
    def _():
        def put(at, source):
            values = source.astype(f32)
            scale = lax.rsqrt(jnp.mean(values * values, -1, keepdims=True) + epsilon)
            normed_ref[at, :] = (values * scale * gain_ref[...]).astype(bf16)

        put(slice(0, halo), before_ref[...])
        tile = 256

        @pl.loop(0, rows // tile)
        def _(i):
            put(pl.ds(pl.multiple_of(halo + i * tile, halo), tile), token_ref[pl.ds(pl.multiple_of(i * tile, tile), tile), :])

    taps = cw_ref.shape[0]
    ci = jnp.dot(normed_ref[...], wc_ref[...], preferred_element_type=f32).astype(bf16)
    ci_ref[...] = ci
    rows_f[...] = ci.astype(f32)
    total = conv_total(rows_f, cw_ref, cb_ref, match_ref, halo, group, rows, taps)
    low = (total * jax.nn.sigmoid(total)).astype(bf16)
    low_ref[...] = low
    gate_ref[...] = jnp.dot(normed_ref[halo:, :], wg_ref[...], preferred_element_type=f32)
    part = jnp.dot(low, wx_ref[...], preferred_element_type=f32)

    @pl.when(pl.program_id(0) == 0)
    def _():
        mixed_ref[...] = part

    @pl.when(pl.program_id(0) > 0)
    def _():
        mixed_ref[...] += part


def conv_total(rows_f, cw_ref, cb_ref, match_ref, halo, group, rows, taps):
    total = cb_ref[...] + cw_ref[taps - 1 : taps, :] * rows_f[halo : halo + rows, :]
    for k in range(taps - 1):
        at = halo - (taps - 1 - k) * group
        total = total + cw_ref[k : k + 1, :] * rows_f[at : at + rows, :] * match_ref[k]
    return total


def front(token_low, before_rows, gain, w_in, conv_w, conv_b, match, w_x, halo, group, lanes):
    width, inner = w_in.shape[0], w_in.shape[1] // 2
    total_rows = token_low.shape[0] + halo
    rows, taps, mixed_width = total_rows - halo, conv_w.shape[0], w_x.shape[1]
    count = inner // lanes
    cols = lambda r: pl.BlockSpec((r, lanes), lambda j: (0, j))
    return pl.pallas_call(
        functools.partial(front_kernel, halo=halo, group=group),
        grid=(count,),
        in_specs=[
            whole_block(token_low.shape), whole_block(before_rows.shape), whole_block(gain.shape), cols(width),
            pl.BlockSpec((width, lanes), lambda j: (0, j + count)),
            cols(taps), cols(1), whole_block(match.shape), pl.BlockSpec((lanes, mixed_width), lambda j: (j, 0)),
        ],
        out_specs=[cols(total_rows), cols(rows), cols(rows), whole_block((rows, mixed_width)), whole_block((total_rows, width))],
        out_shape=[
            shape_of((total_rows, inner), bf16), shape_of((rows, inner), bf16), shape_of((rows, inner), f32),
            shape_of((rows, mixed_width), f32), shape_of((total_rows, width), bf16),
        ],
        scratch_shapes=[pltpu.VMEM((total_rows, lanes), f32), pltpu.VMEM((match.shape[1], rows, lanes), f32)],
        compiler_params=params(),
        name="front",
    )(token_low, before_rows, gain, w_in, w_in, conv_w, conv_b, match, w_x)


def conv_back_kernel(
    cg_ref, low_ref, mpg_ref, wx_ref, ci_ref, cw_ref, cb_ref, compact_ref, proj_ref, outg_ref, up_in, down_in, pg_ref, ext_ref,
    small_ref, outo_ref, up_ref, down_ref, rows_f, ext, match_ref, near_got, passed, far_got, send_sem, recv_sem, *spread_pair,
    halo, group, first_step, last_step,
):
    spread = None
    if last_step > first_step:
        spread = HostedSpread(up_ref.shape[1], spread_pair, (up_ref, down_ref), first_step, last_step)
    broad_match(compact_ref, match_ref)
    spot = lax.axis_index("exp")
    near = spot + 1 - 2 * lax.rem(spot, 2)
    far = lax.rem(spot + 2, 4)
    across = lax.rem(near + 2, 4)
    rows_out = outo_ref.shape[0]

    def share_of(k):
        return pl.ds(pl.multiple_of(k * rows_out, rows_out), rows_out)

    def move(source, target, slot, device):
        return pltpu.make_async_remote_copy(
            src_ref=source, dst_ref=target, send_sem=send_sem.at[slot], recv_sem=recv_sem.at[slot],
            device_id={"exp": device}, device_id_type=MESH,
        )

    def near_move(slot):
        return move(outg_ref.at[share_of(across if slot else near)], near_got.at[slot], slot, near)

    def far_move():
        return move(passed, far_got, 2, far)

    @pl.when(pl.program_id(0) == 0)
    def _():
        barrier = pltpu.get_barrier_semaphore()
        for device in (near, far):
            pl.semaphore_signal(barrier, inc=1, device_id={"exp": device}, device_id_type=MESH)
        if spread:
            spread.enter(barrier)
        pl.semaphore_wait(barrier, 4 if spread else 2)
        if spread:
            spread.open()
        near_move(1).start()
        near_move(0).start()

    rows = pg_ref.shape[0]
    taps = cw_ref.shape[0]
    grad = cg_ref[...] + lax.dot_general(
        mpg_ref[...], wx_ref[...], (((1,), (1,)), ((), ())), preferred_element_type=f32
    )
    rows_f[...] = ci_ref[...].astype(f32)
    total = conv_total(rows_f, cw_ref, cb_ref, match_ref, halo, group, rows, taps)
    sig = jax.nn.sigmoid(total)
    grad = grad * (sig * (1.0 + total * (1.0 - sig)))
    x_part = lax.dot_general(mpg_ref[...], low_ref[...], (((0,), (0,)), ((), ())), preferred_element_type=f32)
    taps_grad = [None] * taps
    ext[:halo, :] = jnp.zeros((halo, ext.shape[1]), f32)
    ext[halo:, :] = grad * cw_ref[taps - 1 : taps, :]
    taps_grad[taps - 1] = jnp.sum(grad * rows_f[halo:, :], 0, keepdims=True)
    for k in range(taps - 1):
        at = halo - (taps - 1 - k) * group
        own = grad * match_ref[k]
        taps_grad[k] = jnp.sum(own * rows_f[at : at + rows, :], 0, keepdims=True)
        ext[at : at + rows, :] += own * cw_ref[k : k + 1, :]
    pg_ref[...] = ext[halo:, :].astype(bf16)
    ext_ref[:halo, :] = ext[:halo, :]
    ext_ref[halo:, :] = ext[rows:, :]
    spare = small_ref.shape[0] - x_part.shape[0] - taps - 1
    parts = [x_part] + taps_grad + [jnp.sum(grad, 0, keepdims=True), jnp.zeros((spare, ext.shape[1]), f32)]
    small_ref[...] = jnp.concatenate(parts, 0).astype(bf16)

    @pl.when(pl.program_id(0) == 0)
    def _():
        near_move(1).wait_recv()
        passed[...] = (outg_ref[share_of(far), :].astype(f32) + near_got[1].astype(f32)).astype(bf16)
        far_move().start()
        near_move(0).wait_recv()
        outo_ref[...] = outg_ref[share_of(spot), :].astype(f32) + near_got[0].astype(f32)

    @pl.when(pl.program_id(0) == pl.num_programs(0) - 1)
    def _():
        far_move().wait_recv()
        outo_ref[...] += far_got[...].astype(f32)
        for slot in range(2):
            near_move(slot).wait_send()
        far_move().wait_send()
        if spread:
            spread.hand(jnp.int32(first_step))
            spread.finish(True)


def conv_back(cg, conv_low, mpg, w_x, ci, conv_w, conv_b, match, proj, out_grad, results, steps, halo, group, lanes, devices):
    out_shape = (out_grad.shape[0] // devices, out_grad.shape[1])
    dma = pltpu.SemaphoreType.DMA
    rows, inner = cg.shape
    taps, mixed_width = conv_w.shape[0], w_x.shape[1]
    small_rows = -(-(mixed_width + taps + 1) // 16) * 16
    cols = lambda r: pl.BlockSpec((r, lanes), lambda j: (0, j))
    return pl.pallas_call(
        functools.partial(conv_back_kernel, halo=halo, group=group, first_step=steps[0], last_step=steps[1]),
        grid=(inner // lanes,),
        in_specs=[
            cols(rows), cols(rows), whole_block((rows, mixed_width)), pl.BlockSpec((lanes, mixed_width), lambda j: (j, 0)),
            cols(rows + halo), cols(taps), cols(1), whole_block(match.shape),
            pl.BlockSpec(memory_space=pl.ANY), pl.BlockSpec(memory_space=pltpu.VMEM),
        ]
        + any_specs(2),
        out_specs=[cols(rows), cols(2 * halo), cols(small_rows), whole_block(out_shape)] + any_specs(2),
        out_shape=[shape_of(proj.shape, bf16), shape_of((2 * halo, inner), f32), shape_of((small_rows, inner), bf16)]
        + [shape_of(out_shape, f32)]
        + [shape_of(v.shape, bf16) for v in results],
        scratch_shapes=[pltpu.VMEM((rows + halo, lanes), f32), pltpu.VMEM((rows + halo, lanes), f32)]
        + [pltpu.VMEM((match.shape[1], rows, lanes), f32), pltpu.VMEM((2,) + out_shape, bf16)]
        + [pltpu.VMEM(out_shape, bf16), pltpu.VMEM(out_shape, bf16), dma((3,)), dma((3,))]
        + (spread_sems(steps[1] - steps[0]) if steps[1] > steps[0] else []),
        input_output_aliases={8: 0, 10: 4, 11: 5},
        compiler_params=pltpu.CompilerParams(collective_id=6, has_side_effects=True, vmem_limit_bytes=vmem_cap),
        name="conv_back",
    )(cg, conv_low, mpg, w_x, ci, conv_w, conv_b, match, proj, out_grad, *results)

def expert_kernel(
    rows_ref, cot_ref, up_ref, down_ref, out_ref, back_ref, upg_ref, downg_ref, grad, out_acc, back_acc, active, pre_grad, *, tile
):
    first = pl.program_id(0) == 0
    final = pl.program_id(0) == pl.num_programs(0) - 1
    slots, width = cot_ref.shape
    tiles = [slice(i * tile, (i + 1) * tile) for i in range(slots // tile)]

    @pl.when(first)
    def _():
        for at in tiles:
            parts = rows_ref[at, width : width + LANES].astype(f32)
            gate = parts[:, 0:1] + parts[:, 1:2] + parts[:, 2:3]
            grad[at, :] = (gate * cot_ref[at, :].astype(f32)).astype(bf16)
            out_acc[at, :] = jnp.zeros((tile, width), f32)
            back_acc[at, :] = jnp.zeros((tile, width), f32)

    for at in tiles:
        pre = jnp.dot(rows_ref[at, :width], up_ref[...], preferred_element_type=f32)
        act_grad = lax.dot_general(grad[at, :], down_ref[...], (((1,), (1,)), ((), ())), preferred_element_type=f32)
        half = 0.5 * lax.erf(pre * 0.7071067811865476) + 0.5
        active[at, :] = (pre * half).astype(bf16)
        slope = half + pre * (jnp.exp(pre * pre * -0.5) * 0.3989422804014327)
        pre_grad[at, :] = (act_grad * slope).astype(bf16)
    for at in tiles:
        out_acc[at, :] += jnp.dot(active[at, :], down_ref[...], preferred_element_type=f32)
        back_acc[at, :] += lax.dot_general(
            pre_grad[at, :], up_ref[...], (((1,), (1,)), ((), ())), preferred_element_type=f32
        )
    downg_ref[...] = lax.dot_general(
        active[...], grad[...], (((0,), (0,)), ((), ())), preferred_element_type=f32
    ).astype(bf16)
    upg_ref[...] = lax.dot_general(
        rows_ref[:, :width], pre_grad[...], (((0,), (0,)), ((), ())), preferred_element_type=f32
    ).astype(bf16)

    @pl.when(final)
    def _():
        for at in tiles:
            out = out_acc[at, :].astype(bf16)
            out_ref[at, :] = out
            back_ref[at, :width] = back_acc[at, :].astype(bf16)
            dot = jnp.sum(out.astype(f32) * cot_ref[at, :].astype(f32), -1, keepdims=True)
            back_ref[at, width:] = in_parts(dot)


def in_parts(column):
    high = column.astype(bf16).astype(f32)
    mid = (column - high).astype(bf16).astype(f32)
    lane = lax.broadcasted_iota(jnp.int32, (column.shape[0], LANES), 1)
    low = column - high - mid
    return jnp.where(lane == 0, high, jnp.where(lane == 1, mid, jnp.where(lane == 2, low, 0.0))).astype(bf16)


def one_expert(rows, cot, up, down):
    slots, width = cot.shape
    hidden = up.shape[1]
    hidden_tile, tile = hidden // 6, slots // 2
    full = whole_block((slots, width))
    broad = whole_block((slots, width + LANES))
    cols = pl.BlockSpec((width, hidden_tile), lambda j: (0, j))
    deep = pl.BlockSpec((hidden_tile, width), lambda j: (j, 0))
    return pl.pallas_call(
        functools.partial(expert_kernel, tile=tile),
        grid=(hidden // hidden_tile,),
        in_specs=[broad, full, cols, deep],
        out_specs=[full, broad, cols, deep],
        out_shape=[
            shape_of((slots, width), bf16), shape_of((slots, width + LANES), bf16), shape_of((width, hidden), bf16),
            shape_of((hidden, width), bf16),
        ],
        scratch_shapes=[
            pltpu.VMEM((slots, width), bf16), pltpu.VMEM((slots, width), f32), pltpu.VMEM((slots, width), f32),
            pltpu.VMEM((slots, hidden_tile), bf16), pltpu.VMEM((slots, hidden_tile), bf16),
        ],
        compiler_params=params(),
        name="one_expert",
    )(rows, cot, up, down)


def exp_barrier(spot, devices, hosted=None):
    barrier = pltpu.get_barrier_semaphore()
    if hosted:
        hosted.enter(barrier)
    for hop in range(1, devices):
        pl.semaphore_signal(barrier, inc=1, device_id={"exp": lax.rem(spot + hop, devices)}, device_id_type=MESH)
    pl.semaphore_wait(barrier, devices + 1 if hosted else devices - 1)


class Dispatch:
    def __init__(self, rows_ref, target_ref, got_ref, staged, send_sem, recv_sem, devices):
        self.rows_ref, self.target_ref, self.got_ref, self.staged = rows_ref, target_ref, got_ref, staged
        self.send_sem, self.recv_sem, self.devices = send_sem, recv_sem, devices
        self.spot = lax.axis_index("exp")
        self.hops = [h for h in range(devices // 2, devices)] + [h for h in range(1, devices // 2)]

    def packed(self, k):
        capacity = self.got_ref.shape[1]
        slot = lax.broadcasted_iota(jnp.int32, (capacity, self.rows_ref.shape[0]), 0) + k * capacity
        pick = jnp.where(slot == self.target_ref[...], 1.0, 0.0).astype(bf16)
        return jnp.dot(pick, self.rows_ref[...], preferred_element_type=f32).astype(bf16)

    def copy(self, hop):
        return pltpu.make_async_remote_copy(
            src_ref=self.staged.at[hop - 1], dst_ref=self.got_ref.at[self.spot], send_sem=self.send_sem.at[hop - 1],
            recv_sem=self.recv_sem.at[hop - 1], device_id={"exp": lax.rem(self.spot + hop, self.devices)},
            device_id_type=MESH,
        )

    def start(self):
        for hop in self.hops:
            self.staged[hop - 1] = self.packed(lax.rem(self.spot + hop, self.devices))
            self.copy(hop).start()
        self.got_ref[self.spot] = self.packed(self.spot)

    def wait(self):
        for hop in self.hops:
            self.copy(hop).wait()


def route_kernel(
    mixed_ref, wout_ref, token_ref, gain_ref, router_ref, route_ref, target_ref, hidden_ref, rows_ref, prob_ref, got_ref,
    staged, send_sem, recv_sem, *, devices, experts, tile,
):
    exp_barrier(lax.axis_index("exp"), devices)
    width = wout_ref.shape[1]

    @pl.loop(0, mixed_ref.shape[0] // tile)
    def _(i):
        at = pl.ds(pl.multiple_of(i * tile, tile), tile)
        hidden = token_ref[at, :].astype(f32) + jnp.dot(mixed_ref[at, :], wout_ref[...], preferred_element_type=f32)
        hidden_ref[at, :] = hidden
        scale = lax.rsqrt(jnp.mean(hidden * hidden, -1, keepdims=True) + epsilon)
        low = (hidden * scale * gain_ref[...]).astype(bf16)
        rows_ref[at, :width] = low
        logits = jnp.dot(low, router_ref[...], preferred_element_type=f32)
        lane = lax.broadcasted_iota(jnp.int32, logits.shape, 1)
        logits = jnp.where(lane < experts, logits, -1e30)
        raised = jnp.exp(logits - jnp.max(logits, -1, keepdims=True))
        prob = raised / jnp.sum(raised, -1, keepdims=True)
        prob_ref[at, :] = prob
        gate = jnp.sum(jnp.where(lane == route_ref[at, :], prob, 0.0), -1, keepdims=True)
        rows_ref[at, width:] = in_parts(gate)

    moved = Dispatch(rows_ref, target_ref, got_ref, staged, send_sem, recv_sem, devices)
    moved.start()
    moved.wait()


def routed(mixed_low, w_out, token_low, gain, router_wide, route_col, target, capacity, devices, experts):
    vm = pl.BlockSpec(memory_space=pltpu.VMEM)
    dma = pltpu.SemaphoreType.DMA
    rows, width = token_low.shape
    return pl.pallas_call(
        functools.partial(route_kernel, devices=devices, experts=experts, tile=256),
        in_specs=[vm] * 7,
        out_specs=[vm] * 4,
        out_shape=[
            shape_of((rows, width), f32), shape_of((rows, width + LANES), bf16), shape_of((rows, LANES), f32),
            shape_of((devices, capacity, width + LANES), bf16),
        ],
        scratch_shapes=[pltpu.VMEM((devices - 1, capacity, width + LANES), bf16), dma((devices - 1,)), dma((devices - 1,))],
        compiler_params=pltpu.CompilerParams(collective_id=3, has_side_effects=True, vmem_limit_bytes=vmem_cap),
        name="routed",
    )(mixed_low, w_out, token_low, gain, router_wide, route_col, target[None, :])


def collect_kernel(
    sent_ref, target_ref, route_ref, rows_ref, prob_ref, hidden_ref, cot_ref, gain_ref, router_ref, *refs, devices, hops,
    tile, peers, first_step,
):
    hosted = None
    if first_step:
        sources, refs = refs[:2], refs[2:]
    hidden_grad_ref, branch_ref, gain_grad_ref, router_grad_ref = refs[:4]
    got, total, send_sem, recv_sem = refs[-4:]
    if first_step:
        hosted = HostedSum(
            peers, refs[12:16], sources, refs[4:6], refs[8:12], 0, first_step, partial=refs[6:8]
        )
    spot = lax.axis_index("exp")
    capacity = got.shape[1]
    count, width = hidden_ref.shape
    exp_barrier(spot, devices, hosted)
    if hosted:
        hosted.open()
    copies = []
    for hop in hops:
        peer = lax.rem(spot + hop, devices)
        c = pltpu.make_async_remote_copy(
            src_ref=sent_ref.at[peer], dst_ref=got.at[devices - hop - 1], send_sem=send_sem.at[hop - 1],
            recv_sem=recv_sem.at[hop - 1], device_id={"exp": peer}, device_id_type=MESH,
        )
        c.start()
        copies.append(c)

    def spread_back(k, rows):
        slot = lax.broadcasted_iota(jnp.int32, (count, capacity), 1) + k * capacity
        pick = jnp.where(slot == target_ref[...], 1.0, 0.0).astype(bf16)
        return jnp.dot(pick, rows, preferred_element_type=f32)

    total[...] = spread_back(spot, sent_ref[spot])
    for at, (hop, c) in enumerate(zip(hops, copies)):
        c.wait_recv()
        if hosted and at < first_step - 1:
            hosted.fetch(jnp.int32(at))
            hosted.add(jnp.int32(at))
        total[...] += spread_back(lax.rem(spot + devices - hop, devices), got[devices - hop - 1])
    gain_grad_ref[...] = jnp.zeros_like(gain_grad_ref)
    router_grad_ref[...] = jnp.zeros_like(router_grad_ref)

    @pl.loop(0, count // tile)
    def _(i):
        at = pl.ds(pl.multiple_of(i * tile, tile), tile)
        parts = total[at, width:]
        gate_grad = parts[:, 0:1] + parts[:, 1:2] + parts[:, 2:3]
        prob = prob_ref[at, :]
        chosen = jnp.where(lax.broadcasted_iota(jnp.int32, prob.shape, 1) == route_ref[at, :], 1.0, 0.0)
        gate = jnp.sum(prob * chosen, -1, keepdims=True)
        logit_grad = prob * (chosen - gate) * gate_grad
        router_grad_ref[...] += lax.dot_general(
            logit_grad, rows_ref[at, :width].astype(f32), (((0,), (0,)), ((), ())), precision=highest,
            preferred_element_type=f32,
        )
        grad = total[at, :width] + jnp.dot(
            logit_grad, router_ref[...], precision=highest, preferred_element_type=f32
        )
        hidden = hidden_ref[at, :]
        scale = lax.rsqrt(jnp.mean(hidden * hidden, -1, keepdims=True) + epsilon)
        unit = hidden * scale
        gain_grad_ref[...] += jnp.sum(grad * unit, 0, keepdims=True)
        scaled = grad * gain_ref[...]
        hidden_grad = cot_ref[at, :].astype(f32) + scale * (
            scaled - unit * jnp.mean(scaled * unit, -1, keepdims=True)
        )
        hidden_grad_ref[at, :] = hidden_grad
        branch_ref[at, :] = hidden_grad.astype(bf16)

    for c in copies:
        c.wait_send()
    if hosted:
        hosted.fetch(jnp.int32(first_step - 1))
        hosted.add(jnp.int32(first_step - 1))
        hosted.finish()


def collect(blocks, target, route_col, rows, prob, hidden, cot, gain, router_t, sources, first_step, devices):
    vm = pl.BlockSpec(memory_space=pltpu.VMEM)
    dma = pltpu.SemaphoreType.DMA
    capacity, wide = blocks.shape[1:]
    count, width = hidden.shape
    peers, pieces = sources[0].shape[1], [v.shape[2:] for v in sources]
    extra = list(sources) if first_step else []
    more, scratch = [], []
    if first_step:
        more = [shape_of((2, first_step) + p, bf16) for p in pieces] + [shape_of((2,) + p, bf16) for p in pieces]
        scratch = sum_buffers(pieces) + sum_sems(first_step)
    return pl.pallas_call(
        functools.partial(collect_kernel, devices=devices, hops=(2, 3, 1), tile=256, peers=peers, first_step=first_step),
        in_specs=[vm] * 9 + any_specs(len(extra)),
        out_specs=[vm] * 4 + any_specs(len(more)),
        out_shape=[
            shape_of((count, width), f32), shape_of((count, width), bf16), shape_of((1, width), f32),
            shape_of((LANES, width), f32),
        ]
        + more,
        scratch_shapes=scratch
        + [
            pltpu.VMEM((devices - 1, capacity, wide), bf16), pltpu.VMEM((count, wide), f32), dma((devices - 1,)),
            dma((devices - 1,)),
        ],
        compiler_params=pltpu.CompilerParams(collective_id=4, has_side_effects=True, vmem_limit_bytes=vmem_cap),
        name="collect",
    )(blocks, target[:, None], route_col, rows, prob, hidden, cot, gain, router_t, *extra)

SEGMENTS = 4
STARTS = (-4, 1, 3, 6)


def ring_order(place, peers):
    odd = lax.rem(place, 2)
    half = lax.div(place, 2)
    return half + odd * (peers - 1 - 2 * half)


def ring_member(position, peers):
    back = lax.div(2 * position, peers)
    return 2 * position + back * (2 * (peers - 1) + 1 - 4 * position)


class Rings:
    def __init__(self, own, total, sent, landed, send, recv, bases, sizes, peers):
        place = lax.axis_index("seq")
        self.own, self.total, self.sent, self.landed, self.send, self.recv = own, total, sent, landed, send, recv
        self.bases, self.sizes, self.peers = bases, sizes, peers
        self.position = ring_order(place, peers)
        self.after = ring_member(lax.rem(self.position + 1, peers), peers)
        self.before = ring_member(lax.rem(self.position + peers - 1, peers), peers)

    def rows(self, ring, steps):
        sign = 1 if ring % 2 == 0 else -1
        chunk = self.sizes[ring] // self.peers
        c = lax.rem(self.position + sign * steps + 2 * self.peers, self.peers)
        return pl.ds(pl.multiple_of(self.bases[ring] + c * chunk, 16), chunk)

    def target(self, ring):
        return {"seq": self.after if ring % 2 == 0 else self.before}

    def first(self, ring, s):
        chunk = self.sizes[ring] // self.peers
        return pltpu.make_async_remote_copy(
            src_ref=self.sent.at[ring, s, pl.ds(0, chunk)], dst_ref=self.landed.at[ring, s, pl.ds(0, chunk)],
            send_sem=self.send.at[ring, s], recv_sem=self.recv.at[ring, s], device_id=self.target(ring),
            device_id_type=MESH,
        )

    def second(self, ring, s):
        part = self.total.at[self.rows(ring, 1 - s)]
        at = self.peers - 1 + s
        return pltpu.make_async_remote_copy(
            src_ref=part, dst_ref=part, send_sem=self.send.at[ring, at], recv_sem=self.recv.at[ring, at],
            device_id=self.target(ring), device_id_type=MESH,
        )

    def begin(self, ring):
        chunk = self.sizes[ring] // self.peers
        self.sent[ring, 0, pl.ds(0, chunk)] = self.own[self.rows(ring, 0), :].astype(bf16)
        self.first(ring, 0).start()

    def advance(self, ring, s):
        peers, chunk = self.peers, self.sizes[ring] // self.peers

        @pl.when(jnp.logical_and(s >= 1, s <= peers - 2))
        def _():
            self.first(ring, s - 1).wait_recv()
            summed = self.landed[ring, s - 1, pl.ds(0, chunk)].astype(f32) + self.own[self.rows(ring, -s), :]
            self.sent[ring, s, pl.ds(0, chunk)] = summed.astype(bf16)
            self.first(ring, s).start()

        @pl.when(s == peers - 1)
        def _():
            self.first(ring, peers - 2).wait_recv()
            summed = self.landed[ring, peers - 2, pl.ds(0, chunk)].astype(f32) + self.own[self.rows(ring, 1), :]
            self.total[self.rows(ring, 1), :] = summed.astype(bf16)
            self.second(ring, 0).start()

        @pl.when(jnp.logical_and(s >= peers, s <= 2 * peers - 3))
        def _():
            self.second(ring, s - peers).wait_recv()
            self.second(ring, s - peers + 1).start()

        @pl.when(s == 2 * peers - 2)
        def _():
            self.second(ring, peers - 2).wait_recv()

    def drain(self):
        @pl.loop(0, self.peers - 1)
        def _(s):
            for ring in range(len(self.sizes)):
                self.first(ring, s).wait_send()
                self.second(ring, s).wait_send()


def finish_kernel(
    proj_ref, normed_ref, win_ref, outo_ref, small_ref, gain_ref, token_ref, hiddeng_ref, hidden_ref, rows_ref, target_ref,
    tok_ref, up_in, down_in,
    in_sum_ref, out_sum_ref, small_sum_ref, tokens_grad_ref, block_ref, up_ref, down_ref,
    own, total, near_stage, small_all, gain_part, near_in, near_small, far_in, far_small, pass_in, pass_small, sent, landed, near_send, near_recv, far_send, far_recv, ring_send, ring_recv,
    *spread_pair, peers, bases, sizes, halo, tile, gain_row, first_step, last_step,
):
    spot = lax.axis_index("exp")
    width, wide = near_in.shape[1:]
    rows_out = outo_ref.shape[0]
    rows_small, share = near_small.shape[1:]
    folds = wide // share
    count = proj_ref.shape[0]
    third = width // 3
    near = spot + 1 - 2 * lax.rem(spot, 2)
    far = lax.rem(spot + 2, 4)
    across = lax.rem(near + 2, 4)
    rings = Rings(own, total, sent, landed, ring_send, ring_recv, bases, sizes, peers)
    barrier = pltpu.get_barrier_semaphore()
    for device in ({"exp": near}, {"exp": far}, {"seq": rings.after}, {"seq": rings.before}):
        pl.semaphore_signal(barrier, inc=1, device_id=device, device_id_type=MESH)
    pl.semaphore_wait(barrier, 4)
    spread = None
    if last_step > first_step:
        spread = HostedSpread(peers, spread_pair, (up_ref, down_ref), first_step, last_step)
        spread.open()

    def columns(k, size):
        return pl.ds(pl.multiple_of(k * size, size), size)

    def copy(source, target, send, recv, device):
        return pltpu.make_async_remote_copy(
            src_ref=source, dst_ref=target, send_sem=send, recv_sem=recv, device_id=device, device_id_type=MESH
        )

    def in_rows(i):
        return slice(i * third, (i + 1) * third)

    def near_copy(slot, piece):
        k = across if slot else near
        if piece == 4:
            source, target = small_all.at[:, columns(k, share)], near_small.at[slot]
        else:
            at = pl.ds((piece - 1) * third, third)
            source, target = near_stage.at[slot, at], near_in.at[slot, at]
        return copy(source, target, near_send.at[slot, piece], near_recv.at[slot, piece], {"exp": near})

    def far_copy(piece):
        if piece == 4:
            source, target = pass_small, far_small
        else:
            at = pl.ds((piece - 1) * third, third)
            source, target = pass_in.at[at], far_in.at[at]
        return copy(source, target, far_send.at[piece], far_recv.at[piece], {"exp": far})

    def in_tile(i, k):
        part = lax.dot_general(
            normed_ref[pl.ds(halo, count), in_rows(i)], proj_ref[:, columns(k, wide)], (((0,), (0,)), ((), ())),
            preferred_element_type=f32,
        )
        scaled = part * win_ref[in_rows(i), columns(k, wide)].astype(f32)
        gain_part[in_rows(i), :] += tree_sum(scaled[:, h * LANES : (h + 1) * LANES] for h in range(wide // LANES))
        return part

    def into_own(base, values, add):
        size = values.shape[0]
        for h in range(values.shape[1] // share):
            at = slice(base + h * size, base + (h + 1) * size)
            part = values[:, h * share : (h + 1) * share]
            if add:
                own[at, :] += part
            else:
                own[at, :] = part

    def pad_own(n, used):
        if used < sizes[n]:
            own[bases[n] + used : bases[n] + sizes[n], :] = jnp.zeros((sizes[n] - used, share), f32)

    small_base = bases[3] + folds * third
    into_own(bases[0], outo_ref[...], False)
    pad_own(0, folds * rows_out)
    rings.begin(0)
    gain_part[...] = jnp.zeros_like(gain_part)
    small_all[...] = small_ref[...]
    for i in range(3):
        for slot, k in ((1, across), (0, near)):
            near_stage[slot, in_rows(i), :] = in_tile(i, k).astype(bf16)
            near_copy(slot, 1 + i).start()
        distant = in_tile(i, far)
        near_copy(1, 1 + i).wait_recv()
        pass_in[in_rows(i), :] = (distant + near_in[1, in_rows(i), :].astype(f32)).astype(bf16)
        far_copy(1 + i).start()
        mine = in_tile(i, spot)
        near_copy(0, 1 + i).wait_recv()
        into_own(bases[1 + i], mine + near_in[0, in_rows(i), :].astype(f32), False)
        pad_own(1 + i, folds * third)
        rings.advance(0, jnp.int32(1 + i))
    quarter = width // 4
    for k in range(4):
        part = jnp.sum(gain_part[k * quarter : (k + 1) * quarter, :], -1, keepdims=True)
        eye = lax.broadcasted_iota(jnp.int32, (quarter, quarter), 0) == lax.broadcasted_iota(
            jnp.int32, (quarter, quarter), 1
        )
        row = jnp.sum(jnp.where(eye, part, 0.0), 0, keepdims=True) / gain_ref[:, k * quarter : (k + 1) * quarter]
        group = slice(gain_row, gain_row + 16)
        old = small_all[group, k * share : k * share + quarter].astype(f32)
        top = lax.broadcasted_iota(jnp.int32, old.shape, 0) == 0
        small_all[group, k * share : k * share + quarter] = jnp.where(top, row, old).astype(bf16)
    for slot in (1, 0):
        near_copy(slot, 4).start()
    near_copy(1, 4).wait_recv()
    pass_small[...] = (small_all[:, columns(far, share)].astype(f32) + near_small[1].astype(f32)).astype(bf16)
    far_copy(4).start()
    near_copy(0, 4).wait_recv()
    own[small_base : small_base + rows_small, :] = (
        small_all[:, columns(spot, share)].astype(f32) + near_small[0].astype(f32)
    )
    def arrived(ring):
        far_copy(ring).wait_recv()
        into_own(bases[ring], far_in[in_rows(ring - 1), :].astype(f32), True)
        if ring == SEGMENTS - 1:
            far_copy(4).wait_recv()
            own[small_base : small_base + rows_small, :] += far_small[...].astype(f32)
        rings.begin(ring)

    def place_rows(out_ref, values, i):
        group = out_ref.shape[0]
        steps = tile // group
        values = jnp.swapaxes(values.reshape(steps, group, width), 0, 1)
        out_ref[:, pl.ds(pl.multiple_of(i * steps, steps), steps), :] = values.astype(out_ref.dtype)

    def token_tile(i):
        at = pl.ds(pl.multiple_of(i * tile, tile), tile)
        grad = lax.dot_general(proj_ref[at, :], win_ref[...], (((1,), (1,)), ((), ())), preferred_element_type=f32)
        values = token_ref[at, :].astype(f32)
        scale = lax.rsqrt(jnp.mean(values * values, -1, keepdims=True) + epsilon)
        unit = values * scale
        scaled = grad * gain_ref[...]
        total_grad = hiddeng_ref[at, :] + scale * (scaled - unit * jnp.mean(scaled * unit, -1, keepdims=True))
        place_rows(tokens_grad_ref, total_grad, i)

    def block_tile(i):
        at = pl.ds(pl.multiple_of(i * tile, tile), tile)
        capacity = tok_ref.shape[1]
        parts = rows_ref[at, width:].astype(f32)
        gate = parts[:, 0:1] + parts[:, 1:2] + parts[:, 2:3]
        tok = jnp.zeros((tile, width), f32)
        for k in range(tok_ref.shape[0]):
            slot = lax.broadcasted_iota(jnp.int32, (tile, capacity), 1) + k * capacity
            pick = jnp.where(slot == target_ref[at, :], 1.0, 0.0).astype(bf16)
            tok = tok + jnp.dot(pick, tok_ref[k], preferred_element_type=f32)
        place_rows(block_ref, hidden_ref[at, :] + gate * tok, i)

    tiles = count // tile

    @pl.loop(0, 2 * peers - 1 + STARTS[-1])
    def _(turn):
        for ring in range(SEGMENTS):
            step = turn - STARTS[ring]
            if ring:

                @pl.when(step == 0)
                def _():
                    arrived(ring)

            rings.advance(ring, step)

        if spread:
            for n in range(last_step - first_step):

                @pl.when(turn == 4 + 6 * n)
                def _():
                    spread.hand(jnp.int32(first_step + n))

        @pl.when(turn < tiles)
        def _():
            token_tile(turn)

        @pl.when(jnp.logical_and(turn >= tiles, turn < 2 * tiles))
        def _():
            block_tile(turn - tiles)

    for i in range(3):
        for h in range(folds):
            at = slice(bases[1 + i] + h * third, bases[1 + i] + (h + 1) * third)
            in_sum_ref[in_rows(i), h * share : (h + 1) * share] = total[at, :].astype(f32)
    for h in range(folds):
        at = slice(bases[0] + h * rows_out, bases[0] + (h + 1) * rows_out)
        out_sum_ref[:, h * share : (h + 1) * share] = total[at, :].astype(f32)
    small_sum_ref[...] = total[small_base : small_base + rows_small, :].astype(f32)
    for piece in range(1, 5):
        for slot in (1, 0):
            near_copy(slot, piece).wait_send()
        far_copy(piece).wait_send()
    rings.drain()
    if spread:
        spread.finish(True)


def finish(proj, normed_ext, w_in, out_own, small, gain, token_low, hidden_grad, hidden_one, moe_rows, target, tok, results, steps, gain_row, group):
    peers, devices = lax.axis_size("seq"), lax.axis_size("exp")
    count, width = token_low.shape
    wide, rows_out = proj.shape[1] // devices, out_own.shape[0]
    rows_small, share = small.shape[0], small.shape[1] // devices
    folds, third, unit = wide // share, width // 3, 16 * peers
    used = (folds * rows_out, folds * third, folds * third, folds * third + rows_small)
    sizes = tuple(-(-u // unit) * unit for u in used)
    bases = tuple(sum(sizes[:i]) for i in range(SEGMENTS))
    length, chunk = sum(sizes), max(sizes) // peers
    vm = pl.BlockSpec(memory_space=pltpu.VMEM)
    dma = pltpu.SemaphoreType.DMA
    shapes = ((width, wide), (rows_small, share))
    return pl.pallas_call(
        functools.partial(
            finish_kernel, peers=peers, bases=bases, sizes=sizes, halo=normed_ext.shape[0] - count, tile=256,
            gain_row=gain_row, first_step=steps[0], last_step=steps[1],
        ),
        in_specs=[vm] * 12 + any_specs(2),
        out_specs=[vm] * 5 + any_specs(2),
        out_shape=[
            shape_of((width, wide), f32), shape_of((rows_out, wide), f32), shape_of((rows_small, share), f32),
            shape_of((group, count // group, width), f32), shape_of((group, count // group, width), bf16),
        ]
        + [shape_of(v.shape, bf16) for v in results],
        scratch_shapes=[
            pltpu.VMEM((length, share), f32), pltpu.VMEM((length, share), bf16), pltpu.VMEM((2, width, wide), bf16),
            pltpu.VMEM(small.shape, bf16), pltpu.VMEM((width, LANES), f32),
        ]
        + [pltpu.VMEM((2,) + s, bf16) for s in shapes]
        + [pltpu.VMEM(s, bf16) for s in shapes]
        + [pltpu.VMEM(s, bf16) for s in shapes]
        + [pltpu.VMEM((SEGMENTS, peers - 1, chunk, share), bf16)] * 2
        + [dma((2, 5)), dma((2, 5)), dma((5,)), dma((5,)), dma((SEGMENTS, 2 * peers - 2)), dma((SEGMENTS, 2 * peers - 2))]
        + (spread_sems(steps[1] - steps[0]) if steps[1] > steps[0] else []),
        input_output_aliases={12: 5, 13: 6},
        compiler_params=pltpu.CompilerParams(collective_id=2, has_side_effects=True, vmem_limit_bytes=64 << 20),
        name="finish",
    )(
        proj, normed_ext, w_in, out_own, small, gain, token_low, hidden_grad, hidden_one, moe_rows, target[:, None], tok, *results,
    )

PIECES = 2


def gather_kernel(in_ref, small_ref, edge_ref, ids_ref, win_ref, wsmall_ref, before_ref, before_ids, near_sems, far_sems, pair_sems, edge_sems, own_sem):
    place, peers = lax.axis_index("seq"), lax.axis_size("seq")
    spot = lax.axis_index("exp")
    near = spot + 1 - 2 * lax.rem(spot, 2)
    far = lax.rem(spot + 2, 4)
    bit = lax.rem(place, 2)
    pair = place + 1 - 2 * bit
    width, wide = in_ref.shape
    share = small_ref.shape[1]
    chunk = width // 2 // PIECES
    has_before, has_after = place > 0, place < peers - 1
    barrier = pltpu.get_barrier_semaphore()
    for target in ({"exp": near}, {"exp": far}, {"seq": pair}):
        pl.semaphore_signal(barrier, inc=1, device_id=target, device_id_type=MESH)

    @pl.when(has_before)
    def _():
        pl.semaphore_signal(barrier, inc=1, device_id={"seq": place - 1}, device_id_type=MESH)

    @pl.when(has_after)
    def _():
        pl.semaphore_signal(barrier, inc=1, device_id={"seq": place + 1}, device_id_type=MESH)

    pl.semaphore_wait(barrier, 3 + has_before.astype(jnp.int32) + has_after.astype(jnp.int32))

    def columns(ref, k, size):
        return ref.at[:, pl.ds(pl.multiple_of(k * size, size), size)]

    def rows(k, half, piece):
        at = pl.multiple_of((half * PIECES + piece) * chunk, chunk)
        return win_ref.at[pl.ds(at, chunk), pl.ds(pl.multiple_of(k * wide, wide), wide)]

    def copy(source, target, sems, slot, device):
        return pltpu.make_async_remote_copy(
            src_ref=source, dst_ref=target, send_sem=sems.at[0, slot], recv_sem=sems.at[1, slot], device_id=device,
            device_id_type=MESH,
        )

    def edge_copies():
        return (
            copy(edge_ref, before_ref, edge_sems, 0, {"seq": place + 1}),
            copy(ids_ref, before_ids, edge_sems, 1, {"seq": place + 1}),
        )

    outward = []
    for piece in range(PIECES):
        at = pl.multiple_of((bit * PIECES + piece) * chunk, chunk)
        outward.append(copy(in_ref.at[pl.ds(at, chunk), :], rows(spot, bit, piece), far_sems, piece, {"exp": far}))
    outward.insert(0, copy(small_ref, columns(wsmall_ref, spot, share), far_sems, PIECES, {"exp": far}))
    for c in outward:
        c.start()
    beside = [
        copy(small_ref, columns(wsmall_ref, spot, share), near_sems, 0, {"exp": near}),
        copy(in_ref, columns(win_ref, spot, wide), near_sems, 1, {"exp": near}),
    ]
    for c in beside:
        c.start()

    @pl.when(has_after)
    def _():
        for c in edge_copies():
            c.start()

    @pl.when(jnp.logical_not(has_before))
    def _():
        before_ref[...] = jnp.zeros_like(before_ref)
        before_ids[...] = jnp.zeros_like(before_ids)

    own = [
        pltpu.make_async_copy(in_ref, columns(win_ref, spot, wide), own_sem.at[0]),
        pltpu.make_async_copy(small_ref, columns(wsmall_ref, spot, share), own_sem.at[1]),
    ]
    for c in own:
        c.start()
    outward[0].wait_recv()
    beside.append(copy(columns(wsmall_ref, far, share), columns(wsmall_ref, far, share), near_sems, 2, {"exp": near}))
    beside[-1].start()
    crossing = []
    for piece in range(PIECES):
        outward[1 + piece].wait_recv()
        part = rows(far, bit, piece)
        crossing.append(copy(part, part, pair_sems, piece, {"seq": pair}))
        crossing[-1].start()
        beside.append(copy(part, part, near_sems, 3 + piece, {"exp": near}))
        beside[-1].start()
    for piece in range(PIECES):
        crossing[piece].wait_recv()
        part = rows(far, 1 - bit, piece)
        beside.append(copy(part, part, near_sems, 3 + PIECES + piece, {"exp": near}))
        beside[-1].start()
    for c in beside:
        c.wait_recv()
    for c in outward + beside + crossing:
        c.wait_send()
    for c in own:
        c.wait()

    @pl.when(has_before)
    def _():
        for c in edge_copies():
            c.wait_recv()

    @pl.when(has_after)
    def _():
        for c in edge_copies():
            c.wait_send()


def gather_weights(in_shard, small, edge, ids, devices):
    vm = pl.BlockSpec(memory_space=pltpu.VMEM)
    dma = pltpu.SemaphoreType.DMA
    return pl.pallas_call(
        gather_kernel,
        in_specs=[pl.BlockSpec(memory_space=pl.ANY), vm, vm, vm],
        out_specs=[pl.BlockSpec(memory_space=pl.ANY), vm, vm, vm],
        out_shape=[
            shape_of((in_shard.shape[0], in_shard.shape[1] * devices), bf16),
            shape_of((small.shape[0], small.shape[1] * devices), bf16), shape_of(edge.shape, edge.dtype),
            shape_of(ids.shape, ids.dtype),
        ],
        scratch_shapes=[dma((2, 3 + 2 * PIECES)), dma((2, PIECES + 1)), dma((2, PIECES)), dma((2, 2)), dma((2,))],
        compiler_params=pltpu.CompilerParams(collective_id=5, has_side_effects=True, vmem_limit_bytes=32 << 20),
        name="gather_weights",
    )(in_shard, small, edge, ids)

def hosting_plan(peers, count):
    if peers == 8 and count == 12:
        return 3, 4, 5
    return 0, peers - 1, peers - 1


class Hosted:
    def __init__(self, peers, send, recv):
        place = lax.axis_index("seq")
        self.peers, self.send, self.recv = peers, send, recv
        self.position = ring_order(place, peers)
        self.after = ring_member(lax.rem(self.position + 1, peers), peers)
        self.before = ring_member(lax.rem(self.position + peers - 1, peers), peers)

    def enter(self, barrier):
        for device in (self.after, self.before):
            pl.semaphore_signal(barrier, inc=1, device_id={"seq": device}, device_id_type=MESH)

    def chunk(self, ring, steps):
        sign = 1 if ring == 0 else -1
        return lax.rem(self.position + sign * steps + 2 * self.peers, self.peers)

    def remote(self, lane, source, target, slot):
        return pltpu.make_async_remote_copy(
            src_ref=source, dst_ref=target, send_sem=self.send.at[lane, slot], recv_sem=self.recv.at[lane, slot],
            device_id={"seq": self.after if lane % 2 == 0 else self.before}, device_id_type=MESH,
        )


class HostedSum(Hosted):
    def __init__(self, peers, sems, sources, landed, buffers, first, last, opening=None, partial=None, spread=None):
        self.load, self.keep = sems[2], sems[3]
        super().__init__(peers, sems[0], sems[1])
        self.sources, self.landed, self.first, self.last = sources, landed, first, last
        self.own, self.got = buffers[:2], buffers[2:]
        self.opening, self.partial, self.spread = opening, partial, spread
        self.lanes = [(2 * a + ring, a, ring) for a in range(2) for ring in range(2)]

    def opened(self, lane, a, ring):
        source = self.opening[a].at[ring] if self.opening else self.sources[a].at[ring, self.chunk(ring, -self.first)]
        return self.remote(lane, source, self.landed[a].at[ring, 0], 0)

    def passing(self, lane, a, ring, s):
        slot = s - self.first
        return self.remote(lane, self.own[a].at[ring, lax.rem(s, 2)], self.landed[a].at[ring, slot], slot)

    def loads(self, lane, a, ring, s):
        return (
            pltpu.make_async_copy(self.landed[a].at[ring, s - self.first], self.got[a].at[ring], self.load.at[lane, 0]),
            pltpu.make_async_copy(
                self.sources[a].at[ring, self.chunk(ring, -s - 1)], self.own[a].at[ring, lax.rem(s + 1, 2)],
                self.load.at[lane, 1],
            ),
        )

    def kept(self, lane, a, ring):
        source = self.own[a].at[ring, self.last % 2]
        if self.partial:
            return pltpu.make_async_copy(source, self.partial[a].at[ring], self.keep.at[lane])
        return pltpu.make_async_copy(source, self.spread.result[a].at[ring, self.chunk(ring, 1)], self.keep.at[lane])

    def closing(self, lane, a, ring):
        target = self.spread.result[a].at[ring, self.chunk(ring, 1)]
        return self.spread.remote(lane, self.own[a].at[ring, self.last % 2], target, 0)

    def open(self):
        for q in self.lanes:
            self.opened(*q).start()

    def fetch(self, s):
        for q in self.lanes:
            self.passing(*q, s).wait_recv()

            @pl.when(s >= self.first + 2)
            def _():
                self.passing(*q, s - 1).wait_send()

            for c in self.loads(*q, s):
                c.start()

    def add(self, s):
        for q in self.lanes:
            lane, a, ring = q
            for c in self.loads(*q, s):
                c.wait()
            slot = lax.rem(s + 1, 2)
            self.own[a][ring, slot] = (self.own[a][ring, slot].astype(f32) + self.got[a][ring].astype(f32)).astype(bf16)

            @pl.when(s < self.last - 1)
            def _():
                self.passing(*q, s + 1).start()

            @pl.when(s == self.last - 1)
            def _():
                self.kept(*q).start()
                if self.spread:
                    self.closing(*q).start()

    def finish(self):
        for q in self.lanes:
            self.opened(*q).wait_send()
            if self.last - 1 > self.first:
                self.passing(*q, self.last - 1).wait_send()
            self.kept(*q).wait()
            if self.spread:
                self.closing(*q).wait_send()


class HostedSpread(Hosted):
    def __init__(self, peers, sems, result, first, last):
        super().__init__(peers, sems[0], sems[1])
        self.result, self.first, self.last = result, first, last
        self.lanes = [(2 * a + ring, a, ring) for a in range(2) for ring in range(2)]

    def handing(self, lane, a, ring, s):
        part = self.result[a].at[ring, self.chunk(ring, 1 - s)]
        return self.remote(lane, part, part, s - self.first)

    def open(self):
        for q in self.lanes:
            self.handing(*q, self.first).start()

    def hand(self, s):
        for q in self.lanes:
            self.handing(*q, s).wait_recv()

            @pl.when(s < self.last - 1)
            def _():
                self.handing(*q, s + 1).start()

    def finish(self, opened):
        for q in self.lanes:

            @pl.loop(self.first + (0 if opened else 1), self.last)
            def _(s):
                self.handing(*q, s).wait_send()


def any_specs(count):
    return [pl.BlockSpec(memory_space=pl.ANY)] * count


def sum_buffers(pieces):
    return [pltpu.VMEM((2, 2) + p, bf16) for p in pieces] + [pltpu.VMEM((2,) + p, bf16) for p in pieces]


def sum_sems(steps):
    dma = pltpu.SemaphoreType.DMA
    return [dma((4, steps)), dma((4, steps)), dma((4, 2)), dma((4,))]


def spread_sems(steps):
    return [pltpu.SemaphoreType.DMA((4, steps)), pltpu.SemaphoreType.DMA((4, steps))]

def rms_norm(values, gain):
    return values * lax.rsqrt(jnp.mean(values * values, -1, keepdims=True) + epsilon) * gain


def passed_along(value, axis, steps):
    count = lax.axis_size(axis)
    initial, last = (max(0, -steps), min(count, count - steps))
    return lax.ppermute(value, axis, [(source, source + steps) for source in range(initial, last)])


def by_time(values):
    values = jnp.swapaxes(values, 0, 1)
    return values.reshape((values.shape[0] * values.shape[1],) + values.shape[2:])


def packed_small(norm_gain, conv_weight, conv_bias, x_proj, dt_proj, dt_bias, a_log, d_skip, moe_gain, router):
    share = conv_bias.shape[0]
    packed = [conv_weight, conv_bias[None], x_proj.T, dt_proj, dt_bias[None], a_log.T, d_skip[None]]
    narrow = jnp.concatenate([norm_gain[None], moe_gain[None], router.T], 0)
    total = jnp.concatenate(packed + [narrow.reshape(-1, share)], 0)
    return jnp.pad(total, ((0, -total.shape[0] % 16), (0, 0))), [p.shape[0] for p in packed], narrow.shape


def unpacked_small(whole, counts, narrow_shape, devices):
    out, at = [], 0
    for c in counts:
        out.append(whole[at : at + c])
        at += c
    share = whole.shape[1] // devices
    fold = narrow_shape[0] * narrow_shape[1] // share
    rest = whole[at : at + fold].reshape(fold, devices, share).transpose(1, 0, 2).reshape((devices,) + narrow_shape)
    rest = rest.transpose(1, 0, 2).reshape(narrow_shape[0], -1)
    return out, rest[0], rest[1], rest[2:].T


def local(
    tokens, segment_ids, routes, slot_index, norm_gain, in_proj, conv_weight, conv_bias, x_proj, dt_proj, dt_bias,
    a_log, d_skip, out_proj, moe_gain, router, expert_up, expert_down, cotangent,
):
    seq_count, part_len, width = tokens.shape
    row_count = seq_count * part_len
    group = seq_count
    kernel_len = conv_weight.shape[0]
    state_width = a_log.shape[1]
    rank_width = dt_proj.shape[0]
    halo = kernel_len * group
    devices = lax.axis_size("exp")
    doc_ids = segment_ids + 1
    edge_start = part_len - kernel_len
    token_low = by_time(tokens)
    edge_ids = jnp.pad(doc_ids[:, edge_start:], ((0, 0), (0, LANES - kernel_len)))
    small_shard, counts, narrow_shape = packed_small(
        norm_gain, conv_weight, conv_bias, x_proj, dt_proj, dt_bias, a_log, d_skip, moe_gain, router
    )
    w_in, small_whole, before_rows, before_ids = gather_weights(
        in_proj, small_shard, token_low[row_count - halo :], edge_ids, devices
    )
    out_proj, small_whole = lax.optimization_barrier((out_proj, small_whole))
    w_out = lax.all_gather(out_proj, "exp", axis=0, tiled=True)
    (w_conv, b_conv, w_x_t, w_dt, b_dt, log_decay, skip_gain), gain_one, gain_two, w_router = unpacked_small(
        small_whole, counts, narrow_shape, devices
    )
    inner_width = w_out.shape[0]
    expert_total = w_router.shape[1]
    capacity = 5 * row_count // (4 * expert_total)
    blocks = inner_width // LANES

    ext_ids = jnp.concatenate([before_ids[:, :kernel_len], doc_ids], 1)
    match = jnp.stack([ext_ids[:, 1 + k : 1 + k + part_len] == doc_ids for k in range(kernel_len - 1)])
    match = jnp.transpose(match, (2, 1, 0)).reshape(row_count, kernel_len - 1).astype(f32)
    lanes = 2 * LANES
    gain_one = gain_one.astype(f32)[None]
    gain_two = gain_two.astype(f32)[None]
    route_rows = by_time(routes)
    slot_rows = by_time(slot_index)
    target = jnp.where(
        slot_rows < capacity, route_rows * capacity + slot_rows, expert_total * capacity
    )
    cot_rows = by_time(cotangent)
    w_conv, b_conv = w_conv.astype(f32), b_conv.astype(f32)
    w_x = w_x_t.T
    ci, conv_low, gate, mixed, normed_ext = front(
        token_low, before_rows, gain_one, w_in, w_conv, b_conv, match, w_x, halo, group, lanes
    )
    rate_low = mixed[:, :rank_width].astype(bf16)
    bc = split_three(mixed[:, rank_width:])
    pick = pick_matrix(2 * state_width)
    bias = b_dt.astype(f32)
    skip = skip_gain.astype(f32)
    a_mat = -jnp.exp(log_decay.astype(f32))
    a2 = a_mat * log2e
    a_blocks = a2.reshape(state_width, blocks, LANES).transpose(1, 0, 2)
    step, z, mixed_low, start, total, cot_recv = forward_scan(
        rate_low, w_dt, bias, conv_low, bc, pick, match, a_blocks, gate, skip, cot_rows, target, capacity, group, devices
    )
    route_col = route_rows[:, None]
    router_wide = jnp.pad(w_router, ((0, 0), (0, LANES - expert_total)))
    hidden_one, moe_rows, prob, received = routed(
        mixed_low, w_out, token_low, gain_two, router_wide, route_col, target, capacity, devices, expert_total
    )
    expert_out, rows_back, up_grad, down_grad = one_expert(
        received.reshape(devices * capacity, width + LANES), cot_recv.reshape(devices * capacity, width),
        expert_up[0], expert_down[0],
    )
    peers = lax.axis_size("seq")
    first_step, spread_first, spread_second = hosting_plan(peers, blocks)
    sources = [up_grad.reshape(2, peers, -1, up_grad.shape[1]), down_grad.reshape(2, peers, -1, width)]
    hidden_grad, branch_grad, gain_two_grad, router_grad_t, *hosted = collect(
        rows_back.reshape(devices, capacity, width + LANES), target, route_col, moe_rows, prob, hidden_one, cot_rows,
        gain_two, router_wide.astype(f32).T, sources, first_step, devices,
    )
    out_proj_grad = jnp.dot(mixed_low.T, branch_grad, preferred_element_type=f32)
    mixed_grad = jnp.dot(branch_grad, w_out.T, preferred_element_type=f32)
    proj, rate_pre_low, cg, small_one, mixed_proj_grad, tok, *hosted = backward_scan(
        mixed_grad, gate, z, step, conv_low, bc, pick, match, a_blocks, total, start, rate_low, w_dt, bias, skip,
        expert_out.reshape(devices, capacity, width), sources, hosted[2:], group, devices,
    )
    proj, ends, small_two, out_own, *results = conv_back(
        cg, conv_low, mixed_proj_grad, w_x, ci, w_conv, b_conv, match, proj, out_proj_grad.astype(bf16), hosted[2:],
        (spread_first, spread_second), halo, group, lanes, devices,
    )
    edge_back = passed_along(ends[:halo].astype(bf16), "seq", -1).astype(f32)
    proj = lax.dynamic_update_slice(proj, (ends[halo:] + edge_back).astype(bf16), (row_count - halo, 0))

    narrow = jnp.concatenate([jnp.zeros_like(gain_two_grad), gain_two_grad, router_grad_t[:expert_total]], 0)
    share, own_width = inner_width // devices, width // devices
    narrow = narrow.reshape(narrow.shape[0], devices, own_width)
    narrow = jnp.pad(narrow, ((0, -narrow.shape[0] % 16), (0, 0), (0, share - own_width))).astype(bf16)
    packed = jnp.concatenate([small_one, small_two, narrow.reshape(-1, inner_width)], 0)
    gain_row = small_one.shape[0] + small_two.shape[0]
    in_sum, out_sum, sums, tokens_grad, block_out, up_sum, down_sum = finish(
        proj, normed_ext, w_in, out_own, packed, gain_one, token_low, hidden_grad, hidden_one, moe_rows,
        target, tok, results, (spread_second, peers - 1), gain_row, group,
    )
    at, own = 0, []
    for first, rows in (
        (0, rank_width), (rank_width, state_width), (rank_width + state_width, 1), (rank_width + state_width + 1, 1)
    ):
        own.append(sums[first : first + rows])
    at = small_one.shape[0]
    mixed_width = mixed_proj_grad.shape[1]
    for first, rows in ((0, mixed_width), (mixed_width, kernel_len), (mixed_width + kernel_len, 1)):
        own.append(sums[at + first : at + first + rows])
    at += small_two.shape[0]
    own_narrow = sums[at : at + 2 + expert_total, :own_width]
    return (
        block_out,
        tokens_grad,
        own_narrow[0],
        in_sum,
        own[5],
        own[6][0],
        own[4].T,
        own[0],
        own[2][0],
        own[1].T,
        own[3][0],
        out_sum,
        own_narrow[1],
        own_narrow[2:].T,
        up_sum.reshape(expert_up.shape).astype(f32),
        down_sum.reshape(expert_down.shape).astype(f32),
    )


def solution(mesh):
    in_specs = (
        P("exp", "seq", None),
        P("exp", "seq"),
        P("exp", "seq"),
        P("exp", "seq"),
        P("exp"),
        P(None, "exp"),
        P(None, "exp"),
        P("exp"),
        P("exp", None),
        P(None, "exp"),
        P("exp"),
        P("exp", None),
        P("exp"),
        P("exp", None),
        P("exp"),
        P("exp", None),
        P("exp", None, None),
        P("exp", None, None),
        P("exp", "seq", None),
    )
    out_specs = (
        P("exp", "seq", None),
        P("exp", "seq", None),
        P("exp"),
        P(None, "exp"),
        P(None, "exp"),
        P("exp"),
        P("exp", None),
        P(None, "exp"),
        P("exp"),
        P("exp", None),
        P("exp"),
        P("exp", None),
        P("exp"),
        P("exp", None),
        P("exp", None, None),
        P("exp", None, None),
    )
    return jax.shard_map(local, mesh=mesh, in_specs=in_specs, out_specs=out_specs, check_vma=False)
```

time: 2100 us -> 697 us (0.33)
  other arithmetic: 678 us -> 24.1 us
  waiting for transfers between devices: 614 us -> 3.39 us
  Pallas kernels: 0 us -> 585 us
  local copies, waits for them, and re-layouts: 387 us -> 46.6 us
  matrix products: 230 us -> 11.4 us
  blocking collectives: 114 us -> 0 us
  starting transfers between devices: 27.2 us -> 1.33 us
    pallas_call x0 -> x9, Pallas kernels: none -> 585 us  [the longest x1 173 us: backward_scan(): pl.pallas_call(functools.partial(backward_kernel, states=states, group=gr...]
    psum x2 -> x0, waiting for transfers between devices: 464 us -> none  [the longest x1 464 us: local(): lax.psum((gain_one_grad, in_proj_grad, conv_weight_grad, conv_bias_grad,...]
    reduce_sum x214 -> x0, other arithmetic: 416 us -> none  [the longest x128 283 us: scan_step(): decay = jnp.exp(step_t[:, :, None] * a_mat) * keep_t[:, None, None]]
    dot_general x21 -> x2, matrix products: 230 us -> 11.4 us  [the longest x1 5.92 us: local(): mixed_grad = jnp.dot(branch_grad, w_out.T, preferred_element_type=f32)]
    squeeze x224 -> x0, local copies, waits for them, and re-layouts: 192 us -> none  [local_scan(): end_state, outputs = lax.scan(jax.checkpoint(run_block), start_state, items)]
    all_gather x5 -> x1, waiting for transfers between devices: 116 us -> 0.01 us  [local(): w_out = lax.all_gather(out_proj, 'exp', axis=0, tiled=True)]
    mul x130 -> x0, other arithmetic: 70.7 us -> none  [the longest x128 62.3 us: scan_step(): state = decay * state + (step_t * x_t)[:, :, None] * b_t[:, None, :]]
    all_gather x8 -> x0, blocking collectives: 64.5 us -> none  [the longest x1 25.2 us: local(): lax.all_gather(router, 'exp', axis=0, tiled=True)]
  transfers between devices with their start and end apart: 14 -> 2, of which waited for: 7 -> 1; matrix products, arithmetic and copies ran while one was open for 36% -> 3% of each run, Pallas kernels for 0% -> 12%
where the time goes in v1:
time: 697 us; the launch traced here: 687 us
  Pallas kernels  585 us (84%)
  local copies, waits for them, and re-layouts  46.6 us (7%)
  other arithmetic  24.1 us (3%)
  between operations  14.8 us (2%)
  matrix products  11.4 us (2%)
    pallas_call x1, Pallas kernels, backward_scan(): pl.pallas_call(functools.partial(backward_kernel, states=states, group=gr...  173 us
    pallas_call x1, Pallas kernels, finish(): pl.pallas_call(functools.partial(finish_kernel, peers=peers, bases=bases,...  128 us
    pallas_call x1, Pallas kernels, forward_scan(): pl.pallas_call(functools.partial(forward_kernel, states=states, group=gro...  66.7 us
    pallas_call x1, Pallas kernels, collect(): pl.pallas_call(functools.partial(collect_kernel, devices=devices, hops=(2...  62.5 us
    pallas_call x1, Pallas kernels, one_expert(): pl.pallas_call(functools.partial(expert_kernel, tile=tile), grid=(hidden...  46.2 us
    pallas_call x1, Pallas kernels, routed(): pl.pallas_call(functools.partial(route_kernel, devices=devices, experts=e...  40.5 us
    pallas_call x1, Pallas kernels, gather_weights(): pl.pallas_call(gather_kernel, in_specs=[pl.BlockSpec(memory_space=pl.ANY)...  29.3 us
    pallas_call x1, Pallas kernels, conv_back(): pl.pallas_call(functools.partial(conv_back_kernel, halo=halo, group=group...  24.7 us
  transfers between devices with their start and end apart: 2, of which 1 were waited for; matrix products, arithmetic and copies ran while one was open for 3% of the time, Pallas kernels for 12%

profile of v1, /device:TPU:0, one launch (start us, length us, event | category | flops | bytes accessed | tf_op | source)
XLA Modules:
  0.0 687.1 jit_solution(17604879676762966068)
XLA Ops:
  13.1 3.4 concatenate.25
  17.8 29.3 %gather_weights.1 = (bf16[768,3072]{1,0:T(8,128)(2,1)S(1)}, bf16[160,1536]{1,0:T(8,128)(2,1)S(1)}, bf16[32,768]{1,0:T(8,128)(2,1)S(1)}, s32[8,128]{1,0:T(8,128)S(1)}) custom-call(bf16[768,768]{1,0:T(8,128)(2,1)S(1)} %copy-done.1, bf16[160,384]{1,0:T(8,128)(2,1)S(1)} %pad.17.small_ref, bf16[32,768]{1,0:T(8,128)(2,1)S(1)} %bitcast.71, s32[8,128]{1,0:T(8,128)S(1)} %pad.18.ids_ref), custom_call_target="tpu_custom_call" | custom-call | tf_op jit(solution)/shard_map/gather_weights/pallas_call | solution.py:1458
  47.1 2.2 copy-done
  50.8 2.0 copy.93
  55.2 3.6 copy.92
  63.7 15.3 %front.1 = (bf16[1056,1536]{1,0:T(8,128)(2,1)}, bf16[1024,1536]{1,0:T(8,128)(2,1)}, f32[1024,1536]{1,0:T(8,128)}, f32[1024,80]{1,0:T(8,128)}, bf16[1056,768]{1,0:T(8,128)(2,1)}) custom-call(bf16[1024,768]{1,0:T(8,128)(2,1)} %bitcast.77, bf16[32,768]{1,0:T(8,128)(2,1)} %copy-done.2, f32[1,768]{1,0:T(1,128)} %reshape.266.gain_ref, bf16[768,3072]{1,0:T(8,128)(2,1)} %copy-done, ...), custom_call_target="tpu_custom_call" | custom-call | tf_op jit(solution)/shard_map/front/pallas_call | solution.py:603
  79.0 1.8 slice.211.rate_ref
  80.7 1.5 subtract_convert_fusion
  84.9 66.7 %forward_scan.1 = (f32[1024,1536]{1,0:T(8,128)}, f32[1024,1536]{1,0:T(8,128)}, bf16[1024,1536]{1,0:T(8,128)(2,1)}, f32[12,16,8,128]{3,2,1,0:T(8,128)}, f32[12,8,...) custom-call(bf16[1024,48]{1,0:T(8,128)(2,1)} %slice.211.rate_ref, bf16[48,1536]{1,0:T(8,128)(2,1)} %slice.124.wdt_ref, ...), custom_call_target="tpu_custom_call" | custom-call | tf_op jit(solution)/shard_map/forward_scan/pallas_call | solution.py:456
  153.3 40.5 %routed.1 = (f32[1024,768]{1,0:T(8,128)}, bf16[1024,896]{1,0:T(8,128)(2,1)}, f32[1024,128]{1,0:T(8,128)}, bf16[4,320,896]{2,1,0:T(8,128)(2,1)}) custom-call(bf16[1024,1536]{1,0:T(8,128)(2,1)} %get-tuple-element.75.mixed_ref, bf16[1536,768]{1,0:T(8,128)(2,1)} %all-gather.2.cloned.1.call-done.wout_ref, bf16[1024,768]{1,0:T(8,128)(2,1)} %bitcast.78, ...), custom_call_target="tpu_custom_call" | custom-call | tf_op jit(solution)/shard_map/routed/pallas_call | solution.py:893
  193.9 46.2 %one_expert.1 = (bf16[1280,768]{1,0:T(8,128)(2,1)}, bf16[1280,896]{1,0:T(8,128)(2,1)}, bf16[768,3072]{1,0:T(8,128)(2,1)}, bf16[3072,768]{1,0:T(8,128)(2,1)}) custom-call(bf16[1280,896]{1,0:T(8,128)(2,1)} %bitcast.92, bf16[1280,768]{1,0:T(8,128)(2,1)} %bitcast.95, bf16[768,3072]{1,0:T(8,128)(2,1)} %bitcast.90, bf16[3072,768]{1,0:T(8,128)(2,1)} %bitcast.91), custom_call_target="tpu_custom_call" | custom-call | tf_op jit(solution)/shard_map/one_expert/pallas_call | solution.py:802
  240.1 62.5 %collect.1 = (f32[1024,768]{1,0:T(8,128)}, bf16[1024,768]{1,0:T(8,128)(2,1)}, f32[1,768]{1,0:T(1,128)}, f32[128,768]{1,0:T(8,128)}, bf16[2,3,48,3072]{3,2,1,0:T(...) custom-call(bf16[4,320,896]{2,1,0:T(8,128)(2,1)} %bitcast.93, ...), custom_call_target="tpu_custom_call" | custom-call | tf_op jit(solution)/shard_map/collect/pallas_call | solution.py:997
  302.7 5.5 convolution_convert_fusion.outg_ref
  309.8 5.9 fusion.17.mg_ref
  315.7 172.5 %backward_scan.1 = (bf16[1024,3072]{1,0:T(8,128)(2,1)}, bf16[1024,1536]{1,0:T(8,128)(2,1)}, f32[1024,1536]{1,0:T(8,128)}, bf16[80,1536]{1,0:T(8,128)(2,1)}, bf16...) custom-call(f32[1024,1536]{1,0:T(8,128)} %fusion.17.mg_ref, ...), custom_call_target="tpu_custom_call" | custom-call | tf_op jit(solution)/shard_map/backward_scan/pallas_call | solution.py:496
  488.3 24.7 %conv_back.1 = (bf16[1024,3072]{1,0:T(8,128)(2,1)}, f32[64,1536]{1,0:T(8,128)}, bf16[96,1536]{1,0:T(8,128)(2,1)}, f32[384,768]{1,0:T(8,128)}, bf16[2,8,48,3072]{...) custom-call(f32[1024,1536]{1,0:T(8,128)} %get-tuple-element.93.cg_re, ...), custom_call_target="tpu_custom_call", output_to_operand_aliasing={{0}: (8, {}), {4}: (10, {}), {5}: (11, {})} | custom-call | tf_op jit(solution)/shard_map/conv_back/pallas_call | solution.py:718
  513.9 1.3 collective-permute-start
  515.2 1.8 pad_maximum_fusion.small_ref
  517.0 3.4 collective-permute-done
  520.4 1.6 fusion.1.proj_ref
  522.0 127.7 %finish.1 = (f32[768,768]{1,0:T(8,128)}, f32[384,768]{1,0:T(8,128)}, f32[192,384]{1,0:T(8,128)}, f32[8,128,768]{2,1,0:T(8,128)}, bf16[8,128,768]{2,1,0:T(8,128)(...) custom-call(bf16[1024,3072]{1,0:T(8,128)(2,1)} %fusion.1.proj_ref, ...), custom_call_target="tpu_custom_call", output_to_operand_aliasing={{5}: (12, {}), {6}: (13, {})} | custom-call | tf_op jit(solution)/shard_map/finish/pallas_call | solution.py:1315
  649.7 1.3 fusion.16
  652.3 1.3 slice.136
  653.6 1.4 slice_reduce_fusion
  655.0 1.3 slice_bitcast_fusion.2
  656.4 1.5 slice.139
  657.9 1.6 slice_bitcast_fusion.1
  659.4 7.5 %convert.30 = f32[1,768,3072]{2,1,0:T(8,128)} convert(bf16[1,768,3072]{2,1,0:T(8,128)(2,1)} %bitcast.73) | non-fusion elementwise | flops 2359296 | bytes 14155776 | tf_op jit(solution)/shard_map/convert_element_type | solution.py:1786
  667.0 4.5 convert.31
  672.6 1.3 copy-done.5
  673.9 1.7 copy.106
  676.7 1.4 copy.107
  (94 shorter events, 28.1 us)
Async XLA Ops:
  7.2 43.6 %copy-start.13 = (s32[8,128]{1,0:T(8,128)S(1)}, s32[8,128]{1,0:T(8,128)}, u32[]{:S(2)}) copy-start(s32[8,128]{1,0:T(8,128)} %param.22) | copy-start | bytes 12292
  7.2 43.6 %copy-start.14 = (s32[8,128]{1,0:T(8,128)S(1)}, s32[8,128]{1,0:T(8,128)}, u32[]{:S(2)}) copy-start(s32[8,128]{1,0:T(8,128)} %param.21) | copy-start | bytes 12292
  7.2 146.1 %all-gather.2.cloned.1.call-start = ((), (), s32[]{:S(2)}) async-start(), calls=%async_computation | async-start | bytes 2949120 | tf_op jit(solution)/shard_map/all_gather | solution.py:1684
  16.5 1.3 copy-start.1
  17.8 33.0 %copy-start.8 = (bf16[8,128,768]{2,1,0:T(8,128)(2,1)S(1)}, bf16[8,128,768]{2,1,0:T(8,128)(2,1)}, u32[]{:S(2)}) copy-start(bf16[8,128,768]{2,1,0:T(8,128)(2,1)} %param.19) | copy-start | bytes 4718596
  47.1 2.2 copy-start
  49.3 0.6 copy-start.2
  55.0 97.4 %copy-start.3 = (s32[1024,1]{1,0:T(8,128)}, s32[1024,1]{1,0:T(8,128)S(1)}, u32[]{:S(2)}) copy-start(s32[1024,1]{1,0:T(8,128)S(1)} %broadcast_in_dim_reshape.4.route_ref) | copy-start | bytes 12292
  240.1 62.5 %copy-start.4 = (bf16[1024,1536]{1,0:T(8,128)(2,1)S(1)}, bf16[1024,1536]{1,0:T(8,128)(2,1)}, u32[]{:S(2)}) copy-start(bf16[1024,1536]{1,0:T(8,128)(2,1)} %get-tuple-element.75.mixed_ref) | copy-start | bytes 9437188
  302.7 5.5 copy-start.15
  302.7 7.1 %copy-start.7 = (bf16[1536,768]{1,0:T(8,128)(2,1)S(1)}, bf16[1536,768]{1,0:T(8,128)(2,1)}, u32[]{:S(2)}) copy-start(bf16[1536,768]{1,0:T(8,128)(2,1)} %all-gather.2.cloned.1.call-done.wout_ref) | copy-start | bytes 7077892
  488.2 26.9 %copy-start.11 = (bf16[80,1536]{1,0:T(8,128)(2,1)S(1)}, bf16[80,1536]{1,0:T(8,128)(2,1)}, u32[]{:S(2)}) copy-start(bf16[80,1536]{1,0:T(8,128)(2,1)} %get-tuple-element.103) | copy-start | bytes 737284
  488.2 26.9 %copy-start.12 = (bf16[2,8,4,384]{3,1,2,0:T(8,128)(2,1)S(1)}, bf16[2,8,4,384]{3,1,2,0:T(8,128)(2,1)}, u32[]{:S(2)}) copy-start(bf16[2,8,4,384]{3,1,2,0:T(8,128)(2,1)} %copy.86) | copy-start | bytes 147460
  513.9 6.5 collective-permute-start
  659.4 7.5 %slice-start = ((s8[4718592]{0:T(1024)(128)(4,1)}), s8[4194304]{0:T(1024)(128)(4,1)S(1)}, s32[]{:S(2)}) async-start(s8[4718592]{0:T(1024)(128)(4,1)} %bitcast.74), calls=%async_computation.1 | async-start | bytes 8388608
  659.4 7.5 %slice-start.1 = ((s8[4718592]{0:T(1024)(128)(4,1)}), s8[524288]{0:T(1024)(128)(4,1)S(1)}, s32[]{:S(2)}) async-start(s8[4718592]{0:T(1024)(128)(4,1)} %bitcast.74), calls=%async_computation.2 | async-start | bytes 1048576
  667.0 4.5 copy-start.9
  671.5 2.5 copy-start.5
  673.9 2.8 copy-start.6
  676.7 2.1 copy-start.10
Sparse Core Ops, SparseCore 0:
  50.1 23.4 all-gather.1

commit v2 on v1

--- a/solution.py
+++ b/solution.py
@@ -61,7 +61,7 @@
         self.has_before, self.has_after = self.rank > 0, self.rank < self.peers - 1
         self.lag = jnp.minimum(self.rank, self.count)
 
-    def enter(self, devices=1, hosted=None):
+    def enter(self, devices=1):
         spot = lax.axis_index("exp")
         barrier = pltpu.get_barrier_semaphore()
 
@@ -76,11 +76,7 @@
         for hop in range(1, devices):
             pl.semaphore_signal(barrier, inc=1, device_id={"exp": lax.rem(spot + hop, devices)}, device_id_type=MESH)
         neighbours = self.has_before.astype(jnp.int32) + self.has_after.astype(jnp.int32)
-        extra = devices - 1
-        if hosted is not None:
-            hosted.enter(barrier)
-            extra += 2
-        pl.semaphore_wait(barrier, neighbours + extra)
+        pl.semaphore_wait(barrier, neighbours + (devices - 1))
 
     def hop(self, u):
         return pltpu.make_async_remote_copy(
@@ -209,19 +205,10 @@
 
 def backward_kernel(
     mg_ref, gate_ref, z_ref, step_ref, conv_ref, bc_ref, pick_ref, match_ref, a_all, total_ref, start_ref, rate_ref, wdt_ref,
-    bias_ref, skip_ref, back_ref, *refs, states, group, devices, peers,
+    bias_ref, skip_ref, back_ref, outg_ref,
+    gg_ref, low_ref, cg_ref, small_ref, mpg_ref, tok_ref, outo_ref,
+    near_got, passed, far_got, mine, out_send, out_recv, out_load, back_send, back_recv, back_own, kb_ref, b_all, c_all, b_acc, c_acc, kept, dt_grad, g_all, rate_acc, ends, last, got, sent, send_sem, recv_sem, *, states, group, devices,
 ):
-    sources, refs = refs[:2], refs[2:]
-    first_step, spread_steps, _ = hosting_plan(peers, a_all.shape[0])
-    opening = None
-    if first_step:
-        opening, refs = refs[:2], refs[2:]
-    gg_ref, low_ref, cg_ref, small_ref, mpg_ref, tok_ref = refs[:6]
-    landed, result, buffers, host_sems, spread_pair = refs[6:8], refs[8:10], refs[10:14], refs[14:18], refs[18:20]
-    (
-        back_send, back_recv, back_own, kb_ref, b_all, c_all, b_acc, c_acc, kept, dt_grad, g_all, rate_acc, ends, last, got, sent, send_sem,
-        recv_sem,
-    ) = refs[20:]
     at = pl.program_id(0)
     count = a_all.shape[0]
     j = lax.rem(at, count)
@@ -230,11 +217,6 @@
     rank = rate_ref.shape[1]
     zero = jnp.zeros((group, LANES), f32)
     spot = lax.axis_index("exp")
-    shared = HostedSpread(peers, spread_pair, result, 0, spread_steps)
-    hosted = HostedSum(
-        peers, host_sems, sources, landed, buffers, first_step, peers - 1, opening=opening, spread=shared
-    )
-    planned = first_step > 0
 
     def back_copy(hop):
         peer = lax.rem(spot + hop, devices)
@@ -243,13 +225,43 @@
             recv_sem=back_recv.at[hop - 1], device_id={"exp": peer}, device_id_type=MESH,
         )
 
+    near = spot + 1 - 2 * lax.rem(spot, 2)
+    far = lax.rem(spot + 2, 4)
+    across = lax.rem(near + 2, 4)
+    rows_out = mine.shape[0]
+
+    def out_rows(k):
+        return outg_ref.at[pl.ds(pl.multiple_of(k * rows_out, rows_out), rows_out), :]
+
+    def out_move(slot):
+        if slot == 2:
+            source, target, device = passed, far_got, far
+        else:
+            source, target, device = out_rows(across if slot else near), near_got.at[slot], near
+        return pltpu.make_async_remote_copy(
+            src_ref=source, dst_ref=target, send_sem=out_send.at[slot], recv_sem=out_recv.at[slot],
+            device_id={"exp": device}, device_id_type=MESH,
+        )
+
+    def out_loads():
+        return (
+            pltpu.make_async_copy(out_rows(far), passed, out_load.at[0]),
+            pltpu.make_async_copy(out_rows(spot), mine, out_load.at[1]),
+        )
+
+    def out_store():
+        return pltpu.make_async_copy(mine, outo_ref, out_load.at[2])
+
     def own_copy():
         return pltpu.make_async_copy(back_ref.at[spot], tok_ref.at[spot], back_own.at[0])
 
     @pl.when(at == 0)
     def _():
-        carry_of.enter(devices, hosted)
-        hosted.open()
+        carry_of.enter(devices)
+        out_move(1).start()
+        out_move(0).start()
+        for c in out_loads():
+            c.start()
         own_copy().start()
         for hop in range(1, devices):
             back_copy(hop).start()
@@ -263,23 +275,20 @@
             b_acc[t] = none
             c_acc[t] = none
 
-    if planned:
-
-        @pl.when(at == 7)
-        def _():
-            hosted.fetch(jnp.int32(3))
-
-        @pl.when(at == 8)
-        def _():
-            hosted.add(jnp.int32(3))
-
-        @pl.when(jnp.logical_and(lax.rem(at, 2) == 1, jnp.logical_and(at >= 13, at <= 17)))
-        def _():
-            hosted.add(lax.div(at - 5, 2))
-
-        @pl.when(at == 19)
-        def _():
-            shared.hand(jnp.int32(0))
+    @pl.when(at == 1)
+    def _():
+        for c in out_loads():
+            c.wait()
+        out_move(1).wait_recv()
+        passed[...] = (passed[...].astype(f32) + near_got[1].astype(f32)).astype(bf16)
+        out_move(2).start()
+
+    @pl.when(at == 2 * count - 1)
+    def _():
+        out_move(0).wait_recv()
+        out_move(2).wait_recv()
+        mine[...] = (mine[...].astype(f32) + near_got[0].astype(f32) + far_got[...].astype(f32)).astype(bf16)
+        out_store().start()
 
     @pl.when(at < count)
     def _():
@@ -332,17 +341,6 @@
             return state
 
         lax.fori_loop(0, steps // fu, forward, [start_ref[0, n] for n in range(states)])
-        if planned:
-            even = lax.rem(at, 2) == 0
-
-            @pl.when(jnp.logical_and(even, at <= 16))
-            def _():
-                hosted.fetch(lax.div(at - 4, 2))
-
-            @pl.when(jnp.logical_and(even, at >= 20))
-            def _():
-                shared.hand(lax.div(at - 18, 2))
-
         skip = skip_ref[...]
 
         def backward(i, carry):
@@ -388,32 +386,24 @@
     @pl.when(at == 2 * count - 1)
     def _():
         carry_of.leave()
-        if planned:
-            shared.hand(jnp.int32(3))
-        else:
-
-            @pl.loop(0, peers - 1)
-            def _(s):
-                hosted.fetch(s)
-                hosted.add(s)
-
-            @pl.loop(0, peers - 1)
-            def _(s):
-                shared.hand(s)
-
-        hosted.finish()
-        shared.finish(False)
+        out_store().wait()
+        for slot in range(3):
+            out_move(slot).wait_send()
         own_copy().wait()
         for hop in range(1, devices):
             back_copy(hop).wait()
         mpg_ref[:, :rank] = rate_acc[...].astype(bf16)
-        lane = lax.broadcasted_iota(jnp.int32, (LANES, 2 * states), 1)
+        lane = lax.broadcasted_iota(jnp.int32, (2 * LANES, 2 * states), 1)
+        own = lax.broadcasted_iota(jnp.int32, (2 * LANES, 2 * states), 0) // LANES * states
         total = jnp.zeros((steps * group, 2 * states), f32)
         for n in range(states):
-            for column, acc in ((n, b_acc), (states + n, c_acc)):
-                rows = acc[:, n].reshape(steps * group, LANES)
-                pick = (lane == column).astype(f32)
-                total = total + jnp.dot(rows, pick, precision=highest, preferred_element_type=f32)
+            both = [acc[:, n].reshape(steps * group, LANES) for acc in (b_acc, c_acc)]
+            rows = jnp.concatenate(both, 1)
+            pick = jnp.where(lane == own + n, 1.0, 0.0).astype(bf16)
+            high = rows.astype(bf16)
+            rest = (rows - high.astype(f32)).astype(bf16)
+            total = total + jnp.dot(high, pick, preferred_element_type=f32)
+            total = total + jnp.dot(rest, pick, preferred_element_type=f32)
         mpg_ref[:, rank:] = total.astype(bf16)
 
 
@@ -479,22 +469,20 @@
     )(rate_low, w_dt, bias, conv_low, bc, pick, match, a_blocks, gate, skip, cot, target[None, :])
 
 
-def backward_scan(mixed_grad, gate, z, step, conv_low, bc, pick, match, a_blocks, total, start, rate_low, w_dt, bias, skip, back, sources, partial, group, devices):
+def backward_scan(mixed_grad, gate, z, step, conv_low, bc, pick, match, a_blocks, total, start, rate_low, w_dt, bias, skip, back, out_grad, group, devices):
     rows, inner = conv_low.shape
     count, states, _ = a_blocks.shape
     rank = rate_low.shape[1]
     small_rows = -(-(rank + states + 2) // 16) * 16
-    peers, pieces = sources[0].shape[1], [v.shape[2:] for v in sources]
-    first_step, spread_steps, _ = hosting_plan(peers, count)
+    out_piece = (out_grad.shape[0] // devices, out_grad.shape[1])
     dma = pltpu.SemaphoreType.DMA
-    extra = list(sources) + (list(partial) if first_step else [])
     first = lambda at: (0, jnp.minimum(at, count - 1))
     both = lambda at: (0, lax.rem(at, count))
     second = lambda at: (0, jnp.maximum(at - count, 0))
     shape = (count, states, group, LANES)
     big = pltpu.VMEM((rows // group, states, group, LANES), f32)
     return pl.pallas_call(
-        functools.partial(backward_kernel, states=states, group=group, devices=devices, peers=peers),
+        functools.partial(backward_kernel, states=states, group=group, devices=devices),
         grid=(2 * count,),
         in_specs=[
             pl.BlockSpec((rows, LANES), first), pl.BlockSpec((rows, LANES), first), pl.BlockSpec((rows, LANES), first),
@@ -502,29 +490,27 @@
             whole_block(pick.shape), whole_block(match.shape), whole_block(a_blocks.shape), whole_block(total.shape),
             pl.BlockSpec((1, states, group, LANES), lambda at: (jnp.maximum(at - count, 0), 0, 0, 0)),
             whole_block((rows, rank)), pl.BlockSpec((rank, LANES), second), pl.BlockSpec((1, LANES), second),
-            pl.BlockSpec((1, LANES), second), pl.BlockSpec(memory_space=pl.ANY),
-        ]
-        + any_specs(len(extra)),
+            pl.BlockSpec((1, LANES), second), pl.BlockSpec(memory_space=pl.ANY), pl.BlockSpec(memory_space=pl.ANY),
+        ],
         out_specs=[
             pl.BlockSpec((rows, LANES), lambda at: (0, jnp.minimum(at, count - 1) + count)),
             pl.BlockSpec((rows, LANES), second), pl.BlockSpec((rows, LANES), second),
             pl.BlockSpec((small_rows, LANES), second), whole_block((rows, rank + 2 * states)),
-        ]
-        + any_specs(5),
+            pl.BlockSpec(memory_space=pl.ANY), pl.BlockSpec(memory_space=pl.ANY),
+        ],
         out_shape=[
             shape_of((rows, 2 * inner), bf16), shape_of((rows, inner), bf16), shape_of((rows, inner), f32),
             shape_of((small_rows, inner), bf16), shape_of((rows, rank + 2 * states), bf16), shape_of(back.shape, bf16),
-        ]
-        + [shape_of((2, peers - 1 - first_step) + p, bf16) for p in pieces]
-        + [shape_of(v.shape, bf16) for v in sources],
-        scratch_shapes=sum_buffers(pieces) + sum_sems(peers - 1 - first_step) + spread_sems(spread_steps)
-        + [dma((devices - 1,)), dma((devices - 1,)), dma((1,))]
-        + [pltpu.VMEM((rows, LANES), f32), big, big, big, big, big]
+            shape_of(out_piece, bf16),
+        ],
+        scratch_shapes=[pltpu.VMEM((2,) + out_piece, bf16), pltpu.VMEM(out_piece, bf16), pltpu.VMEM(out_piece, bf16)]
+        + [pltpu.VMEM(out_piece, bf16), dma((3,)), dma((3,)), dma((3,)), dma((devices - 1,)), dma((devices - 1,))]
+        + [dma((1,)), pltpu.VMEM((rows, LANES), f32), big, big, big, big, big]
         + [pltpu.VMEM((rows, LANES), f32), pltpu.VMEM((count, rows, LANES), bf16)]
         + [pltpu.VMEM((rows, rank), f32), pltpu.VMEM(shape, f32), pltpu.VMEM(shape, f32)] + carry_scratch(shape),
         compiler_params=pltpu.CompilerParams(collective_id=1, has_side_effects=True, vmem_limit_bytes=64 << 20),
         name="backward_scan",
-    )(mixed_grad, gate, z, step, conv_low, bc, pick, match, a_blocks, total, start, rate_low, w_dt, bias, skip, back, *extra)
+    )(mixed_grad, gate, z, step, conv_low, bc, pick, match, a_blocks, total, start, rate_low, w_dt, bias, skip, back, out_grad)
 
 
 def split_three(v):
@@ -620,48 +606,10 @@
 
 
 def conv_back_kernel(
-    cg_ref, low_ref, mpg_ref, wx_ref, ci_ref, cw_ref, cb_ref, compact_ref, proj_ref, outg_ref, up_in, down_in, pg_ref, ext_ref,
-    small_ref, outo_ref, up_ref, down_ref, rows_f, ext, match_ref, near_got, passed, far_got, send_sem, recv_sem, *spread_pair,
-    halo, group, first_step, last_step,
+    cg_ref, low_ref, mpg_ref, wx_ref, ci_ref, cw_ref, cb_ref, compact_ref, proj_ref, pg_ref, ext_ref, small_ref, rows_f, ext, match_ref,
+    *, halo, group,
 ):
-    spread = None
-    if last_step > first_step:
-        spread = HostedSpread(up_ref.shape[1], spread_pair, (up_ref, down_ref), first_step, last_step)
     broad_match(compact_ref, match_ref)
-    spot = lax.axis_index("exp")
-    near = spot + 1 - 2 * lax.rem(spot, 2)
-    far = lax.rem(spot + 2, 4)
-    across = lax.rem(near + 2, 4)
-    rows_out = outo_ref.shape[0]
-
-    def share_of(k):
-        return pl.ds(pl.multiple_of(k * rows_out, rows_out), rows_out)
-
-    def move(source, target, slot, device):
-        return pltpu.make_async_remote_copy(
-            src_ref=source, dst_ref=target, send_sem=send_sem.at[slot], recv_sem=recv_sem.at[slot],
-            device_id={"exp": device}, device_id_type=MESH,
-        )
-
-    def near_move(slot):
-        return move(outg_ref.at[share_of(across if slot else near)], near_got.at[slot], slot, near)
-
-    def far_move():
-        return move(passed, far_got, 2, far)
-
-    @pl.when(pl.program_id(0) == 0)
-    def _():
-        barrier = pltpu.get_barrier_semaphore()
-        for device in (near, far):
-            pl.semaphore_signal(barrier, inc=1, device_id={"exp": device}, device_id_type=MESH)
-        if spread:
-            spread.enter(barrier)
-        pl.semaphore_wait(barrier, 4 if spread else 2)
-        if spread:
-            spread.open()
-        near_move(1).start()
-        near_move(0).start()
-
     rows = pg_ref.shape[0]
     taps = cw_ref.shape[0]
     grad = cg_ref[...] + lax.dot_general(
@@ -688,54 +636,28 @@
     parts = [x_part] + taps_grad + [jnp.sum(grad, 0, keepdims=True), jnp.zeros((spare, ext.shape[1]), f32)]
     small_ref[...] = jnp.concatenate(parts, 0).astype(bf16)
 
-    @pl.when(pl.program_id(0) == 0)
-    def _():
-        near_move(1).wait_recv()
-        passed[...] = (outg_ref[share_of(far), :].astype(f32) + near_got[1].astype(f32)).astype(bf16)
-        far_move().start()
-        near_move(0).wait_recv()
-        outo_ref[...] = outg_ref[share_of(spot), :].astype(f32) + near_got[0].astype(f32)
-
-    @pl.when(pl.program_id(0) == pl.num_programs(0) - 1)
-    def _():
-        far_move().wait_recv()
-        outo_ref[...] += far_got[...].astype(f32)
-        for slot in range(2):
-            near_move(slot).wait_send()
-        far_move().wait_send()
-        if spread:
-            spread.hand(jnp.int32(first_step))
-            spread.finish(True)
-
-
-def conv_back(cg, conv_low, mpg, w_x, ci, conv_w, conv_b, match, proj, out_grad, results, steps, halo, group, lanes, devices):
-    out_shape = (out_grad.shape[0] // devices, out_grad.shape[1])
-    dma = pltpu.SemaphoreType.DMA
+
+def conv_back(cg, conv_low, mpg, w_x, ci, conv_w, conv_b, match, proj, halo, group, lanes):
     rows, inner = cg.shape
     taps, mixed_width = conv_w.shape[0], w_x.shape[1]
     small_rows = -(-(mixed_width + taps + 1) // 16) * 16
     cols = lambda r: pl.BlockSpec((r, lanes), lambda j: (0, j))
     return pl.pallas_call(
-        functools.partial(conv_back_kernel, halo=halo, group=group, first_step=steps[0], last_step=steps[1]),
+        functools.partial(conv_back_kernel, halo=halo, group=group),
         grid=(inner // lanes,),
         in_specs=[
             cols(rows), cols(rows), whole_block((rows, mixed_width)), pl.BlockSpec((lanes, mixed_width), lambda j: (j, 0)),
             cols(rows + halo), cols(taps), cols(1), whole_block(match.shape),
-            pl.BlockSpec(memory_space=pl.ANY), pl.BlockSpec(memory_space=pltpu.VMEM),
-        ]
-        + any_specs(2),
-        out_specs=[cols(rows), cols(2 * halo), cols(small_rows), whole_block(out_shape)] + any_specs(2),
-        out_shape=[shape_of(proj.shape, bf16), shape_of((2 * halo, inner), f32), shape_of((small_rows, inner), bf16)]
-        + [shape_of(out_shape, f32)]
-        + [shape_of(v.shape, bf16) for v in results],
+            pl.BlockSpec(memory_space=pl.ANY),
+        ],
+        out_specs=[cols(rows), cols(2 * halo), cols(small_rows)],
+        out_shape=[shape_of(proj.shape, bf16), shape_of((2 * halo, inner), f32), shape_of((small_rows, inner), bf16)],
         scratch_shapes=[pltpu.VMEM((rows + halo, lanes), f32), pltpu.VMEM((rows + halo, lanes), f32)]
-        + [pltpu.VMEM((match.shape[1], rows, lanes), f32), pltpu.VMEM((2,) + out_shape, bf16)]
-        + [pltpu.VMEM(out_shape, bf16), pltpu.VMEM(out_shape, bf16), dma((3,)), dma((3,))]
-        + (spread_sems(steps[1] - steps[0]) if steps[1] > steps[0] else []),
-        input_output_aliases={8: 0, 10: 4, 11: 5},
-        compiler_params=pltpu.CompilerParams(collective_id=6, has_side_effects=True, vmem_limit_bytes=vmem_cap),
+        + [pltpu.VMEM((match.shape[1], rows, lanes), f32)],
+        input_output_aliases={8: 0},
+        compiler_params=params(),
         name="conv_back",
-    )(cg, conv_low, mpg, w_x, ci, conv_w, conv_b, match, proj, out_grad, *results)
+    )(cg, conv_low, mpg, w_x, ci, conv_w, conv_b, match, proj)
 
 def expert_kernel(
     rows_ref, cot_ref, up_ref, down_ref, out_ref, back_ref, upg_ref, downg_ref, grad, out_acc, back_acc, active, pre_grad, *, tile
@@ -817,13 +739,11 @@
     )(rows, cot, up, down)
 
 
-def exp_barrier(spot, devices, hosted=None):
+def exp_barrier(spot, devices):
     barrier = pltpu.get_barrier_semaphore()
-    if hosted:
-        hosted.enter(barrier)
     for hop in range(1, devices):
         pl.semaphore_signal(barrier, inc=1, device_id={"exp": lax.rem(spot + hop, devices)}, device_id_type=MESH)
-    pl.semaphore_wait(barrier, devices + 1 if hosted else devices - 1)
+    pl.semaphore_wait(barrier, devices - 1)
 
 
 class Dispatch:
@@ -905,24 +825,13 @@
 
 
 def collect_kernel(
-    sent_ref, target_ref, route_ref, rows_ref, prob_ref, hidden_ref, cot_ref, gain_ref, router_ref, *refs, devices, hops,
-    tile, peers, first_step,
+    sent_ref, target_ref, route_ref, rows_ref, prob_ref, hidden_ref, cot_ref, gain_ref, router_ref,
+    hidden_grad_ref, branch_ref, gain_grad_ref, router_grad_ref, got, total, send_sem, recv_sem, *, devices, hops, tile,
 ):
-    hosted = None
-    if first_step:
-        sources, refs = refs[:2], refs[2:]
-    hidden_grad_ref, branch_ref, gain_grad_ref, router_grad_ref = refs[:4]
-    got, total, send_sem, recv_sem = refs[-4:]
-    if first_step:
-        hosted = HostedSum(
-            peers, refs[12:16], sources, refs[4:6], refs[8:12], 0, first_step, partial=refs[6:8]
-        )
     spot = lax.axis_index("exp")
     capacity = got.shape[1]
     count, width = hidden_ref.shape
-    exp_barrier(spot, devices, hosted)
-    if hosted:
-        hosted.open()
+    exp_barrier(spot, devices)
     copies = []
     for hop in hops:
         peer = lax.rem(spot + hop, devices)
@@ -939,11 +848,8 @@
         return jnp.dot(pick, rows, preferred_element_type=f32)
 
     total[...] = spread_back(spot, sent_ref[spot])
-    for at, (hop, c) in enumerate(zip(hops, copies)):
+    for hop, c in zip(hops, copies):
         c.wait_recv()
-        if hosted and at < first_step - 1:
-            hosted.fetch(jnp.int32(at))
-            hosted.add(jnp.int32(at))
         total[...] += spread_back(lax.rem(spot + devices - hop, devices), got[devices - hop - 1])
     gain_grad_ref[...] = jnp.zeros_like(gain_grad_ref)
     router_grad_ref[...] = jnp.zeros_like(router_grad_ref)
@@ -977,40 +883,28 @@
 
     for c in copies:
         c.wait_send()
-    if hosted:
-        hosted.fetch(jnp.int32(first_step - 1))
-        hosted.add(jnp.int32(first_step - 1))
-        hosted.finish()
-
-
-def collect(blocks, target, route_col, rows, prob, hidden, cot, gain, router_t, sources, first_step, devices):
+
+
+def collect(blocks, target, route_col, rows, prob, hidden, cot, gain, router_t, devices):
     vm = pl.BlockSpec(memory_space=pltpu.VMEM)
     dma = pltpu.SemaphoreType.DMA
     capacity, wide = blocks.shape[1:]
     count, width = hidden.shape
-    peers, pieces = sources[0].shape[1], [v.shape[2:] for v in sources]
-    extra = list(sources) if first_step else []
-    more, scratch = [], []
-    if first_step:
-        more = [shape_of((2, first_step) + p, bf16) for p in pieces] + [shape_of((2,) + p, bf16) for p in pieces]
-        scratch = sum_buffers(pieces) + sum_sems(first_step)
     return pl.pallas_call(
-        functools.partial(collect_kernel, devices=devices, hops=(2, 3, 1), tile=256, peers=peers, first_step=first_step),
-        in_specs=[vm] * 9 + any_specs(len(extra)),
-        out_specs=[vm] * 4 + any_specs(len(more)),
+        functools.partial(collect_kernel, devices=devices, hops=(2, 3, 1), tile=256),
+        in_specs=[vm] * 9,
+        out_specs=[vm] * 4,
         out_shape=[
             shape_of((count, width), f32), shape_of((count, width), bf16), shape_of((1, width), f32),
             shape_of((LANES, width), f32),
-        ]
-        + more,
-        scratch_shapes=scratch
-        + [
+        ],
+        scratch_shapes=[
             pltpu.VMEM((devices - 1, capacity, wide), bf16), pltpu.VMEM((count, wide), f32), dma((devices - 1,)),
             dma((devices - 1,)),
         ],
         compiler_params=pltpu.CompilerParams(collective_id=4, has_side_effects=True, vmem_limit_bytes=vmem_cap),
         name="collect",
-    )(blocks, target[:, None], route_col, rows, prob, hidden, cot, gain, router_t, *extra)
+    )(blocks, target[:, None], route_col, rows, prob, hidden, cot, gain, router_t)
 
 SEGMENTS = 4
 STARTS = (-4, 1, 3, 6)
@@ -1102,10 +996,10 @@
 
 def finish_kernel(
     proj_ref, normed_ref, win_ref, outo_ref, small_ref, gain_ref, token_ref, hiddeng_ref, hidden_ref, rows_ref, target_ref,
-    tok_ref, up_in, down_in,
-    in_sum_ref, out_sum_ref, small_sum_ref, tokens_grad_ref, block_ref, up_ref, down_ref,
+    tok_ref,
+    in_sum_ref, out_sum_ref, small_sum_ref, tokens_grad_ref, block_ref,
     own, total, near_stage, small_all, gain_part, near_in, near_small, far_in, far_small, pass_in, pass_small, sent, landed, near_send, near_recv, far_send, far_recv, ring_send, ring_recv,
-    *spread_pair, peers, bases, sizes, halo, tile, gain_row, first_step, last_step,
+    *, peers, bases, sizes, halo, tile, gain_row,
 ):
     spot = lax.axis_index("exp")
     width, wide = near_in.shape[1:]
@@ -1122,10 +1016,6 @@
     for device in ({"exp": near}, {"exp": far}, {"seq": rings.after}, {"seq": rings.before}):
         pl.semaphore_signal(barrier, inc=1, device_id=device, device_id_type=MESH)
     pl.semaphore_wait(barrier, 4)
-    spread = None
-    if last_step > first_step:
-        spread = HostedSpread(peers, spread_pair, (up_ref, down_ref), first_step, last_step)
-        spread.open()
 
     def columns(k, size):
         return pl.ds(pl.multiple_of(k * size, size), size)
@@ -1179,7 +1069,7 @@
             own[bases[n] + used : bases[n] + sizes[n], :] = jnp.zeros((sizes[n] - used, share), f32)
 
     small_base = bases[3] + folds * third
-    into_own(bases[0], outo_ref[...], False)
+    into_own(bases[0], outo_ref[...].astype(f32), False)
     pad_own(0, folds * rows_out)
     rings.begin(0)
     gain_part[...] = jnp.zeros_like(gain_part)
@@ -1267,13 +1157,6 @@
 
             rings.advance(ring, step)
 
-        if spread:
-            for n in range(last_step - first_step):
-
-                @pl.when(turn == 4 + 6 * n)
-                def _():
-                    spread.hand(jnp.int32(first_step + n))
-
         @pl.when(turn < tiles)
         def _():
             token_tile(turn)
@@ -1295,11 +1178,9 @@
             near_copy(slot, piece).wait_send()
         far_copy(piece).wait_send()
     rings.drain()
-    if spread:
-        spread.finish(True)
-
-
-def finish(proj, normed_ext, w_in, out_own, small, gain, token_low, hidden_grad, hidden_one, moe_rows, target, tok, results, steps, gain_row, group):
+
+
+def finish(proj, normed_ext, w_in, out_own, small, gain, token_low, hidden_grad, hidden_one, moe_rows, target, tok, gain_row, group):
     peers, devices = lax.axis_size("seq"), lax.axis_size("exp")
     count, width = token_low.shape
     wide, rows_out = proj.shape[1] // devices, out_own.shape[0]
@@ -1315,15 +1196,14 @@
     return pl.pallas_call(
         functools.partial(
             finish_kernel, peers=peers, bases=bases, sizes=sizes, halo=normed_ext.shape[0] - count, tile=256,
-            gain_row=gain_row, first_step=steps[0], last_step=steps[1],
+            gain_row=gain_row,
         ),
-        in_specs=[vm] * 12 + any_specs(2),
-        out_specs=[vm] * 5 + any_specs(2),
+        in_specs=[vm] * 12,
+        out_specs=[vm] * 5,
         out_shape=[
             shape_of((width, wide), f32), shape_of((rows_out, wide), f32), shape_of((rows_small, share), f32),
             shape_of((group, count // group, width), f32), shape_of((group, count // group, width), bf16),
-        ]
-        + [shape_of(v.shape, bf16) for v in results],
+        ],
         scratch_shapes=[
             pltpu.VMEM((length, share), f32), pltpu.VMEM((length, share), bf16), pltpu.VMEM((2, width, wide), bf16),
             pltpu.VMEM(small.shape, bf16), pltpu.VMEM((width, LANES), f32),
@@ -1332,13 +1212,11 @@
         + [pltpu.VMEM(s, bf16) for s in shapes]
         + [pltpu.VMEM(s, bf16) for s in shapes]
         + [pltpu.VMEM((SEGMENTS, peers - 1, chunk, share), bf16)] * 2
-        + [dma((2, 5)), dma((2, 5)), dma((5,)), dma((5,)), dma((SEGMENTS, 2 * peers - 2)), dma((SEGMENTS, 2 * peers - 2))]
-        + (spread_sems(steps[1] - steps[0]) if steps[1] > steps[0] else []),
-        input_output_aliases={12: 5, 13: 6},
+        + [dma((2, 5)), dma((2, 5)), dma((5,)), dma((5,)), dma((SEGMENTS, 2 * peers - 2)), dma((SEGMENTS, 2 * peers - 2))],
         compiler_params=pltpu.CompilerParams(collective_id=2, has_side_effects=True, vmem_limit_bytes=64 << 20),
         name="finish",
     )(
-        proj, normed_ext, w_in, out_own, small, gain, token_low, hidden_grad, hidden_one, moe_rows, target[:, None], tok, *results,
+        proj, normed_ext, w_in, out_own, small, gain, token_low, hidden_grad, hidden_one, moe_rows, target[:, None], tok
     )
 
 PIECES = 2
@@ -1469,160 +1347,6 @@
         name="gather_weights",
     )(in_shard, small, edge, ids)
 
-def hosting_plan(peers, count):
-    if peers == 8 and count == 12:
-        return 3, 4, 5
-    return 0, peers - 1, peers - 1
-
-
-class Hosted:
-    def __init__(self, peers, send, recv):
-        place = lax.axis_index("seq")
-        self.peers, self.send, self.recv = peers, send, recv
-        self.position = ring_order(place, peers)
-        self.after = ring_member(lax.rem(self.position + 1, peers), peers)
-        self.before = ring_member(lax.rem(self.position + peers - 1, peers), peers)
-
-    def enter(self, barrier):
-        for device in (self.after, self.before):
-            pl.semaphore_signal(barrier, inc=1, device_id={"seq": device}, device_id_type=MESH)
-
-    def chunk(self, ring, steps):
-        sign = 1 if ring == 0 else -1
-        return lax.rem(self.position + sign * steps + 2 * self.peers, self.peers)
-
-    def remote(self, lane, source, target, slot):
-        return pltpu.make_async_remote_copy(
-            src_ref=source, dst_ref=target, send_sem=self.send.at[lane, slot], recv_sem=self.recv.at[lane, slot],
-            device_id={"seq": self.after if lane % 2 == 0 else self.before}, device_id_type=MESH,
-        )
-
-
-class HostedSum(Hosted):
-    def __init__(self, peers, sems, sources, landed, buffers, first, last, opening=None, partial=None, spread=None):
-        self.load, self.keep = sems[2], sems[3]
-        super().__init__(peers, sems[0], sems[1])
-        self.sources, self.landed, self.first, self.last = sources, landed, first, last
-        self.own, self.got = buffers[:2], buffers[2:]
-        self.opening, self.partial, self.spread = opening, partial, spread
-        self.lanes = [(2 * a + ring, a, ring) for a in range(2) for ring in range(2)]
-
-    def opened(self, lane, a, ring):
-        source = self.opening[a].at[ring] if self.opening else self.sources[a].at[ring, self.chunk(ring, -self.first)]
-        return self.remote(lane, source, self.landed[a].at[ring, 0], 0)
-
-    def passing(self, lane, a, ring, s):
-        slot = s - self.first
-        return self.remote(lane, self.own[a].at[ring, lax.rem(s, 2)], self.landed[a].at[ring, slot], slot)
-
-    def loads(self, lane, a, ring, s):
-        return (
-            pltpu.make_async_copy(self.landed[a].at[ring, s - self.first], self.got[a].at[ring], self.load.at[lane, 0]),
-            pltpu.make_async_copy(
-                self.sources[a].at[ring, self.chunk(ring, -s - 1)], self.own[a].at[ring, lax.rem(s + 1, 2)],
-                self.load.at[lane, 1],
-            ),
-        )
-
-    def kept(self, lane, a, ring):
-        source = self.own[a].at[ring, self.last % 2]
-        if self.partial:
-            return pltpu.make_async_copy(source, self.partial[a].at[ring], self.keep.at[lane])
-        return pltpu.make_async_copy(source, self.spread.result[a].at[ring, self.chunk(ring, 1)], self.keep.at[lane])
-
-    def closing(self, lane, a, ring):
-        target = self.spread.result[a].at[ring, self.chunk(ring, 1)]
-        return self.spread.remote(lane, self.own[a].at[ring, self.last % 2], target, 0)
-
-    def open(self):
-        for q in self.lanes:
-            self.opened(*q).start()
-
-    def fetch(self, s):
-        for q in self.lanes:
-            self.passing(*q, s).wait_recv()
-
-            @pl.when(s >= self.first + 2)
-            def _():
-                self.passing(*q, s - 1).wait_send()
-
-            for c in self.loads(*q, s):
-                c.start()
-
-    def add(self, s):
-        for q in self.lanes:
-            lane, a, ring = q
-            for c in self.loads(*q, s):
-                c.wait()
-            slot = lax.rem(s + 1, 2)
-            self.own[a][ring, slot] = (self.own[a][ring, slot].astype(f32) + self.got[a][ring].astype(f32)).astype(bf16)
-
-            @pl.when(s < self.last - 1)
-            def _():
-                self.passing(*q, s + 1).start()
-
-            @pl.when(s == self.last - 1)
-            def _():
-                self.kept(*q).start()
-                if self.spread:
-                    self.closing(*q).start()
-
-    def finish(self):
-        for q in self.lanes:
-            self.opened(*q).wait_send()
-            if self.last - 1 > self.first:
-                self.passing(*q, self.last - 1).wait_send()
-            self.kept(*q).wait()
-            if self.spread:
-                self.closing(*q).wait_send()
-
-
-class HostedSpread(Hosted):
-    def __init__(self, peers, sems, result, first, last):
-        super().__init__(peers, sems[0], sems[1])
-        self.result, self.first, self.last = result, first, last
-        self.lanes = [(2 * a + ring, a, ring) for a in range(2) for ring in range(2)]
-
-    def handing(self, lane, a, ring, s):
-        part = self.result[a].at[ring, self.chunk(ring, 1 - s)]
-        return self.remote(lane, part, part, s - self.first)
-
-    def open(self):
-        for q in self.lanes:
-            self.handing(*q, self.first).start()
-
-    def hand(self, s):
-        for q in self.lanes:
-            self.handing(*q, s).wait_recv()
-
-            @pl.when(s < self.last - 1)
-            def _():
-                self.handing(*q, s + 1).start()
-
-    def finish(self, opened):
-        for q in self.lanes:
-
-            @pl.loop(self.first + (0 if opened else 1), self.last)
-            def _(s):
-                self.handing(*q, s).wait_send()
-
-
-def any_specs(count):
-    return [pl.BlockSpec(memory_space=pl.ANY)] * count
-
-
-def sum_buffers(pieces):
-    return [pltpu.VMEM((2, 2) + p, bf16) for p in pieces] + [pltpu.VMEM((2,) + p, bf16) for p in pieces]
-
-
-def sum_sems(steps):
-    dma = pltpu.SemaphoreType.DMA
-    return [dma((4, steps)), dma((4, steps)), dma((4, 2)), dma((4,))]
-
-
-def spread_sems(steps):
-    return [pltpu.SemaphoreType.DMA((4, steps)), pltpu.SemaphoreType.DMA((4, steps))]
-
 def rms_norm(values, gain):
     return values * lax.rsqrt(jnp.mean(values * values, -1, keepdims=True) + epsilon) * gain
 
@@ -1727,22 +1451,33 @@
         received.reshape(devices * capacity, width + LANES), cot_recv.reshape(devices * capacity, width),
         expert_up[0], expert_down[0],
     )
+    hidden_grad, branch_grad, gain_two_grad, router_grad_t = collect(
+        rows_back.reshape(devices, capacity, width + LANES), target, route_col, moe_rows, prob, hidden_one, cot_rows,
+        gain_two, router_wide.astype(f32).T, devices,
+    )
     peers = lax.axis_size("seq")
-    first_step, spread_first, spread_second = hosting_plan(peers, blocks)
-    sources = [up_grad.reshape(2, peers, -1, up_grad.shape[1]), down_grad.reshape(2, peers, -1, width)]
-    hidden_grad, branch_grad, gain_two_grad, router_grad_t, *hosted = collect(
-        rows_back.reshape(devices, capacity, width + LANES), target, route_col, moe_rows, prob, hidden_one, cot_rows,
-        gain_two, router_wide.astype(f32).T, sources, first_step, devices,
-    )
+    order = [list(range(0, peers, 2)) + list(range(peers - 1, 0, -2))]
+
+    def scattered(values):
+        return lax.psum_scatter(values, "seq", scatter_dimension=0, axis_index_groups=order, tiled=True)
+
+    def regathered(part):
+        return lax.all_gather(part, "seq", axis=0, axis_index_groups=order, tiled=True)
+
+    down_part = scattered(down_grad)
+    up_part = scattered(up_grad)
     out_proj_grad = jnp.dot(mixed_low.T, branch_grad, preferred_element_type=f32)
     mixed_grad = jnp.dot(branch_grad, w_out.T, preferred_element_type=f32)
-    proj, rate_pre_low, cg, small_one, mixed_proj_grad, tok, *hosted = backward_scan(
+    down_part, mixed_grad = lax.optimization_barrier((down_part, mixed_grad))
+    down_sum = regathered(down_part)
+    proj, rate_pre_low, cg, small_one, mixed_proj_grad, tok, out_own = backward_scan(
         mixed_grad, gate, z, step, conv_low, bc, pick, match, a_blocks, total, start, rate_low, w_dt, bias, skip,
-        expert_out.reshape(devices, capacity, width), sources, hosted[2:], group, devices,
-    )
-    proj, ends, small_two, out_own, *results = conv_back(
-        cg, conv_low, mixed_proj_grad, w_x, ci, w_conv, b_conv, match, proj, out_proj_grad.astype(bf16), hosted[2:],
-        (spread_first, spread_second), halo, group, lanes, devices,
+        expert_out.reshape(devices, capacity, width), out_proj_grad.astype(bf16), group, devices,
+    )
+    up_part, cg = lax.optimization_barrier((up_part, cg))
+    up_sum = regathered(up_part)
+    proj, ends, small_two = conv_back(
+        cg, conv_low, mixed_proj_grad, w_x, ci, w_conv, b_conv, match, proj, halo, group, lanes
     )
     edge_back = passed_along(ends[:halo].astype(bf16), "seq", -1).astype(f32)
     proj = lax.dynamic_update_slice(proj, (ends[halo:] + edge_back).astype(bf16), (row_count - halo, 0))
@@ -1753,9 +1488,9 @@
     narrow = jnp.pad(narrow, ((0, -narrow.shape[0] % 16), (0, 0), (0, share - own_width))).astype(bf16)
     packed = jnp.concatenate([small_one, small_two, narrow.reshape(-1, inner_width)], 0)
     gain_row = small_one.shape[0] + small_two.shape[0]
-    in_sum, out_sum, sums, tokens_grad, block_out, up_sum, down_sum = finish(
+    in_sum, out_sum, sums, tokens_grad, block_out = finish(
         proj, normed_ext, w_in, out_own, packed, gain_one, token_low, hidden_grad, hidden_one, moe_rows,
-        target, tok, results, (spread_second, peers - 1), gain_row, group,
+        target, tok, gain_row, group,
     )
     at, own = 0, []
     for first, rows in (
@@ -1783,8 +1518,8 @@
         out_sum,
         own_narrow[1],
         own_narrow[2:].T,
-        up_sum.reshape(expert_up.shape).astype(f32),
-        down_sum.reshape(expert_down.shape).astype(f32),
+        up_sum.astype(f32)[None],
+        down_sum.astype(f32)[None],
     )
 
 

time: 697 us -> 631 us (0.905)
  Pallas kernels: 585 us -> 508 us
  waiting for transfers between devices: 3.39 us -> 17.2 us
    pallas_call x1, Pallas kernels: 173 us -> 145 us  [backward_scan(): pl.pallas_call(functools.partial(backward_kernel, states=states, group=gr...]
    pallas_call x1, Pallas kernels: 62.5 us -> 41.6 us  [collect(): pl.pallas_call(functools.partial(collect_kernel, devices=devices, hops=(2...]
    pallas_call x1, Pallas kernels: 128 us -> 109 us  [finish(): pl.pallas_call(functools.partial(finish_kernel, peers=peers, bases=bases,...]
    broadcast_in_dim x0 -> x2, other arithmetic: none -> 14.3 us  [the longest x1 7.49 us: local(): up_sum.astype(f32)[None]]
    convert_element_type x2 -> x0, other arithmetic: 12 us -> none  [the longest x1 7.52 us: local(): up_sum.reshape(expert_up.shape).astype(f32)]
    reduce_scatter x0 -> x2, waiting for transfers between devices: none -> 11.2 us  [scattered(): lax.psum_scatter(values, 'seq', scatter_dimension=0, axis_index_groups=or...]
    pallas_call x1, Pallas kernels: 24.7 us -> 13.4 us  [conv_back(): pl.pallas_call(functools.partial(conv_back_kernel, halo=halo, group=group...]
  transfers between devices with their start and end apart: 2 -> 6, of which waited for: 1 -> 2; matrix products, arithmetic and copies ran while one was open for 3% -> 9% of each run, Pallas kernels for 12% -> 63%
where the time goes in v2:
time: 631 us; the launch traced here: 627 us
  Pallas kernels  508 us (81%)
  local copies, waits for them, and re-layouts  46.8 us (7%)
  other arithmetic  27 us (4%)
  waiting for transfers between devices  17.2 us (3%)
  between operations  14.4 us (2%)
  matrix products  11.5 us (2%)
    pallas_call x1, Pallas kernels, backward_scan(): pl.pallas_call(functools.partial(backward_kernel, states=states, group=gr...  145 us
    pallas_call x1, Pallas kernels, finish(): pl.pallas_call(functools.partial(finish_kernel, peers=peers, bases=bases,...  109 us
    pallas_call x1, Pallas kernels, forward_scan(): pl.pallas_call(functools.partial(forward_kernel, states=states, group=gro...  66.8 us
    pallas_call x1, Pallas kernels, one_expert(): pl.pallas_call(functools.partial(expert_kernel, tile=tile), grid=(hidden...  46.5 us
    pallas_call x1, Pallas kernels, collect(): pl.pallas_call(functools.partial(collect_kernel, devices=devices, hops=(2...  41.6 us
    pallas_call x1, Pallas kernels, routed(): pl.pallas_call(functools.partial(route_kernel, devices=devices, experts=e...  40.2 us
    pallas_call x1, Pallas kernels, gather_weights(): pl.pallas_call(gather_kernel, in_specs=[pl.BlockSpec(memory_space=pl.ANY)...  29.3 us
    pallas_call x1, Pallas kernels, front(): pl.pallas_call(functools.partial(front_kernel, halo=halo, group=group), g...  15.6 us
  transfers between devices with their start and end apart: 6, of which 2 were waited for; matrix products, arithmetic and copies ran while one was open for 9% of the time, Pallas kernels for 63%

profile of v2, /device:TPU:0, one launch (start us, length us, event | category | flops | bytes accessed | tf_op | source)
XLA Modules:
  0.0 626.5 jit_solution(9052729499278935572)
XLA Ops:
  13.1 3.4 concatenate.25
  17.8 29.3 %gather_weights.1 = (bf16[768,3072]{1,0:T(8,128)(2,1)S(1)}, bf16[160,1536]{1,0:T(8,128)(2,1)S(1)}, bf16[32,768]{1,0:T(8,128)(2,1)S(1)}, s32[8,128]{1,0:T(8,128)S(1)}) custom-call(bf16[768,768]{1,0:T(8,128)(2,1)S(1)} %copy-done.1, bf16[160,384]{1,0:T(8,128)(2,1)S(1)} %pad.17.small_ref, bf16[32,768]{1,0:T(8,128)(2,1)S(1)} %bitcast.71, s32[8,128]{1,0:T(8,128)S(1)} %pad.18.ids_ref), custom_call_target="tpu_custom_call" | custom-call | tf_op jit(solution)/shard_map/gather_weights/pallas_call | solution.py:1336
  47.1 2.2 copy-done
  50.0 3.5 copy.89
  56.6 2.0 copy.88
  64.2 15.6 %front.1 = (bf16[1056,1536]{1,0:T(8,128)(2,1)}, bf16[1024,1536]{1,0:T(8,128)(2,1)}, f32[1024,1536]{1,0:T(8,128)}, f32[1024,80]{1,0:T(8,128)}, bf16[1056,768]{1,0:T(8,128)(2,1)}) custom-call(bf16[1024,768]{1,0:T(8,128)(2,1)} %bitcast.73, bf16[32,768]{1,0:T(8,128)(2,1)} %copy-done.2, f32[1,768]{1,0:T(1,128)} %reshape.228.gain_ref, bf16[768,3072]{1,0:T(8,128)(2,1)} %copy-done, ...), custom_call_target="tpu_custom_call" | custom-call | tf_op jit(solution)/shard_map/front/pallas_call | solution.py:589
  79.8 1.8 slice.211.rate_ref
  81.6 1.5 subtract_convert_fusion
  85.7 66.8 %forward_scan.1 = (f32[1024,1536]{1,0:T(8,128)}, f32[1024,1536]{1,0:T(8,128)}, bf16[1024,1536]{1,0:T(8,128)(2,1)}, f32[12,16,8,128]{3,2,1,0:T(8,128)}, f32[12,8,...) custom-call(bf16[1024,48]{1,0:T(8,128)(2,1)} %slice.211.rate_ref, bf16[48,1536]{1,0:T(8,128)(2,1)} %slice.124.wdt_ref, ...), custom_call_target="tpu_custom_call" | custom-call | tf_op jit(solution)/shard_map/forward_scan/pallas_call | solution.py:446
  152.5 40.2 %routed.1 = (f32[1024,768]{1,0:T(8,128)}, bf16[1024,896]{1,0:T(8,128)(2,1)}, f32[1024,128]{1,0:T(8,128)}, bf16[4,320,896]{2,1,0:T(8,128)(2,1)}) custom-call(bf16[1024,1536]{1,0:T(8,128)(2,1)} %get-tuple-element.71.mixed_ref, bf16[1536,768]{1,0:T(8,128)(2,1)} %all-gather.4.cloned.1.call-done.wout_ref, bf16[1024,768]{1,0:T(8,128)(2,1)} %bitcast.74, ...), custom_call_target="tpu_custom_call" | custom-call | tf_op jit(solution)/shard_map/routed/pallas_call | solution.py:813
  192.7 46.5 %one_expert.1 = (bf16[1280,768]{1,0:T(8,128)(2,1)}, bf16[1280,896]{1,0:T(8,128)(2,1)}, bf16[768,3072]{1,0:T(8,128)(2,1)}, bf16[3072,768]{1,0:T(8,128)(2,1)}) custom-call(bf16[1280,896]{1,0:T(8,128)(2,1)} %bitcast.84, bf16[1280,768]{1,0:T(8,128)(2,1)} %bitcast.87, bf16[768,3072]{1,0:T(8,128)(2,1)} %bitcast.82, bf16[3072,768]{1,0:T(8,128)(2,1)} %bitcast.83), custom_call_target="tpu_custom_call" | custom-call | tf_op jit(solution)/shard_map/one_expert/pallas_call | solution.py:724
  242.2 41.6 %collect.1 = (f32[1024,768]{1,0:T(8,128)}, bf16[1024,768]{1,0:T(8,128)(2,1)}, f32[1,768]{1,0:T(1,128)}, f32[128,768]{1,0:T(8,128)}) custom-call(bf16[4,320,896]{2,1,0:T(8,128)(2,1)} %bitcast.85, s32[1024,1]{1,0:T(8,128)} %add_select_fusion.target_ref, s32[1024,1]{1,0:T(8,128)} %broadcast_in_dim_reshape.4.route_ref, ...), custom_call_target="tpu_custom_call" | custom-call | tf_op jit(solution)/shard_map/collect/pallas_call | solution.py:893
  283.8 6.1 fusion.17.mg_ref
  289.9 11.2 %reduce-scatter.5.cloned.1.call-done = bf16[384,768]{1,0:T(8,128)(2,1)} async-done(((bf16[3072,768]{1,0:T(8,128)(2,1)}), bf16[384,768]{1,0:T(8,128)(2,1)}) %reduce-scatter.5.cloned.1.call-update) | async-done | bytes 589840 | tf_op jit(solution)/shard_map/reduce_scatter | solution.py:1462
  301.4 5.4 convolution_convert_fusion.outg_ref
  306.8 144.9 %backward_scan.1 = (bf16[1024,3072]{1,0:T(8,128)(2,1)}, bf16[1024,1536]{1,0:T(8,128)(2,1)}, f32[1024,1536]{1,0:T(8,128)}, bf16[80,1536]{1,0:T(8,128)(2,1)}, bf16...) custom-call(f32[1024,1536]{1,0:T(8,128)} %fusion.17.mg_ref, ...), custom_call_target="tpu_custom_call" | custom-call | tf_op jit(solution)/shard_map/backward_scan/pallas_call | solution.py:484
  453.4 13.4 %conv_back.1 = (bf16[1024,3072]{1,0:T(8,128)(2,1)}, f32[64,1536]{1,0:T(8,128)}, bf16[96,1536]{1,0:T(8,128)(2,1)}) custom-call(f32[1024,1536]{1,0:T(8,128)} %get-tuple-element.89.cg_ref, bf16[1024,1536]{1,0:T(8,128)(2,1)} %get-tuple-element.69.conv_ref.low_ref, bf16[1024,80]{1,0:T(8,128)(2,1)} %get-tuple-element.90.mpg_ref, ...), custom_call_target="tpu_custom_call", output_to_operand_aliasing={{0}: (8, {})} | custom-call | tf_op jit(solution)/shard_map/conv_back/pallas_call | solution.py:645
  467.7 1.5 collective-permute-start
  469.3 1.8 pad_maximum_fusion.small_ref
  471.1 5.2 collective-permute-done
  476.3 1.6 fusion.1.proj_ref
  477.9 109.3 %finish.1 = (f32[768,768]{1,0:T(8,128)}, f32[384,768]{1,0:T(8,128)}, f32[192,384]{1,0:T(8,128)}, f32[8,128,768]{2,1,0:T(8,128)}, bf16[8,128,768]{2,1,0:T(8,128)(2,1)}) custom-call(bf16[1024,3072]{1,0:T(8,128)(2,1)} %fusion.1.proj_ref, bf16[1056,768]{1,0:T(8,128)(2,1)} %get-tuple-element.95.normed_ref, bf16[768,3072]{1,0:T(8,128)(2,1)} %copy-done, ...), custom_call_target="tpu_custom_call" | custom-call | tf_op jit(solution)/shard_map/finish/pallas_call | solution.py:1196
  588.5 1.5 slice.139
  590.1 1.4 slice_reduce_fusion
  591.5 1.3 fusion.16
  594.1 1.3 slice_bitcast_fusion.2
  595.4 1.6 slice_bitcast_fusion.1
  597.0 6.8 %bitcast_convert_fusion = f32[1,3072,768]{2,1,0:T(8,128)} fusion(bf16[3072,768]{1,0:T(8,128)(2,1)} %all-gather.8.cloned.1.call-done), kind=kLoop, calls=%fused_computation | loop fusion | flops 2359296 | bytes 14155776 | tf_op jit(solution)/shard_map/broadcast_in_dim | solution.py:1522
  603.8 7.5 %bitcast_convert_fusion.1 = f32[1,768,3072]{2,1,0:T(8,128)} fusion(bf16[768,3072]{1,0:T(8,128)(2,1)} %all-gather.6.cloned.1.call-done), kind=kLoop, calls=%fused_computation.1 | loop fusion | flops 2359296 | bytes 14155776 | tf_op jit(solution)/shard_map/broadcast_in_dim | solution.py:1521
  612.5 1.3 copy-done.5
  613.8 1.7 copy.98
  616.6 1.4 copy.99
  (97 shorter events, 31.5 us)
Async XLA Ops:
  7.2 145.3 %all-gather.4.cloned.1.call-start = ((), (), s32[]{:S(2)}) async-start(), calls=%async_computation.2 | async-start | bytes 2949120 | tf_op jit(solution)/shard_map/all_gather | solution.py:1408
  16.5 1.3 copy-start.1
  17.8 36.9 %copy-start.12 = (s32[8,128]{1,0:T(8,128)S(1)}, s32[8,128]{1,0:T(8,128)}, u32[]{:S(2)}) copy-start(s32[8,128]{1,0:T(8,128)} %param.21) | copy-start | bytes 12292
  17.8 36.9 %copy-start.13 = (s32[8,128]{1,0:T(8,128)S(1)}, s32[8,128]{1,0:T(8,128)}, u32[]{:S(2)}) copy-start(s32[8,128]{1,0:T(8,128)} %param.22) | copy-start | bytes 12292
  47.1 2.2 copy-start
  49.3 0.6 copy-start.2
  49.9 6.7 %copy-start.8 = (bf16[8,128,768]{2,1,0:T(8,128)(2,1)S(1)}, bf16[8,128,768]{2,1,0:T(8,128)(2,1)}, u32[]{:S(2)}) copy-start(bf16[8,128,768]{2,1,0:T(8,128)(2,1)} %param.37) | copy-start | bytes 4718596
  49.9 251.2 %reduce-scatter.5.cloned.1.call-start = ((), (), s32[]{:S(2)}) async-start(), calls=%async_computation.4 | async-start | bytes 5308416 | tf_op jit(solution)/shard_map/reduce_scatter | solution.py:1462
  239.2 2.1 copy-start.3
  239.2 212.4 %reduce-scatter.3.cloned.1.call-start = ((), (), s32[]{:S(2)}) async-start(), calls=%async_computation.3 | async-start | bytes 5308416 | tf_op jit(solution)/shard_map/reduce_scatter | solution.py:1462
  240.0 357.0 %all-gather.8.cloned.1.call-start = ((), (), s32[]{:S(2)}) async-start(), calls=%async_computation.6 | async-start | bytes 5308416 | tf_op jit(solution)/shard_map/all_gather | solution.py:1465
  242.2 41.6 %copy-start.7 = (bf16[1536,768]{1,0:T(8,128)(2,1)S(1)}, bf16[1536,768]{1,0:T(8,128)(2,1)}, u32[]{:S(2)}) copy-start(bf16[1536,768]{1,0:T(8,128)(2,1)} %all-gather.4.cloned.1.call-done.wout_ref) | copy-start | bytes 7077892
  283.8 17.6 %copy-start.4 = (bf16[1024,1536]{1,0:T(8,128)(2,1)S(1)}, bf16[1024,1536]{1,0:T(8,128)(2,1)}, u32[]{:S(2)}) copy-start(bf16[1024,1536]{1,0:T(8,128)(2,1)} %get-tuple-element.71.mixed_ref) | copy-start | bytes 9437188
  301.1 302.7 %all-gather.6.cloned.1.call-start = ((), (), s32[]{:S(2)}) async-start(), calls=%async_computation.5 | async-start | bytes 5308416 | tf_op jit(solution)/shard_map/all_gather | solution.py:1465
  453.4 15.9 %copy-start.11 = (bf16[80,1536]{1,0:T(8,128)(2,1)S(1)}, bf16[80,1536]{1,0:T(8,128)(2,1)}, u32[]{:S(2)}) copy-start(bf16[80,1536]{1,0:T(8,128)(2,1)} %get-tuple-element.97) | copy-start | bytes 737284
  467.7 8.6 %collective-permute-start = (bf16[32,1536]{1,0:T(8,128)(2,1)S(1)}, bf16[32,1536]{1,0:T(8,128)(2,1)S(1)}, u32[]{:S(2)}, u32[]{:S(2)}) collective-permute-start(bf16[32,1536]{1,0:T(8,128)(2,1)S(1)} %slice.213), channel_id=1, source_target_pairs={{4,0},{8,4},{12,8},{16,12},{20,16},{24,20},{28,24},{5,1},{9,5},{13... | collective-permute-start | bytes 294920 | tf_op jit(solution)/shard_map/ppermute | solution.py:1357
  603.8 7.5 %copy-start.9 = (bf16[8,128,768]{2,1,0:T(8,128)(2,1)S(1)}, bf16[8,128,768]{2,1,0:T(8,128)(2,1)}, u32[]{:S(2)}) copy-start(bf16[8,128,768]{2,1,0:T(8,128)(2,1)} %get-tuple-element.142) | copy-start | bytes 4718596
  611.3 2.5 copy-start.5
  613.8 2.8 copy-start.6
  616.6 2.1 copy-start.10
Sparse Core Ops, SparseCore 0:
  50.1 23.4 all-gather.3
  239.4 61.7 reduce-scatter.4
  303.4 59.3 reduce-scatter.2
  364.2 57.2 all-gather.7
  451.8 61.3 all-gather.5

commit v3 on v2

--- a/solution.py
+++ b/solution.py
@@ -30,6 +30,10 @@
 
 
 def spread(rows_ref, pick_ref, outs, states, group):
+    shape = pick_ref.shape
+    row = lax.broadcasted_iota(jnp.int32, shape, 0)
+    lane = lax.broadcasted_iota(jnp.int32, shape, 1)
+    pick_ref[...] = jnp.where(lax.rem(row, 2 * states) == lax.div(lane, LANES), 1.0, 0.0).astype(bf16)
     steps = rows_ref.shape[0] // group
     chunk = 16
     wide = 2 * LANES
@@ -114,9 +118,9 @@
 
 
 def forward_kernel(
-    rate_ref, wdt_ref, bias_ref, conv_ref, bc_ref, pick_ref, match_ref, a_all, gate_ref, skip_ref, cot_ref, target_ref,
+    rate_ref, wdt_ref, bias_ref, conv_ref, bc_ref, match_ref, a_all, gate_ref, skip_ref, cot_ref, target_ref,
     step_ref, z_ref, mixed_ref, start_ref, total_ref, cot_out,
-    cot_got, kb_ref, b_all, c_all, step_all, ends, staged, cot_send, cot_recv, got, sent, send_sem, recv_sem, *, states, group, devices,
+    cot_got, pick_ref, kb_ref, b_all, c_all, step_all, ends, staged, cot_send, cot_recv, got, sent, send_sem, recv_sem, *, states, group, devices,
 ):
     at = pl.program_id(0)
     count = a_all.shape[0]
@@ -204,10 +208,10 @@
 
 
 def backward_kernel(
-    mg_ref, gate_ref, z_ref, step_ref, conv_ref, bc_ref, pick_ref, match_ref, a_all, total_ref, start_ref, rate_ref, wdt_ref,
+    mg_ref, gate_ref, z_ref, step_ref, conv_ref, bc_ref, match_ref, a_all, total_ref, start_ref, rate_ref, wdt_ref,
     bias_ref, skip_ref, back_ref, outg_ref,
     gg_ref, low_ref, cg_ref, small_ref, mpg_ref, tok_ref, outo_ref,
-    near_got, passed, far_got, mine, out_send, out_recv, out_load, back_send, back_recv, back_own, kb_ref, b_all, c_all, b_acc, c_acc, kept, dt_grad, g_all, rate_acc, ends, last, got, sent, send_sem, recv_sem, *, states, group, devices,
+    near_got, passed, far_got, mine, out_send, out_recv, out_load, back_send, back_recv, back_own, pick_ref, kb_ref, b_all, c_all, b_acc, c_acc, kept, dt_grad, g_all, rate_acc, ends, last, got, sent, send_sem, recv_sem, *, states, group, devices,
 ):
     at = pl.program_id(0)
     count = a_all.shape[0]
@@ -434,7 +438,7 @@
     ]
 
 
-def forward_scan(rate_low, w_dt, bias, conv_low, bc, pick, match, a_blocks, gate, skip, cot, target, capacity, group, devices):
+def forward_scan(rate_low, w_dt, bias, conv_low, bc, match, a_blocks, gate, skip, cot, target, capacity, group, devices):
     rows, inner = conv_low.shape
     count, states, _ = a_blocks.shape
     rank = rate_low.shape[1]
@@ -448,7 +452,7 @@
         grid=(2 * count,),
         in_specs=[
             whole_block((rows, rank)), pl.BlockSpec((rank, LANES), first), pl.BlockSpec((1, LANES), first),
-            pl.BlockSpec((rows, LANES), both), whole_block(bc.shape), whole_block(pick.shape),
+            pl.BlockSpec((rows, LANES), both), whole_block(bc.shape),
             whole_block(match.shape), whole_block(a_blocks.shape), pl.BlockSpec((rows, LANES), second),
             pl.BlockSpec((1, LANES), second), whole_block(cot.shape), whole_block((1, rows)),
         ],
@@ -460,16 +464,17 @@
             shape_of((rows, inner), f32), shape_of((rows, inner), f32), shape_of((rows, inner), bf16),
             shape_of(shape, f32), shape_of((count, group, LANES), f32), shape_of((devices, capacity, cot.shape[1]), bf16),
         ],
-        scratch_shapes=[pltpu.VMEM((devices, capacity, cot.shape[1]), bf16), pltpu.VMEM((rows, LANES), f32), big, big]
+        scratch_shapes=[pltpu.VMEM((devices, capacity, cot.shape[1]), bf16), pltpu.VMEM((bc.shape[1], 2 * states * LANES), bf16)]
+        + [pltpu.VMEM((rows, LANES), f32), big, big]
         + [pltpu.VMEM((count, rows, LANES), f32), pltpu.VMEM(shape, f32)]
         + [pltpu.VMEM((devices - 1, capacity, cot.shape[1]), bf16)]
         + [pltpu.SemaphoreType.DMA((devices - 1,)), pltpu.SemaphoreType.DMA((devices - 1,))] + carry_scratch(shape),
         compiler_params=pltpu.CompilerParams(collective_id=0, has_side_effects=True, vmem_limit_bytes=vmem_cap),
         name="forward_scan",
-    )(rate_low, w_dt, bias, conv_low, bc, pick, match, a_blocks, gate, skip, cot, target[None, :])
-
-
-def backward_scan(mixed_grad, gate, z, step, conv_low, bc, pick, match, a_blocks, total, start, rate_low, w_dt, bias, skip, back, out_grad, group, devices):
+    )(rate_low, w_dt, bias, conv_low, bc, match, a_blocks, gate, skip, cot, target[None, :])
+
+
+def backward_scan(mixed_grad, gate, z, step, conv_low, bc, match, a_blocks, total, start, rate_low, w_dt, bias, skip, back, out_grad, group, devices):
     rows, inner = conv_low.shape
     count, states, _ = a_blocks.shape
     rank = rate_low.shape[1]
@@ -487,7 +492,7 @@
         in_specs=[
             pl.BlockSpec((rows, LANES), first), pl.BlockSpec((rows, LANES), first), pl.BlockSpec((rows, LANES), first),
             pl.BlockSpec((rows, LANES), both), pl.BlockSpec((rows, LANES), second), whole_block(bc.shape),
-            whole_block(pick.shape), whole_block(match.shape), whole_block(a_blocks.shape), whole_block(total.shape),
+            whole_block(match.shape), whole_block(a_blocks.shape), whole_block(total.shape),
             pl.BlockSpec((1, states, group, LANES), lambda at: (jnp.maximum(at - count, 0), 0, 0, 0)),
             whole_block((rows, rank)), pl.BlockSpec((rank, LANES), second), pl.BlockSpec((1, LANES), second),
             pl.BlockSpec((1, LANES), second), pl.BlockSpec(memory_space=pl.ANY), pl.BlockSpec(memory_space=pl.ANY),
@@ -505,25 +510,12 @@
         ],
         scratch_shapes=[pltpu.VMEM((2,) + out_piece, bf16), pltpu.VMEM(out_piece, bf16), pltpu.VMEM(out_piece, bf16)]
         + [pltpu.VMEM(out_piece, bf16), dma((3,)), dma((3,)), dma((3,)), dma((devices - 1,)), dma((devices - 1,))]
-        + [dma((1,)), pltpu.VMEM((rows, LANES), f32), big, big, big, big, big]
+        + [dma((1,)), pltpu.VMEM((bc.shape[1], 2 * states * LANES), bf16), pltpu.VMEM((rows, LANES), f32), big, big, big, big, big]
         + [pltpu.VMEM((rows, LANES), f32), pltpu.VMEM((count, rows, LANES), bf16)]
         + [pltpu.VMEM((rows, rank), f32), pltpu.VMEM(shape, f32), pltpu.VMEM(shape, f32)] + carry_scratch(shape),
         compiler_params=pltpu.CompilerParams(collective_id=1, has_side_effects=True, vmem_limit_bytes=64 << 20),
         name="backward_scan",
-    )(mixed_grad, gate, z, step, conv_low, bc, pick, match, a_blocks, total, start, rate_low, w_dt, bias, skip, back, out_grad)
-
-
-def split_three(v):
-    high = v.astype(bf16)
-    rest = v - high.astype(f32)
-    mid = rest.astype(bf16)
-    low = (rest - mid.astype(f32)).astype(bf16)
-    return jnp.concatenate([high, mid, low], -1)
-
-
-def pick_matrix(columns):
-    eye = (jnp.arange(columns)[:, None] == jnp.arange(columns * LANES)[None, :] // LANES).astype(bf16)
-    return jnp.concatenate([eye] * 3, 0)
+    )(mixed_grad, gate, z, step, conv_low, bc, match, a_blocks, total, start, rate_low, w_dt, bias, skip, back, out_grad)
 
 def broad_match(match_ref, wide):
     @pl.when(pl.program_id(0) == 0)
@@ -533,8 +525,8 @@
 
 
 def front_kernel(
-    token_ref, before_ref, gain_ref, wc_ref, wg_ref, cw_ref, cb_ref, compact_ref, wx_ref, ci_ref, low_ref, gate_ref, mixed_ref,
-    normed_ref, rows_f, match_ref, *, halo, group,
+    token_ref, before_ref, gain_ref, wc_ref, wg_ref, cw_ref, cb_ref, compact_ref, wx_ref, ci_ref, low_ref, gate_ref, rate_ref, bc_ref,
+    normed_ref, mixed_ref, rows_f, match_ref, *, halo, group,
 ):
     rows = low_ref.shape[0]
     broad_match(compact_ref, match_ref)
@@ -571,6 +563,16 @@
     def _():
         mixed_ref[...] += part
 
+    @pl.when(pl.program_id(0) == pl.num_programs(0) - 1)
+    def _():
+        rank, wide = rate_ref.shape[1], bc_ref.shape[1] // 3
+        rate_ref[...] = mixed_ref[:, :rank].astype(bf16)
+        rest = mixed_ref[:, rank:]
+        for k in range(3):
+            part_low = rest.astype(bf16)
+            bc_ref[:, k * wide : (k + 1) * wide] = part_low
+            rest = rest - part_low.astype(f32)
+
 
 def conv_total(rows_f, cw_ref, cb_ref, match_ref, halo, group, rows, taps):
     total = cb_ref[...] + cw_ref[taps - 1 : taps, :] * rows_f[halo : halo + rows, :]
@@ -580,7 +582,7 @@
     return total
 
 
-def front(token_low, before_rows, gain, w_in, conv_w, conv_b, match, w_x, halo, group, lanes):
+def front(token_low, before_rows, gain, w_in, conv_w, conv_b, match, w_x, rank, halo, group, lanes):
     width, inner = w_in.shape[0], w_in.shape[1] // 2
     total_rows = token_low.shape[0] + halo
     rows, taps, mixed_width = total_rows - halo, conv_w.shape[0], w_x.shape[1]
@@ -594,12 +596,15 @@
             pl.BlockSpec((width, lanes), lambda j: (0, j + count)),
             cols(taps), cols(1), whole_block(match.shape), pl.BlockSpec((lanes, mixed_width), lambda j: (j, 0)),
         ],
-        out_specs=[cols(total_rows), cols(rows), cols(rows), whole_block((rows, mixed_width)), whole_block((total_rows, width))],
+        out_specs=[
+            cols(total_rows), cols(rows), cols(rows), whole_block((rows, rank)), whole_block((rows, 3 * (mixed_width - rank))),
+            whole_block((total_rows, width)),
+        ],
         out_shape=[
             shape_of((total_rows, inner), bf16), shape_of((rows, inner), bf16), shape_of((rows, inner), f32),
-            shape_of((rows, mixed_width), f32), shape_of((total_rows, width), bf16),
-        ],
-        scratch_shapes=[pltpu.VMEM((total_rows, lanes), f32), pltpu.VMEM((match.shape[1], rows, lanes), f32)],
+            shape_of((rows, rank), bf16), shape_of((rows, 3 * (mixed_width - rank)), bf16), shape_of((total_rows, width), bf16),
+        ],
+        scratch_shapes=[pltpu.VMEM((rows, mixed_width), f32), pltpu.VMEM((total_rows, lanes), f32), pltpu.VMEM((match.shape[1], rows, lanes), f32)],
         compiler_params=params(),
         name="front",
     )(token_low, before_rows, gain, w_in, w_in, conv_w, conv_b, match, w_x)
@@ -907,7 +912,7 @@
     )(blocks, target[:, None], route_col, rows, prob, hidden, cot, gain, router_t)
 
 SEGMENTS = 4
-STARTS = (-4, 1, 3, 6)
+STARTS = (-4, 0, 1, 2)
 
 
 def ring_order(place, peers):
@@ -1222,7 +1227,10 @@
 PIECES = 2
 
 
-def gather_kernel(in_ref, small_ref, edge_ref, ids_ref, win_ref, wsmall_ref, before_ref, before_ids, near_sems, far_sems, pair_sems, edge_sems, own_sem):
+def gather_kernel(
+    in_ref, small_ref, token_ref, cot_ref, ids_ref, win_ref, wsmall_ref, before_ref, before_ids, rows_ref, cot_rows_ref, edge_ref,
+    near_sems, far_sems, pair_sems, edge_sems, own_sem, *, kernel_len,
+):
     place, peers = lax.axis_index("seq"), lax.axis_size("seq")
     spot = lax.axis_index("exp")
     near = spot + 1 - 2 * lax.rem(spot, 2)
@@ -1279,6 +1287,13 @@
     ]
     for c in beside:
         c.start()
+    group, part_len, features = token_ref.shape
+
+    def by_place(source, start, steps):
+        values = source[:, pl.ds(start, steps), :].astype(f32)
+        return jnp.swapaxes(values, 0, 1).reshape(steps * group, features).astype(bf16)
+
+    edge_ref[...] = by_place(token_ref, part_len - 8, 8)[(8 - kernel_len) * group :, :]
 
     @pl.when(has_after)
     def _():
@@ -1296,6 +1311,15 @@
     ]
     for c in own:
         c.start()
+    tile = 16
+
+    @pl.loop(0, part_len // tile)
+    def _(i):
+        start = pl.multiple_of(i * tile, tile)
+        at = pl.ds(pl.multiple_of(i * tile * group, tile * group), tile * group)
+        rows_ref[at, :] = by_place(token_ref, start, tile)
+        cot_rows_ref[at, :] = by_place(cot_ref, start, tile)
+
     outward[0].wait_recv()
     beside.append(copy(columns(wsmall_ref, far, share), columns(wsmall_ref, far, share), near_sems, 2, {"exp": near}))
     beside[-1].start()
@@ -1330,22 +1354,25 @@
             c.wait_send()
 
 
-def gather_weights(in_shard, small, edge, ids, devices):
+def gather_weights(in_shard, small, tokens, cot, ids, kernel_len, devices):
+    group, part_len, width = tokens.shape
+    edge = shape_of((kernel_len * group, width), bf16)
+    rows = shape_of((part_len * group, width), bf16)
     vm = pl.BlockSpec(memory_space=pltpu.VMEM)
     dma = pltpu.SemaphoreType.DMA
     return pl.pallas_call(
-        gather_kernel,
-        in_specs=[pl.BlockSpec(memory_space=pl.ANY), vm, vm, vm],
-        out_specs=[pl.BlockSpec(memory_space=pl.ANY), vm, vm, vm],
+        functools.partial(gather_kernel, kernel_len=kernel_len),
+        in_specs=[pl.BlockSpec(memory_space=pl.ANY), vm, vm, vm, vm],
+        out_specs=[pl.BlockSpec(memory_space=pl.ANY), vm, vm, vm, vm, vm],
         out_shape=[
             shape_of((in_shard.shape[0], in_shard.shape[1] * devices), bf16),
             shape_of((small.shape[0], small.shape[1] * devices), bf16), shape_of(edge.shape, edge.dtype),
-            shape_of(ids.shape, ids.dtype),
-        ],
-        scratch_shapes=[dma((2, 3 + 2 * PIECES)), dma((2, PIECES + 1)), dma((2, PIECES)), dma((2, 2)), dma((2,))],
+            shape_of(ids.shape, ids.dtype), rows, rows,
+        ],
+        scratch_shapes=[pltpu.VMEM(edge.shape, bf16), dma((2, 3 + 2 * PIECES)), dma((2, PIECES + 1)), dma((2, PIECES)), dma((2, 2)), dma((2,))],
         compiler_params=pltpu.CompilerParams(collective_id=5, has_side_effects=True, vmem_limit_bytes=32 << 20),
         name="gather_weights",
-    )(in_shard, small, edge, ids)
+    )(in_shard, small, tokens, cot, ids)
 
 def rms_norm(values, gain):
     return values * lax.rsqrt(jnp.mean(values * values, -1, keepdims=True) + epsilon) * gain
@@ -1396,13 +1423,12 @@
     devices = lax.axis_size("exp")
     doc_ids = segment_ids + 1
     edge_start = part_len - kernel_len
-    token_low = by_time(tokens)
     edge_ids = jnp.pad(doc_ids[:, edge_start:], ((0, 0), (0, LANES - kernel_len)))
     small_shard, counts, narrow_shape = packed_small(
         norm_gain, conv_weight, conv_bias, x_proj, dt_proj, dt_bias, a_log, d_skip, moe_gain, router
     )
-    w_in, small_whole, before_rows, before_ids = gather_weights(
-        in_proj, small_shard, token_low[row_count - halo :], edge_ids, devices
+    w_in, small_whole, before_rows, before_ids, token_low, cot_rows = gather_weights(
+        in_proj, small_shard, tokens, cotangent, edge_ids, kernel_len, devices
     )
     out_proj, small_whole = lax.optimization_barrier((out_proj, small_whole))
     w_out = lax.all_gather(out_proj, "exp", axis=0, tiled=True)
@@ -1425,22 +1451,18 @@
     target = jnp.where(
         slot_rows < capacity, route_rows * capacity + slot_rows, expert_total * capacity
     )
-    cot_rows = by_time(cotangent)
     w_conv, b_conv = w_conv.astype(f32), b_conv.astype(f32)
     w_x = w_x_t.T
-    ci, conv_low, gate, mixed, normed_ext = front(
-        token_low, before_rows, gain_one, w_in, w_conv, b_conv, match, w_x, halo, group, lanes
-    )
-    rate_low = mixed[:, :rank_width].astype(bf16)
-    bc = split_three(mixed[:, rank_width:])
-    pick = pick_matrix(2 * state_width)
+    ci, conv_low, gate, rate_low, bc, normed_ext = front(
+        token_low, before_rows, gain_one, w_in, w_conv, b_conv, match, w_x, rank_width, halo, group, lanes
+    )
     bias = b_dt.astype(f32)
     skip = skip_gain.astype(f32)
     a_mat = -jnp.exp(log_decay.astype(f32))
     a2 = a_mat * log2e
     a_blocks = a2.reshape(state_width, blocks, LANES).transpose(1, 0, 2)
     step, z, mixed_low, start, total, cot_recv = forward_scan(
-        rate_low, w_dt, bias, conv_low, bc, pick, match, a_blocks, gate, skip, cot_rows, target, capacity, group, devices
+        rate_low, w_dt, bias, conv_low, bc, match, a_blocks, gate, skip, cot_rows, target, capacity, group, devices
     )
     route_col = route_rows[:, None]
     router_wide = jnp.pad(w_router, ((0, 0), (0, LANES - expert_total)))
@@ -1468,11 +1490,12 @@
     up_part = scattered(up_grad)
     out_proj_grad = jnp.dot(mixed_low.T, branch_grad, preferred_element_type=f32)
     mixed_grad = jnp.dot(branch_grad, w_out.T, preferred_element_type=f32)
-    down_part, mixed_grad = lax.optimization_barrier((down_part, mixed_grad))
+    out_proj_grad = out_proj_grad.astype(bf16)
+    down_part, mixed_grad, out_proj_grad = lax.optimization_barrier((down_part, mixed_grad, out_proj_grad))
     down_sum = regathered(down_part)
     proj, rate_pre_low, cg, small_one, mixed_proj_grad, tok, out_own = backward_scan(
-        mixed_grad, gate, z, step, conv_low, bc, pick, match, a_blocks, total, start, rate_low, w_dt, bias, skip,
-        expert_out.reshape(devices, capacity, width), out_proj_grad.astype(bf16), group, devices,
+        mixed_grad, gate, z, step, conv_low, bc, match, a_blocks, total, start, rate_low, w_dt, bias, skip,
+        expert_out.reshape(devices, capacity, width), out_proj_grad, group, devices,
     )
     up_part, cg = lax.optimization_barrier((up_part, cg))
     up_sum = regathered(up_part)

time: 631 us -> 616 us (0.976)
  Pallas kernels: 508 us -> 499 us
    pallas_call x1, Pallas kernels: 109 us -> 98.1 us  [finish(): pl.pallas_call(functools.partial(finish_kernel, peers=peers, bases=bases,...]
    unnamed x34 -> x42, local copies, waits for them, and re-layouts: 12.7 us -> 17.8 us
  transfers between devices with their start and end apart: 6 -> 6, of which waited for: 2 -> 2; matrix products, arithmetic and copies ran while one was open for 9% -> 7% of each run, Pallas kernels for 63% -> 63%
where the time goes in v3:
time: 616 us; the launch traced here: 606 us
  Pallas kernels  499 us (81%)
  local copies, waits for them, and re-layouts  43.6 us (7%)
  other arithmetic  23.5 us (4%)
  between operations  14.3 us (2%)
  waiting for transfers between devices  13 us (2%)
  matrix products  10 us (2%)
    pallas_call x1, Pallas kernels, backward_scan(): pl.pallas_call(functools.partial(backward_kernel, states=states, group=gr...  148 us
    pallas_call x1, Pallas kernels, finish(): pl.pallas_call(functools.partial(finish_kernel, peers=peers, bases=bases,...  98.1 us
    pallas_call x1, Pallas kernels, forward_scan(): pl.pallas_call(functools.partial(forward_kernel, states=states, group=gro...  66.7 us
    pallas_call x1, Pallas kernels, one_expert(): pl.pallas_call(functools.partial(expert_kernel, tile=tile), grid=(hidden...  46.2 us
    pallas_call x1, Pallas kernels, collect(): pl.pallas_call(functools.partial(collect_kernel, devices=devices, hops=(2...  41.6 us
    pallas_call x1, Pallas kernels, routed(): pl.pallas_call(functools.partial(route_kernel, devices=devices, experts=e...  40.2 us
    pallas_call x1, Pallas kernels, gather_weights(): pl.pallas_call(functools.partial(gather_kernel, kernel_len=kernel_len), i...  29.3 us
    unnamed x42, local copies, waits for them, and re-layouts  17.8 us
  transfers between devices with their start and end apart: 6, of which 2 were waited for; matrix products, arithmetic and copies ran while one was open for 7% of the time, Pallas kernels for 63%

profile of v3, /device:TPU:0, one launch (start us, length us, event | category | flops | bytes accessed | tf_op | source)
XLA Modules:
  0.0 606.0 jit_solution(8248207821833652455)
XLA Ops:
  12.1 3.4 concatenate.17
  15.6 1.4 copy-done.3
  17.0 1.4 copy-done.4
  19.7 29.3 %gather_weights.1 = (bf16[768,3072]{1,0:T(8,128)(2,1)S(1)}, bf16[160,1536]{1,0:T(8,128)(2,1)S(1)}, bf16[32,768]{1,0:T(8,128)(2,1)S(1)}, s32[8,128]{1,0:T(8,128)S...) custom-call(bf16[768,768]{1,0:T(8,128)(2,1)S(1)} %copy-done.5, bf16[160,384]{1,0:T(8,128)(2,1)S(1)} %pad.17.small_ref, ...), custom_call_target="tpu_custom_call" | custom-call | tf_op jit(solution)/shard_map/gather_weights/pallas_call | solution.py:1363
  48.9 2.2 copy-done
  62.8 15.7 %front.1 = (bf16[1056,1536]{1,0:T(8,128)(2,1)}, bf16[1024,1536]{1,0:T(8,128)(2,1)}, f32[1024,1536]{1,0:T(8,128)}, bf16[1024,48]{1,0:T(8,128)(2,1)}, bf16[1024,96]{1,0:T(8,128)(2,1)}, /*index=5*/bf16[1056,768]{1,0:T(8,128)(2,1)}) custom-call(bf16[1024,768]{1,0:T(8,128)(2,1)} %copy-done.1, bf16[32,768]{1,0:T(8,128)(2,1)} %copy-done.6, ...), custom_call_target="tpu_custom_call" | custom-call | tf_op jit(solution)/shard_map/front/pallas_call | solution.py:591
  79.2 66.7 %forward_scan.1 = (f32[1024,1536]{1,0:T(8,128)}, f32[1024,1536]{1,0:T(8,128)}, bf16[1024,1536]{1,0:T(8,128)(2,1)}, f32[12,16,8,128]{3,2,1,0:T(8,128)}, f32[12,8,...) custom-call(bf16[1024,48]{1,0:T(8,128)(2,1)} %get-tuple-element.73.rate_ref, bf16[48,1536]{1,0:T(8,128)(2,1)} %slice.108.wdt_ref, ...), custom_call_target="tpu_custom_call" | custom-call | tf_op jit(solution)/shard_map/forward_scan/pallas_call | solution.py:450
  145.9 40.2 %routed.1 = (f32[1024,768]{1,0:T(8,128)}, bf16[1024,896]{1,0:T(8,128)(2,1)}, f32[1024,128]{1,0:T(8,128)}, bf16[4,320,896]{2,1,0:T(8,128)(2,1)}) custom-call(bf16[1024,1536]{1,0:T(8,128)(2,1)} %get-tuple-element.78.mixed_ref, bf16[1536,768]{1,0:T(8,128)(2,1)} %all-gather.4.cloned.1.call-done.wout_ref, bf16[1024,768]{1,0:T(8,128)(2,1)} %copy-done.1, ...), custom_call_target="tpu_custom_call" | custom-call | tf_op jit(solution)/shard_map/routed/pallas_call | solution.py:818
  186.1 46.2 %one_expert.1 = (bf16[1280,768]{1,0:T(8,128)(2,1)}, bf16[1280,896]{1,0:T(8,128)(2,1)}, bf16[768,3072]{1,0:T(8,128)(2,1)}, bf16[3072,768]{1,0:T(8,128)(2,1)}) custom-call(bf16[1280,896]{1,0:T(8,128)(2,1)} %bitcast.67, bf16[1280,768]{1,0:T(8,128)(2,1)} %bitcast.70, bf16[768,3072]{1,0:T(8,128)(2,1)} %bitcast.65, bf16[3072,768]{1,0:T(8,128)(2,1)} %bitcast.66), custom_call_target="tpu_custom_call" | custom-call | tf_op jit(solution)/shard_map/one_expert/pallas_call | solution.py:729
  235.6 41.6 %collect.1 = (f32[1024,768]{1,0:T(8,128)}, bf16[1024,768]{1,0:T(8,128)(2,1)}, f32[1,768]{1,0:T(1,128)}, f32[128,768]{1,0:T(8,128)}) custom-call(bf16[4,320,896]{2,1,0:T(8,128)(2,1)} %bitcast.68, s32[1024,1]{1,0:T(8,128)} %add_select_fusion.target_ref, s32[1024,1]{1,0:T(8,128)} %broadcast_in_dim_reshape.4.route_ref, ...), custom_call_target="tpu_custom_call" | custom-call | tf_op jit(solution)/shard_map/collect/pallas_call | solution.py:898
  277.2 6.1 %fusion.12.mg_ref = f32[1024,1536]{1,0:T(8,128)} fusion(bf16[1024,768]{1,0:T(8,128)(2,1)} %get-tuple-element.88, bf16[1536,768]{1,0:T(8,128)(2,1)S(1)} %copy-done.11), kind=kOutput, calls=%fused_computation.46 | convolution fusion | flops 2415919104 | bytes 10223616 | tf_op jit(solution)/shard_map/dot_general | solution.py:1492
  283.3 3.9 convolution_convert_fusion.outg_ref
  287.2 6.9 %reduce-scatter.5.cloned.1.call-done = bf16[384,768]{1,0:T(8,128)(2,1)} async-done(((bf16[3072,768]{1,0:T(8,128)(2,1)}), bf16[384,768]{1,0:T(8,128)(2,1)}) %reduce-scatter.5.cloned.1.call-update) | async-done | bytes 589840 | tf_op jit(solution)/shard_map/reduce_scatter | solution.py:1484
  294.4 147.9 %backward_scan.1 = (bf16[1024,3072]{1,0:T(8,128)(2,1)}, bf16[1024,1536]{1,0:T(8,128)(2,1)}, f32[1024,1536]{1,0:T(8,128)}, bf16[80,1536]{1,0:T(8,128)(2,1)}, bf16...) custom-call(f32[1024,1536]{1,0:T(8,128)} %fusion.12.mg_ref, ...), custom_call_target="tpu_custom_call" | custom-call | tf_op jit(solution)/shard_map/backward_scan/pallas_call | solution.py:489
  444.0 13.5 %conv_back.1 = (bf16[1024,3072]{1,0:T(8,128)(2,1)}, f32[64,1536]{1,0:T(8,128)}, bf16[96,1536]{1,0:T(8,128)(2,1)}) custom-call(f32[1024,1536]{1,0:T(8,128)} %get-tuple-element.97.cg_ref, bf16[1024,1536]{1,0:T(8,128)(2,1)} %get-tuple-element.74.conv_ref.low_ref, bf16[1024,80]{1,0:T(8,128)(2,1)} %get-tuple-element.98.mpg_ref, ...), custom_call_target="tpu_custom_call", output_to_operand_aliasing={{0}: (8, {})} | custom-call | tf_op jit(solution)/shard_map/conv_back/pallas_call | solution.py:650
  458.5 1.5 collective-permute-start
  460.0 1.8 pad_maximum_fusion.small_ref
  461.8 5.2 collective-permute-done
  467.1 1.6 fusion.proj_ref
  468.7 98.1 %finish.1 = (f32[768,768]{1,0:T(8,128)}, f32[384,768]{1,0:T(8,128)}, f32[192,384]{1,0:T(8,128)}, f32[8,128,768]{2,1,0:T(8,128)}, bf16[8,128,768]{2,1,0:T(8,128)(2,1)}) custom-call(bf16[1024,3072]{1,0:T(8,128)(2,1)} %fusion.proj_ref, bf16[1056,768]{1,0:T(8,128)(2,1)} %get-tuple-element.103.normed_ref, bf16[768,3072]{1,0:T(8,128)(2,1)} %copy-done, ...), custom_call_target="tpu_custom_call" | custom-call | tf_op jit(solution)/shard_map/finish/pallas_call | solution.py:1201
  566.8 1.3 slice.119
  568.1 1.5 slice.122
  569.6 1.4 slice_reduce_fusion
  571.0 1.3 fusion.11
  572.3 1.3 slice_bitcast_fusion.3
  573.6 1.3 slice_bitcast_fusion.2
  574.9 1.6 slice_bitcast_fusion.1
  576.5 6.8 %bitcast_convert_fusion = f32[1,3072,768]{2,1,0:T(8,128)} fusion(bf16[3072,768]{1,0:T(8,128)(2,1)} %all-gather.8.cloned.1.call-done), kind=kLoop, calls=%fused_computation | loop fusion | flops 2359296 | bytes 14155776 | tf_op jit(solution)/shard_map/broadcast_in_dim | solution.py:1545
  583.3 7.5 %bitcast_convert_fusion.1 = f32[1,768,3072]{2,1,0:T(8,128)} fusion(bf16[768,3072]{1,0:T(8,128)(2,1)} %all-gather.6.cloned.1.call-done), kind=kLoop, calls=%fused_computation.1 | loop fusion | flops 2359296 | bytes 14155776 | tf_op jit(solution)/shard_map/broadcast_in_dim | solution.py:1544
  592.0 1.3 copy-done.9
  593.3 1.7 copy.83
  596.1 1.4 copy.84
  (95 shorter events, 28.6 us)
Async XLA Ops:
  7.2 138.7 %all-gather.4.cloned.1.call-start = ((), (), s32[]{:S(2)}) async-start(), calls=%async_computation.2 | async-start | bytes 2949120 | tf_op jit(solution)/shard_map/all_gather | solution.py:1434
  15.6 1.4 copy-start.3
  17.0 1.4 copy-start.4
  18.4 1.3 copy-start.5
  19.6 35.5 %copy-start.15 = (s32[8,128]{1,0:T(8,128)S(1)}, s32[8,128]{1,0:T(8,128)}, u32[]{:S(2)}) copy-start(s32[8,128]{1,0:T(8,128)} %param.21) | copy-start | bytes 12292
  19.6 35.5 %copy-start.16 = (s32[8,128]{1,0:T(8,128)S(1)}, s32[8,128]{1,0:T(8,128)}, u32[]{:S(2)}) copy-start(s32[8,128]{1,0:T(8,128)} %param.22) | copy-start | bytes 12292
  48.9 2.2 copy-start
  51.1 1.1 copy-start.1
  52.3 1.1 copy-start.2
  53.4 0.6 copy-start.6
  54.1 240.1 %reduce-scatter.5.cloned.1.call-start = ((), (), s32[]{:S(2)}) async-start(), calls=%async_computation.4 | async-start | bytes 5308416 | tf_op jit(solution)/shard_map/reduce_scatter | solution.py:1484
  232.3 2.4 copy-start.7
  232.3 210.0 %reduce-scatter.3.cloned.1.call-start = ((), (), s32[]{:S(2)}) async-start(), calls=%async_computation.3 | async-start | bytes 5308416 | tf_op jit(solution)/shard_map/reduce_scatter | solution.py:1484
  233.0 343.5 %all-gather.8.cloned.1.call-start = ((), (), s32[]{:S(2)}) async-start(), calls=%async_computation.6 | async-start | bytes 5308416 | tf_op jit(solution)/shard_map/all_gather | solution.py:1487
  235.6 41.6 %copy-start.11 = (bf16[1536,768]{1,0:T(8,128)(2,1)S(1)}, bf16[1536,768]{1,0:T(8,128)(2,1)}, u32[]{:S(2)}) copy-start(bf16[1536,768]{1,0:T(8,128)(2,1)} %all-gather.4.cloned.1.call-done.wout_ref) | copy-start | bytes 7077892
  277.1 6.1 %copy-start.8 = (bf16[1024,1536]{1,0:T(8,128)(2,1)S(1)}, bf16[1024,1536]{1,0:T(8,128)(2,1)}, u32[]{:S(2)}) copy-start(bf16[1024,1536]{1,0:T(8,128)(2,1)} %get-tuple-element.78.mixed_ref) | copy-start | bytes 9437188
  277.2 6.1 %copy-start.17 = (bf16[1024,768]{1,0:T(8,128)(2,1)S(1)}, bf16[1024,768]{1,0:T(8,128)(2,1)}, u32[]{:S(2)}) copy-start(bf16[1024,768]{1,0:T(8,128)(2,1)} %get-tuple-element.88) | copy-start | bytes 4718596
  294.2 289.2 %all-gather.6.cloned.1.call-start = ((), (), s32[]{:S(2)}) async-start(), calls=%async_computation.5 | async-start | bytes 5308416 | tf_op jit(solution)/shard_map/all_gather | solution.py:1487
  444.0 16.0 %copy-start.14 = (bf16[80,1536]{1,0:T(8,128)(2,1)S(1)}, bf16[80,1536]{1,0:T(8,128)(2,1)}, u32[]{:S(2)}) copy-start(bf16[80,1536]{1,0:T(8,128)(2,1)} %get-tuple-element.105) | copy-start | bytes 737284
  458.5 8.6 %collective-permute-start = (bf16[32,1536]{1,0:T(8,128)(2,1)S(1)}, bf16[32,1536]{1,0:T(8,128)(2,1)S(1)}, u32[]{:S(2)}, u32[]{:S(2)}) collective-permute-start(bf16[32,1536]{1,0:T(8,128)(2,1)S(1)} %slice.185), channel_id=1, source_target_pairs={{4,0},{8,4},{12,8},{16,12},{20,16},{24,20},{28,24},{5,1},{9,5},{13... | collective-permute-start | bytes 294920 | tf_op jit(solution)/shard_map/ppermute | solution.py:1384
  583.3 7.5 %copy-start.12 = (bf16[8,128,768]{2,1,0:T(8,128)(2,1)S(1)}, bf16[8,128,768]{2,1,0:T(8,128)(2,1)}, u32[]{:S(2)}) copy-start(bf16[8,128,768]{2,1,0:T(8,128)(2,1)} %get-tuple-element.147) | copy-start | bytes 4718596
  590.8 2.5 copy-start.9
  593.3 2.8 copy-start.10
  596.1 2.1 copy-start.13
Sparse Core Ops, SparseCore 0:
  54.2 23.5 all-gather.3
  232.4 61.6 reduce-scatter.4
  296.5 59.6 reduce-scatter.2
  357.5 56.6 all-gather.7
  442.5 61.4 all-gather.5

commit v4 on v3

--- a/solution.py
+++ b/solution.py
@@ -664,8 +664,17 @@
         name="conv_back",
     )(cg, conv_low, mpg, w_x, ci, conv_w, conv_b, match, proj)
 
+def routing(low, router, experts):
+    logits = jnp.dot(low, router, preferred_element_type=f32)
+    lane = lax.broadcasted_iota(jnp.int32, logits.shape, 1)
+    logits = jnp.where(lane < experts, logits, -1e30)
+    raised = jnp.exp(logits - jnp.max(logits, -1, keepdims=True))
+    return raised / jnp.sum(raised, -1, keepdims=True)
+
+
 def expert_kernel(
-    rows_ref, cot_ref, up_ref, down_ref, out_ref, back_ref, upg_ref, downg_ref, grad, out_acc, back_acc, active, pre_grad, *, tile
+    rows_ref, cot_ref, up_ref, down_ref, router_ref, turned_ref, chosen_ref, out_ref, back_ref, upg_ref, downg_ref, routerg_ref,
+    grad, out_acc, back_acc, active, pre_grad, prob, *, tile, experts,
 ):
     first = pl.program_id(0) == 0
     final = pl.program_id(0) == pl.num_programs(0) - 1
@@ -675,14 +684,15 @@
     @pl.when(first)
     def _():
         for at in tiles:
-            parts = rows_ref[at, width : width + LANES].astype(f32)
-            gate = parts[:, 0:1] + parts[:, 1:2] + parts[:, 2:3]
+            own = routing(rows_ref[at, :], router_ref[...], experts)
+            prob[at, :] = own
+            gate = jnp.sum(own * chosen_ref[...], -1, keepdims=True)
             grad[at, :] = (gate * cot_ref[at, :].astype(f32)).astype(bf16)
             out_acc[at, :] = jnp.zeros((tile, width), f32)
             back_acc[at, :] = jnp.zeros((tile, width), f32)
 
     for at in tiles:
-        pre = jnp.dot(rows_ref[at, :width], up_ref[...], preferred_element_type=f32)
+        pre = jnp.dot(rows_ref[at, :], up_ref[...], preferred_element_type=f32)
         act_grad = lax.dot_general(grad[at, :], down_ref[...], (((1,), (1,)), ((), ())), preferred_element_type=f32)
         half = 0.5 * lax.erf(pre * 0.7071067811865476) + 0.5
         active[at, :] = (pre * half).astype(bf16)
@@ -697,51 +707,52 @@
         active[...], grad[...], (((0,), (0,)), ((), ())), preferred_element_type=f32
     ).astype(bf16)
     upg_ref[...] = lax.dot_general(
-        rows_ref[:, :width], pre_grad[...], (((0,), (0,)), ((), ())), preferred_element_type=f32
+        rows_ref[...], pre_grad[...], (((0,), (0,)), ((), ())), preferred_element_type=f32
     ).astype(bf16)
 
     @pl.when(final)
     def _():
+        routerg_ref[...] = jnp.zeros_like(routerg_ref)
         for at in tiles:
             out = out_acc[at, :].astype(bf16)
             out_ref[at, :] = out
-            back_ref[at, :width] = back_acc[at, :].astype(bf16)
-            dot = jnp.sum(out.astype(f32) * cot_ref[at, :].astype(f32), -1, keepdims=True)
-            back_ref[at, width:] = in_parts(dot)
-
-
-def in_parts(column):
-    high = column.astype(bf16).astype(f32)
-    mid = (column - high).astype(bf16).astype(f32)
-    lane = lax.broadcasted_iota(jnp.int32, (column.shape[0], LANES), 1)
-    low = column - high - mid
-    return jnp.where(lane == 0, high, jnp.where(lane == 1, mid, jnp.where(lane == 2, low, 0.0))).astype(bf16)
-
-
-def one_expert(rows, cot, up, down):
+            gate_grad = jnp.sum(out.astype(f32) * cot_ref[at, :].astype(f32), -1, keepdims=True)
+            own = prob[at, :]
+            gate = jnp.sum(own * chosen_ref[...], -1, keepdims=True)
+            logit_grad = own * (chosen_ref[...] - gate) * gate_grad
+            routerg_ref[...] += lax.dot_general(
+                logit_grad, rows_ref[at, :].astype(f32), (((0,), (0,)), ((), ())), precision=highest,
+                preferred_element_type=f32,
+            )
+            through = jnp.dot(logit_grad, turned_ref[...], precision=highest, preferred_element_type=f32)
+            back_ref[at, :] = (back_acc[at, :] + through).astype(bf16)
+
+
+def one_expert(rows, cot, up, down, router_wide, chosen, experts):
     slots, width = cot.shape
     hidden = up.shape[1]
     hidden_tile, tile = hidden // 6, slots // 2
     full = whole_block((slots, width))
-    broad = whole_block((slots, width + LANES))
     cols = pl.BlockSpec((width, hidden_tile), lambda j: (0, j))
     deep = pl.BlockSpec((hidden_tile, width), lambda j: (j, 0))
     return pl.pallas_call(
-        functools.partial(expert_kernel, tile=tile),
+        functools.partial(expert_kernel, tile=tile, experts=experts),
         grid=(hidden // hidden_tile,),
-        in_specs=[broad, full, cols, deep],
-        out_specs=[full, broad, cols, deep],
+        in_specs=[
+            full, full, cols, deep, whole_block(router_wide.shape), whole_block((LANES, width)), whole_block((1, LANES)),
+        ],
+        out_specs=[full, full, cols, deep, whole_block((LANES, width))],
         out_shape=[
-            shape_of((slots, width), bf16), shape_of((slots, width + LANES), bf16), shape_of((width, hidden), bf16),
-            shape_of((hidden, width), bf16),
+            shape_of((slots, width), bf16), shape_of((slots, width), bf16), shape_of((width, hidden), bf16),
+            shape_of((hidden, width), bf16), shape_of((LANES, width), f32),
         ],
         scratch_shapes=[
             pltpu.VMEM((slots, width), bf16), pltpu.VMEM((slots, width), f32), pltpu.VMEM((slots, width), f32),
-            pltpu.VMEM((slots, hidden_tile), bf16), pltpu.VMEM((slots, hidden_tile), bf16),
+            pltpu.VMEM((slots, hidden_tile), bf16), pltpu.VMEM((slots, hidden_tile), bf16), pltpu.VMEM((slots, LANES), f32),
         ],
         compiler_params=params(),
         name="one_expert",
-    )(rows, cot, up, down)
+    )(rows, cot, up, down, router_wide, router_wide.astype(f32).T, chosen)
 
 
 def exp_barrier(spot, devices):
@@ -783,7 +794,7 @@
 
 
 def route_kernel(
-    mixed_ref, wout_ref, token_ref, gain_ref, router_ref, route_ref, target_ref, hidden_ref, rows_ref, prob_ref, got_ref,
+    mixed_ref, wout_ref, token_ref, gain_ref, router_ref, route_ref, target_ref, hidden_ref, gate_ref, got_ref, rows_ref,
     staged, send_sem, recv_sem, *, devices, experts, tile,
 ):
     exp_barrier(lax.axis_index("exp"), devices)
@@ -796,15 +807,11 @@
         hidden_ref[at, :] = hidden
         scale = lax.rsqrt(jnp.mean(hidden * hidden, -1, keepdims=True) + epsilon)
         low = (hidden * scale * gain_ref[...]).astype(bf16)
-        rows_ref[at, :width] = low
-        logits = jnp.dot(low, router_ref[...], preferred_element_type=f32)
-        lane = lax.broadcasted_iota(jnp.int32, logits.shape, 1)
-        logits = jnp.where(lane < experts, logits, -1e30)
-        raised = jnp.exp(logits - jnp.max(logits, -1, keepdims=True))
-        prob = raised / jnp.sum(raised, -1, keepdims=True)
-        prob_ref[at, :] = prob
+        rows_ref[at, :] = low
+        prob = routing(low, router_ref[...], experts)
+        lane = lax.broadcasted_iota(jnp.int32, prob.shape, 1)
         gate = jnp.sum(jnp.where(lane == route_ref[at, :], prob, 0.0), -1, keepdims=True)
-        rows_ref[at, width:] = in_parts(gate)
+        gate_ref[at, :] = jnp.broadcast_to(gate, (tile, LANES))
 
     moved = Dispatch(rows_ref, target_ref, got_ref, staged, send_sem, recv_sem, devices)
     moved.start()
@@ -818,20 +825,22 @@
     return pl.pallas_call(
         functools.partial(route_kernel, devices=devices, experts=experts, tile=256),
         in_specs=[vm] * 7,
-        out_specs=[vm] * 4,
+        out_specs=[vm] * 3,
         out_shape=[
-            shape_of((rows, width), f32), shape_of((rows, width + LANES), bf16), shape_of((rows, LANES), f32),
-            shape_of((devices, capacity, width + LANES), bf16),
-        ],
-        scratch_shapes=[pltpu.VMEM((devices - 1, capacity, width + LANES), bf16), dma((devices - 1,)), dma((devices - 1,))],
+            shape_of((rows, width), f32), shape_of((rows, LANES), f32), shape_of((devices, capacity, width), bf16),
+        ],
+        scratch_shapes=[
+            pltpu.VMEM((rows, width), bf16), pltpu.VMEM((devices - 1, capacity, width), bf16), dma((devices - 1,)),
+            dma((devices - 1,)),
+        ],
         compiler_params=pltpu.CompilerParams(collective_id=3, has_side_effects=True, vmem_limit_bytes=vmem_cap),
         name="routed",
     )(mixed_low, w_out, token_low, gain, router_wide, route_col, target[None, :])
 
 
 def collect_kernel(
-    sent_ref, target_ref, route_ref, rows_ref, prob_ref, hidden_ref, cot_ref, gain_ref, router_ref,
-    hidden_grad_ref, branch_ref, gain_grad_ref, router_grad_ref, got, total, send_sem, recv_sem, *, devices, hops, tile,
+    sent_ref, target_ref, hidden_ref, cot_ref, gain_ref, hidden_grad_ref, branch_ref, gain_grad_ref, got, total, send_sem,
+    recv_sem, *, devices, hops, tile,
 ):
     spot = lax.axis_index("exp")
     capacity = got.shape[1]
@@ -857,24 +866,11 @@
         c.wait_recv()
         total[...] += spread_back(lax.rem(spot + devices - hop, devices), got[devices - hop - 1])
     gain_grad_ref[...] = jnp.zeros_like(gain_grad_ref)
-    router_grad_ref[...] = jnp.zeros_like(router_grad_ref)
 
     @pl.loop(0, count // tile)
     def _(i):
         at = pl.ds(pl.multiple_of(i * tile, tile), tile)
-        parts = total[at, width:]
-        gate_grad = parts[:, 0:1] + parts[:, 1:2] + parts[:, 2:3]
-        prob = prob_ref[at, :]
-        chosen = jnp.where(lax.broadcasted_iota(jnp.int32, prob.shape, 1) == route_ref[at, :], 1.0, 0.0)
-        gate = jnp.sum(prob * chosen, -1, keepdims=True)
-        logit_grad = prob * (chosen - gate) * gate_grad
-        router_grad_ref[...] += lax.dot_general(
-            logit_grad, rows_ref[at, :width].astype(f32), (((0,), (0,)), ((), ())), precision=highest,
-            preferred_element_type=f32,
-        )
-        grad = total[at, :width] + jnp.dot(
-            logit_grad, router_ref[...], precision=highest, preferred_element_type=f32
-        )
+        grad = total[at, :]
         hidden = hidden_ref[at, :]
         scale = lax.rsqrt(jnp.mean(hidden * hidden, -1, keepdims=True) + epsilon)
         unit = hidden * scale
@@ -890,26 +886,23 @@
         c.wait_send()
 
 
-def collect(blocks, target, route_col, rows, prob, hidden, cot, gain, router_t, devices):
+def collect(blocks, target, hidden, cot, gain, devices):
     vm = pl.BlockSpec(memory_space=pltpu.VMEM)
     dma = pltpu.SemaphoreType.DMA
-    capacity, wide = blocks.shape[1:]
+    capacity = blocks.shape[1]
     count, width = hidden.shape
     return pl.pallas_call(
         functools.partial(collect_kernel, devices=devices, hops=(2, 3, 1), tile=256),
-        in_specs=[vm] * 9,
-        out_specs=[vm] * 4,
-        out_shape=[
-            shape_of((count, width), f32), shape_of((count, width), bf16), shape_of((1, width), f32),
-            shape_of((LANES, width), f32),
-        ],
+        in_specs=[vm] * 5,
+        out_specs=[vm] * 3,
+        out_shape=[shape_of((count, width), f32), shape_of((count, width), bf16), shape_of((1, width), f32)],
         scratch_shapes=[
-            pltpu.VMEM((devices - 1, capacity, wide), bf16), pltpu.VMEM((count, wide), f32), dma((devices - 1,)),
+            pltpu.VMEM((devices - 1, capacity, width), bf16), pltpu.VMEM((count, width), f32), dma((devices - 1,)),
             dma((devices - 1,)),
         ],
         compiler_params=pltpu.CompilerParams(collective_id=4, has_side_effects=True, vmem_limit_bytes=vmem_cap),
         name="collect",
-    )(blocks, target[:, None], route_col, rows, prob, hidden, cot, gain, router_t)
+    )(blocks, target[:, None], hidden, cot, gain)
 
 SEGMENTS = 4
 STARTS = (-4, 0, 1, 2)
@@ -1000,7 +993,7 @@
 
 
 def finish_kernel(
-    proj_ref, normed_ref, win_ref, outo_ref, small_ref, gain_ref, token_ref, hiddeng_ref, hidden_ref, rows_ref, target_ref,
+    proj_ref, normed_ref, win_ref, outo_ref, small_ref, gain_ref, token_ref, hiddeng_ref, hidden_ref, chance_ref, target_ref,
     tok_ref,
     in_sum_ref, out_sum_ref, small_sum_ref, tokens_grad_ref, block_ref,
     own, total, near_stage, small_all, gain_part, near_in, near_small, far_in, far_small, pass_in, pass_small, sent, landed, near_send, near_recv, far_send, far_recv, ring_send, ring_recv,
@@ -1139,8 +1132,7 @@
     def block_tile(i):
         at = pl.ds(pl.multiple_of(i * tile, tile), tile)
         capacity = tok_ref.shape[1]
-        parts = rows_ref[at, width:].astype(f32)
-        gate = parts[:, 0:1] + parts[:, 1:2] + parts[:, 2:3]
+        gate = chance_ref[at, 0:1]
         tok = jnp.zeros((tile, width), f32)
         for k in range(tok_ref.shape[0]):
             slot = lax.broadcasted_iota(jnp.int32, (tile, capacity), 1) + k * capacity
@@ -1185,7 +1177,7 @@
     rings.drain()
 
 
-def finish(proj, normed_ext, w_in, out_own, small, gain, token_low, hidden_grad, hidden_one, moe_rows, target, tok, gain_row, group):
+def finish(proj, normed_ext, w_in, out_own, small, gain, token_low, hidden_grad, hidden_one, chance, target, tok, gain_row, group):
     peers, devices = lax.axis_size("seq"), lax.axis_size("exp")
     count, width = token_low.shape
     wide, rows_out = proj.shape[1] // devices, out_own.shape[0]
@@ -1221,7 +1213,7 @@
         compiler_params=pltpu.CompilerParams(collective_id=2, has_side_effects=True, vmem_limit_bytes=64 << 20),
         name="finish",
     )(
-        proj, normed_ext, w_in, out_own, small, gain, token_low, hidden_grad, hidden_one, moe_rows, target[:, None], tok
+        proj, normed_ext, w_in, out_own, small, gain, token_low, hidden_grad, hidden_one, chance, target[:, None], tok
     )
 
 PIECES = 2
@@ -1466,16 +1458,16 @@
     )
     route_col = route_rows[:, None]
     router_wide = jnp.pad(w_router, ((0, 0), (0, LANES - expert_total)))
-    hidden_one, moe_rows, prob, received = routed(
+    hidden_one, chance, received = routed(
         mixed_low, w_out, token_low, gain_two, router_wide, route_col, target, capacity, devices, expert_total
     )
-    expert_out, rows_back, up_grad, down_grad = one_expert(
-        received.reshape(devices * capacity, width + LANES), cot_recv.reshape(devices * capacity, width),
-        expert_up[0], expert_down[0],
-    )
-    hidden_grad, branch_grad, gain_two_grad, router_grad_t = collect(
-        rows_back.reshape(devices, capacity, width + LANES), target, route_col, moe_rows, prob, hidden_one, cot_rows,
-        gain_two, router_wide.astype(f32).T, devices,
+    chosen = (jnp.arange(LANES) == lax.axis_index("exp")).astype(f32)[None]
+    expert_out, rows_back, up_grad, down_grad, router_grad_t = one_expert(
+        received.reshape(devices * capacity, width), cot_recv.reshape(devices * capacity, width), expert_up[0],
+        expert_down[0], router_wide, chosen, expert_total,
+    )
+    hidden_grad, branch_grad, gain_two_grad = collect(
+        rows_back.reshape(devices, capacity, width), target, hidden_one, cot_rows, gain_two, devices
     )
     peers = lax.axis_size("seq")
     order = [list(range(0, peers, 2)) + list(range(peers - 1, 0, -2))]
@@ -1512,7 +1504,7 @@
     packed = jnp.concatenate([small_one, small_two, narrow.reshape(-1, inner_width)], 0)
     gain_row = small_one.shape[0] + small_two.shape[0]
     in_sum, out_sum, sums, tokens_grad, block_out = finish(
-        proj, normed_ext, w_in, out_own, packed, gain_one, token_low, hidden_grad, hidden_one, moe_rows,
+        proj, normed_ext, w_in, out_own, packed, gain_one, token_low, hidden_grad, hidden_one, chance,
         target, tok, gain_row, group,
     )
     at, own = 0, []

time: 616 us -> 615 us (level)
  Pallas kernels: 499 us -> 488 us
  waiting for transfers between devices: 13 us -> 23.7 us
    reduce_scatter x2, waiting for transfers between devices: 6.95 us -> 17.8 us  [scattered(): lax.psum_scatter(values, 'seq', scatter_dimension=0, axis_index_groups=or...]
    pallas_call x1, Pallas kernels: 41.6 us -> 32 us  [collect(): pl.pallas_call(functools.partial(collect_kernel, devices=devices, hops=(2...]
  transfers between devices with their start and end apart: 6 -> 6, of which waited for: 2 -> 2; matrix products, arithmetic and copies ran while one was open for 7% -> 7% of each run, Pallas kernels for 63% -> 61%
where the time goes in v4:
time: 615 us; the launch traced here: 606 us
  Pallas kernels  488 us (79%)
  local copies, waits for them, and re-layouts  43.7 us (7%)
  other arithmetic  24 us (4%)
  waiting for transfers between devices  23.7 us (4%)
  between operations  14.6 us (2%)
  matrix products  10.1 us (2%)
    pallas_call x1, Pallas kernels, backward_scan(): pl.pallas_call(functools.partial(backward_kernel, states=states, group=gr...  145 us
    pallas_call x1, Pallas kernels, finish(): pl.pallas_call(functools.partial(finish_kernel, peers=peers, bases=bases,...  97.8 us
    pallas_call x1, Pallas kernels, forward_scan(): pl.pallas_call(functools.partial(forward_kernel, states=states, group=gro...  66.6 us
    pallas_call x1, Pallas kernels, one_expert(): pl.pallas_call(functools.partial(expert_kernel, tile=tile, experts=expert...  51.7 us
    pallas_call x1, Pallas kernels, routed(): pl.pallas_call(functools.partial(route_kernel, devices=devices, experts=e...  36 us
    pallas_call x1, Pallas kernels, collect(): pl.pallas_call(functools.partial(collect_kernel, devices=devices, hops=(2...  32 us
    pallas_call x1, Pallas kernels, gather_weights(): pl.pallas_call(functools.partial(gather_kernel, kernel_len=kernel_len), i...  29.3 us
    reduce_scatter x2, waiting for transfers between devices, scattered(): lax.psum_scatter(values, 'seq', scatter_dimension=0, axis_index_groups=or...  17.8 us
  transfers between devices with their start and end apart: 6, of which 2 were waited for; matrix products, arithmetic and copies ran while one was open for 7% of the time, Pallas kernels for 61%

profile of v4, /device:TPU:0, one launch (start us, length us, event | category | flops | bytes accessed | tf_op | source)
XLA Modules:
  0.0 605.5 jit_solution(13827576622738039400)
XLA Ops:
  12.1 3.4 concatenate.17
  15.6 1.4 copy-done.3
  17.0 1.4 copy-done.4
  19.7 29.3 %gather_weights.1 = (bf16[768,3072]{1,0:T(8,128)(2,1)S(1)}, bf16[160,1536]{1,0:T(8,128)(2,1)S(1)}, bf16[32,768]{1,0:T(8,128)(2,1)S(1)}, s32[8,128]{1,0:T(8,128)S...) custom-call(bf16[768,768]{1,0:T(8,128)(2,1)S(1)} %copy-done.5, bf16[160,384]{1,0:T(8,128)(2,1)S(1)} %pad.17.small_ref, ...), custom_call_target="tpu_custom_call" | custom-call | tf_op jit(solution)/shard_map/gather_weights/pallas_call | solution.py:1355
  48.9 2.2 copy-done
  62.8 15.7 %front.1 = (bf16[1056,1536]{1,0:T(8,128)(2,1)}, bf16[1024,1536]{1,0:T(8,128)(2,1)}, f32[1024,1536]{1,0:T(8,128)}, bf16[1024,48]{1,0:T(8,128)(2,1)}, bf16[1024,96]{1,0:T(8,128)(2,1)}, /*index=5*/bf16[1056,768]{1,0:T(8,128)(2,1)}) custom-call(bf16[1024,768]{1,0:T(8,128)(2,1)} %copy-done.1, bf16[32,768]{1,0:T(8,128)(2,1)} %copy-done.6, ...), custom_call_target="tpu_custom_call" | custom-call | tf_op jit(solution)/shard_map/front/pallas_call | solution.py:591
  79.2 66.6 %forward_scan.1 = (f32[1024,1536]{1,0:T(8,128)}, f32[1024,1536]{1,0:T(8,128)}, bf16[1024,1536]{1,0:T(8,128)(2,1)}, f32[12,16,8,128]{3,2,1,0:T(8,128)}, f32[12,8,...) custom-call(bf16[1024,48]{1,0:T(8,128)(2,1)} %get-tuple-element.72.rate_ref, bf16[48,1536]{1,0:T(8,128)(2,1)} %slice.108.wdt_ref, ...), custom_call_target="tpu_custom_call" | custom-call | tf_op jit(solution)/shard_map/forward_scan/pallas_call | solution.py:450
  147.2 36.0 %routed.1 = (f32[1024,768]{1,0:T(8,128)}, f32[1024,128]{1,0:T(8,128)}, bf16[4,320,768]{2,1,0:T(8,128)(2,1)}) custom-call(bf16[1024,1536]{1,0:T(8,128)(2,1)} %get-tuple-element.77.mixed_ref, bf16[1536,768]{1,0:T(8,128)(2,1)} %all-gather.4.cloned.1.call-done.wout_ref, bf16[1024,768]{1,0:T(8,128)(2,1)} %copy-done.1, f32[1,768]{1,0:T(1,128)} %reshape.194.gain_ref, ...), custom_call_target="tpu_custom_call" | custom-call | tf_op jit(solution)/shard_map/routed/pallas_call | solution.py:825
  183.2 51.7 %one_expert.1 = (bf16[1280,768]{1,0:T(8,128)(2,1)}, bf16[1280,768]{1,0:T(8,128)(2,1)}, bf16[768,3072]{1,0:T(8,128)(2,1)}, bf16[3072,768]{1,0:T(8,128)(2,1)}, f32[128,768]{1,0:T(8,128)}) custom-call(bf16[1280,768]{1,0:T(8,128)(2,1)} %bitcast.70, bf16[1280,768]{1,0:T(8,128)(2,1)} %bitcast.69, bf16[768,3072]{1,0:T(8,128)(2,1)} %bitcast.65, ...), custom_call_target="tpu_custom_call" | custom-call | tf_op jit(solution)/shard_map/one_expert/pallas_call | solution.py:738
  236.9 32.0 %collect.1 = (f32[1024,768]{1,0:T(8,128)}, bf16[1024,768]{1,0:T(8,128)(2,1)}, f32[1,768]{1,0:T(1,128)}) custom-call(bf16[4,320,768]{2,1,0:T(8,128)(2,1)} %bitcast.68, s32[1024,1]{1,0:T(8,128)} %add_select_fusion.target_ref, f32[1024,768]{1,0:T(8,128)} %get-tuple-element.84.hidden_ref, bf16[1024,768]{1,0:T(8,128)(2,1)} %copy-done.2, f32[1,768]{1,0:T(1,128)} %reshape.194.gain_ref), custom_call_target="tpu_custom_call" | custom-call | tf_op jit(solution)/shard_map/collect/pallas_call | solution.py:894
  268.9 6.1 %fusion.12.mg_ref = f32[1024,1536]{1,0:T(8,128)} fusion(bf16[1024,768]{1,0:T(8,128)(2,1)} %get-tuple-element.85, bf16[1536,768]{1,0:T(8,128)(2,1)S(1)} %copy-done.11), kind=kOutput, calls=%fused_computation.47 | convolution fusion | flops 2415919104 | bytes 10223616 | tf_op jit(solution)/shard_map/dot_general | solution.py:1484
  275.0 3.9 convolution_convert_fusion.outg_ref
  279.0 17.8 %reduce-scatter.5.cloned.1.call-done = bf16[384,768]{1,0:T(8,128)(2,1)} async-done(((bf16[3072,768]{1,0:T(8,128)(2,1)}), bf16[384,768]{1,0:T(8,128)(2,1)}) %reduce-scatter.5.cloned.1.call-update) | async-done | bytes 589840 | tf_op jit(solution)/shard_map/reduce_scatter | solution.py:1476
  296.8 145.1 %backward_scan.1 = (bf16[1024,3072]{1,0:T(8,128)(2,1)}, bf16[1024,1536]{1,0:T(8,128)(2,1)}, f32[1024,1536]{1,0:T(8,128)}, bf16[80,1536]{1,0:T(8,128)(2,1)}, bf16...) custom-call(f32[1024,1536]{1,0:T(8,128)} %fusion.12.mg_ref, ...), custom_call_target="tpu_custom_call" | custom-call | tf_op jit(solution)/shard_map/backward_scan/pallas_call | solution.py:489
  443.7 13.4 %conv_back.1 = (bf16[1024,3072]{1,0:T(8,128)(2,1)}, f32[64,1536]{1,0:T(8,128)}, bf16[96,1536]{1,0:T(8,128)(2,1)}) custom-call(f32[1024,1536]{1,0:T(8,128)} %get-tuple-element.94.cg_ref, bf16[1024,1536]{1,0:T(8,128)(2,1)} %get-tuple-element.73.conv_ref.low_ref, bf16[1024,80]{1,0:T(8,128)(2,1)} %get-tuple-element.95.mpg_ref, ...), custom_call_target="tpu_custom_call", output_to_operand_aliasing={{0}: (8, {})} | custom-call | tf_op jit(solution)/shard_map/conv_back/pallas_call | solution.py:650
  458.1 1.5 collective-permute-start
  459.6 1.8 pad_maximum_fusion.small_ref
  461.5 5.2 collective-permute-done
  466.7 1.6 fusion.proj_ref
  468.3 97.8 %finish.1 = (f32[768,768]{1,0:T(8,128)}, f32[384,768]{1,0:T(8,128)}, f32[192,384]{1,0:T(8,128)}, f32[8,128,768]{2,1,0:T(8,128)}, bf16[8,128,768]{2,1,0:T(8,128)(2,1)}) custom-call(bf16[1024,3072]{1,0:T(8,128)(2,1)} %fusion.proj_ref, bf16[1056,768]{1,0:T(8,128)(2,1)} %get-tuple-element.100.normed_ref, bf16[768,3072]{1,0:T(8,128)(2,1)} %copy-done, ...), custom_call_target="tpu_custom_call" | custom-call | tf_op jit(solution)/shard_map/finish/pallas_call | solution.py:1193
  566.1 1.3 slice.119
  567.4 1.5 slice.122
  568.9 1.4 slice_reduce_fusion
  570.3 1.3 fusion.11
  571.6 1.3 slice_bitcast_fusion.3
  572.9 1.3 slice_bitcast_fusion.2
  574.3 1.6 slice_bitcast_fusion.1
  575.8 6.8 %bitcast_convert_fusion = f32[1,3072,768]{2,1,0:T(8,128)} fusion(bf16[3072,768]{1,0:T(8,128)(2,1)} %all-gather.8.cloned.1.call-done), kind=kLoop, calls=%fused_computation | loop fusion | flops 2359296 | bytes 14155776 | tf_op jit(solution)/shard_map/broadcast_in_dim | solution.py:1537
  582.7 7.5 %bitcast_convert_fusion.1 = f32[1,768,3072]{2,1,0:T(8,128)} fusion(bf16[768,3072]{1,0:T(8,128)(2,1)} %all-gather.6.cloned.1.call-done), kind=kLoop, calls=%fused_computation.1 | loop fusion | flops 2359296 | bytes 14155776 | tf_op jit(solution)/shard_map/broadcast_in_dim | solution.py:1536
  591.3 1.3 copy-done.9
  592.6 1.7 copy.84
  595.4 1.4 copy.85
  (96 shorter events, 28.4 us)
Async XLA Ops:
  7.2 140.0 %all-gather.4.cloned.1.call-start = ((), (), s32[]{:S(2)}) async-start(), calls=%async_computation.2 | async-start | bytes 2949120 | tf_op jit(solution)/shard_map/all_gather | solution.py:1426
  15.6 1.4 copy-start.3
  17.0 1.4 copy-start.4
  18.4 1.3 copy-start.5
  19.6 35.5 %copy-start.15 = (s32[8,128]{1,0:T(8,128)S(1)}, s32[8,128]{1,0:T(8,128)}, u32[]{:S(2)}) copy-start(s32[8,128]{1,0:T(8,128)} %param.21) | copy-start | bytes 12292
  19.6 35.5 %copy-start.16 = (s32[8,128]{1,0:T(8,128)S(1)}, s32[8,128]{1,0:T(8,128)}, u32[]{:S(2)}) copy-start(s32[8,128]{1,0:T(8,128)} %param.22) | copy-start | bytes 12292
  48.9 2.2 copy-start
  51.1 1.1 copy-start.1
  52.3 1.1 copy-start.2
  53.4 0.6 copy-start.6
  54.1 242.7 %reduce-scatter.5.cloned.1.call-start = ((), (), s32[]{:S(2)}) async-start(), calls=%async_computation.4 | async-start | bytes 5308416 | tf_op jit(solution)/shard_map/reduce_scatter | solution.py:1476
  234.9 1.1 copy-start.7
  234.9 207.1 %reduce-scatter.3.cloned.1.call-start = ((), (), s32[]{:S(2)}) async-start(), calls=%async_computation.3 | async-start | bytes 5308416 | tf_op jit(solution)/shard_map/reduce_scatter | solution.py:1476
  235.7 340.2 %all-gather.8.cloned.1.call-start = ((), (), s32[]{:S(2)}) async-start(), calls=%async_computation.6 | async-start | bytes 5308416 | tf_op jit(solution)/shard_map/all_gather | solution.py:1479
  236.9 32.0 %copy-start.11 = (bf16[1536,768]{1,0:T(8,128)(2,1)S(1)}, bf16[1536,768]{1,0:T(8,128)(2,1)}, u32[]{:S(2)}) copy-start(bf16[1536,768]{1,0:T(8,128)(2,1)} %all-gather.4.cloned.1.call-done.wout_ref) | copy-start | bytes 7077892
  268.9 6.1 %copy-start.8 = (bf16[1024,1536]{1,0:T(8,128)(2,1)S(1)}, bf16[1024,1536]{1,0:T(8,128)(2,1)}, u32[]{:S(2)}) copy-start(bf16[1024,1536]{1,0:T(8,128)(2,1)} %get-tuple-element.77.mixed_ref) | copy-start | bytes 9437188
  268.9 6.1 %copy-start.17 = (bf16[1024,768]{1,0:T(8,128)(2,1)S(1)}, bf16[1024,768]{1,0:T(8,128)(2,1)}, u32[]{:S(2)}) copy-start(bf16[1024,768]{1,0:T(8,128)(2,1)} %get-tuple-element.85) | copy-start | bytes 4718596
  296.8 285.9 %all-gather.6.cloned.1.call-start = ((), (), s32[]{:S(2)}) async-start(), calls=%async_computation.5 | async-start | bytes 5308416 | tf_op jit(solution)/shard_map/all_gather | solution.py:1479
  443.7 15.9 %copy-start.14 = (bf16[80,1536]{1,0:T(8,128)(2,1)S(1)}, bf16[80,1536]{1,0:T(8,128)(2,1)}, u32[]{:S(2)}) copy-start(bf16[80,1536]{1,0:T(8,128)(2,1)} %get-tuple-element.102) | copy-start | bytes 737284
  458.1 8.6 %collective-permute-start = (bf16[32,1536]{1,0:T(8,128)(2,1)S(1)}, bf16[32,1536]{1,0:T(8,128)(2,1)S(1)}, u32[]{:S(2)}, u32[]{:S(2)}) collective-permute-start(bf16[32,1536]{1,0:T(8,128)(2,1)S(1)} %slice.185), channel_id=1, source_target_pairs={{4,0},{8,4},{12,8},{16,12},{20,16},{24,20},{28,24},{5,1},{9,5},{13... | collective-permute-start | bytes 294920 | tf_op jit(solution)/shard_map/ppermute | solution.py:1376
  582.7 7.5 %copy-start.12 = (bf16[8,128,768]{2,1,0:T(8,128)(2,1)S(1)}, bf16[8,128,768]{2,1,0:T(8,128)(2,1)}, u32[]{:S(2)}) copy-start(bf16[8,128,768]{2,1,0:T(8,128)(2,1)} %get-tuple-element.145) | copy-start | bytes 4718596
  590.1 2.5 copy-start.9
  592.6 2.8 copy-start.10
  595.4 2.1 copy-start.13
Sparse Core Ops, SparseCore 0:
  54.2 23.4 all-gather.3
  235.0 61.6 reduce-scatter.4
  299.1 60.0 reduce-scatter.2
  360.5 55.9 all-gather.7
  442.2 62.3 all-gather.5

commit v5 on v4

--- a/solution.py
+++ b/solution.py
@@ -905,6 +905,7 @@
     )(blocks, target[:, None], hidden, cot, gain)
 
 SEGMENTS = 4
+WIDEN = 5
 STARTS = (-4, 0, 1, 2)
 
 
@@ -994,8 +995,9 @@
 
 def finish_kernel(
     proj_ref, normed_ref, win_ref, outo_ref, small_ref, gain_ref, token_ref, hiddeng_ref, hidden_ref, chance_ref, target_ref,
-    tok_ref,
-    in_sum_ref, out_sum_ref, small_sum_ref, tokens_grad_ref, block_ref,
+    tok_ref, narrow_ref,
+    in_sum_ref, out_sum_ref, small_sum_ref, tokens_grad_ref, block_ref, wide_ref,
+    narrow_buf, wide_buf, narrow_sem, wide_sem,
     own, total, near_stage, small_all, gain_part, near_in, near_small, far_in, far_small, pass_in, pass_small, sent, landed, near_send, near_recv, far_send, far_recv, ring_send, ring_recv,
     *, peers, bases, sizes, halo, tile, gain_row,
 ):
@@ -1141,6 +1143,31 @@
         place_rows(block_ref, hidden_ref[at, :] + gate * tok, i)
 
     tiles = count // tile
+    pieces, piece = narrow_ref.shape[0] // tile, tile
+
+    def load(i):
+        at = pl.ds(pl.multiple_of(i * piece, piece), piece)
+        return pltpu.make_async_copy(narrow_ref.at[at], narrow_buf.at[lax.rem(i, 2)], narrow_sem.at[lax.rem(i, 2)])
+
+    def store(i):
+        at = pl.ds(pl.multiple_of(i * piece, piece), piece)
+        return pltpu.make_async_copy(wide_buf.at[lax.rem(i, 2)], wide_ref.at[at], wide_sem.at[lax.rem(i, 2)])
+
+    load(0).start()
+
+    def widen(i):
+        @pl.when(i + 1 < pieces)
+        def _():
+            load(i + 1).start()
+
+        load(i).wait()
+
+        @pl.when(i >= 2)
+        def _():
+            store(i - 2).wait()
+
+        wide_buf[lax.rem(i, 2)] = narrow_buf[lax.rem(i, 2)].astype(f32)
+        store(i).start()
 
     @pl.loop(0, 2 * peers - 1 + STARTS[-1])
     def _(turn):
@@ -1154,6 +1181,12 @@
 
             rings.advance(ring, step)
 
+        late = turn - WIDEN
+
+        @pl.when(jnp.logical_and(late >= 0, late < pieces))
+        def _():
+            widen(late)
+
         @pl.when(turn < tiles)
         def _():
             token_tile(turn)
@@ -1162,6 +1195,8 @@
         def _():
             block_tile(turn - tiles)
 
+    for i in (pieces - 2, pieces - 1):
+        store(i).wait()
     for i in range(3):
         for h in range(folds):
             at = slice(bases[1 + i] + h * third, bases[1 + i] + (h + 1) * third)
@@ -1177,7 +1212,7 @@
     rings.drain()
 
 
-def finish(proj, normed_ext, w_in, out_own, small, gain, token_low, hidden_grad, hidden_one, chance, target, tok, gain_row, group):
+def finish(proj, normed_ext, w_in, out_own, small, gain, token_low, hidden_grad, hidden_one, chance, target, tok, narrow, gain_row, group):
     peers, devices = lax.axis_size("seq"), lax.axis_size("exp")
     count, width = token_low.shape
     wide, rows_out = proj.shape[1] // devices, out_own.shape[0]
@@ -1195,13 +1230,14 @@
             finish_kernel, peers=peers, bases=bases, sizes=sizes, halo=normed_ext.shape[0] - count, tile=256,
             gain_row=gain_row,
         ),
-        in_specs=[vm] * 12,
-        out_specs=[vm] * 5,
+        in_specs=[vm] * 12 + [pl.BlockSpec(memory_space=pl.ANY)],
+        out_specs=[vm] * 5 + [pl.BlockSpec(memory_space=pl.ANY)],
         out_shape=[
             shape_of((width, wide), f32), shape_of((rows_out, wide), f32), shape_of((rows_small, share), f32),
-            shape_of((group, count // group, width), f32), shape_of((group, count // group, width), bf16),
+            shape_of((group, count // group, width), f32), shape_of((group, count // group, width), bf16), shape_of(narrow.shape, f32),
         ],
         scratch_shapes=[
+            pltpu.VMEM((2, 256, narrow.shape[1]), bf16), pltpu.VMEM((2, 256, narrow.shape[1]), f32), dma((2,)), dma((2,)),
             pltpu.VMEM((length, share), f32), pltpu.VMEM((length, share), bf16), pltpu.VMEM((2, width, wide), bf16),
             pltpu.VMEM(small.shape, bf16), pltpu.VMEM((width, LANES), f32),
         ]
@@ -1213,7 +1249,8 @@
         compiler_params=pltpu.CompilerParams(collective_id=2, has_side_effects=True, vmem_limit_bytes=64 << 20),
         name="finish",
     )(
-        proj, normed_ext, w_in, out_own, small, gain, token_low, hidden_grad, hidden_one, chance, target[:, None], tok
+        proj, normed_ext, w_in, out_own, small, gain, token_low, hidden_grad, hidden_one, chance, target[:, None], tok,
+        narrow,
     )
 
 PIECES = 2
@@ -1503,9 +1540,9 @@
     narrow = jnp.pad(narrow, ((0, -narrow.shape[0] % 16), (0, 0), (0, share - own_width))).astype(bf16)
     packed = jnp.concatenate([small_one, small_two, narrow.reshape(-1, inner_width)], 0)
     gain_row = small_one.shape[0] + small_two.shape[0]
-    in_sum, out_sum, sums, tokens_grad, block_out = finish(
+    in_sum, out_sum, sums, tokens_grad, block_out, down_wide = finish(
         proj, normed_ext, w_in, out_own, packed, gain_one, token_low, hidden_grad, hidden_one, chance,
-        target, tok, gain_row, group,
+        target, tok, down_sum, gain_row, group,
     )
     at, own = 0, []
     for first, rows in (
@@ -1534,7 +1571,7 @@
         own_narrow[1],
         own_narrow[2:].T,
         up_sum.astype(f32)[None],
-        down_sum.astype(f32)[None],
+        down_wide[None],
     )
 
 

time: 615 us -> 618 us (level)
  Pallas kernels: 488 us -> 498 us
  other arithmetic: 24 us -> 17.3 us
    pallas_call x1, Pallas kernels: 51.7 us -> 60.4 us  [one_expert(): pl.pallas_call(functools.partial(expert_kernel, tile=tile, experts=expert...]
    broadcast_in_dim x1 -> x0, other arithmetic: 6.82 us -> none  [local(): down_sum.astype(f32)[None]]
    unnamed x42 -> x49, local copies, waits for them, and re-layouts: 17.8 us -> 21.5 us
  transfers between devices with their start and end apart: 6 -> 6, of which waited for: 2 -> 2; matrix products, arithmetic and copies ran while one was open for 7% -> 6% of each run, Pallas kernels for 61% -> 61%
where the time goes in v5:
time: 618 us; the launch traced here: 612 us
  Pallas kernels  498 us (81%)
  local copies, waits for them, and re-layouts  47.4 us (8%)
  waiting for transfers between devices  23.8 us (4%)
  other arithmetic  17.3 us (3%)
  between operations  14.3 us (2%)
  matrix products  10.1 us (2%)
    pallas_call x1, Pallas kernels, backward_scan(): pl.pallas_call(functools.partial(backward_kernel, states=states, group=gr...  145 us
    pallas_call x1, Pallas kernels, finish(): pl.pallas_call(functools.partial(finish_kernel, peers=peers, bases=bases,...  99 us
    pallas_call x1, Pallas kernels, forward_scan(): pl.pallas_call(functools.partial(forward_kernel, states=states, group=gro...  66.6 us
    pallas_call x1, Pallas kernels, one_expert(): pl.pallas_call(functools.partial(expert_kernel, tile=tile, experts=expert...  60.4 us
    pallas_call x1, Pallas kernels, routed(): pl.pallas_call(functools.partial(route_kernel, devices=devices, experts=e...  36 us
    pallas_call x1, Pallas kernels, collect(): pl.pallas_call(functools.partial(collect_kernel, devices=devices, hops=(2...  32 us
    pallas_call x1, Pallas kernels, gather_weights(): pl.pallas_call(functools.partial(gather_kernel, kernel_len=kernel_len), i...  29.3 us
    unnamed x49, local copies, waits for them, and re-layouts  21.5 us
  transfers between devices with their start and end apart: 6, of which 2 were waited for; matrix products, arithmetic and copies ran while one was open for 6% of the time, Pallas kernels for 61%

profile of v5, /device:TPU:0, one launch (start us, length us, event | category | flops | bytes accessed | tf_op | source)
XLA Modules:
  0.0 612.4 jit_solution(14897412131638929948)
XLA Ops:
  12.1 3.4 concatenate.17
  15.6 1.4 copy-done.3
  17.0 1.4 copy-done.4
  19.7 29.3 %gather_weights.1 = (bf16[768,3072]{1,0:T(8,128)(2,1)S(1)}, bf16[160,1536]{1,0:T(8,128)(2,1)S(1)}, bf16[32,768]{1,0:T(8,128)(2,1)S(1)}, s32[8,128]{1,0:T(8,128)S...) custom-call(bf16[768,768]{1,0:T(8,128)(2,1)S(1)} %copy-done.5, bf16[160,384]{1,0:T(8,128)(2,1)S(1)} %pad.17.small_ref, ...), custom_call_target="tpu_custom_call" | custom-call | tf_op jit(solution)/shard_map/gather_weights/pallas_call | solution.py:1392
  48.9 2.2 copy-done
  62.9 15.7 %front.1 = (bf16[1056,1536]{1,0:T(8,128)(2,1)}, bf16[1024,1536]{1,0:T(8,128)(2,1)}, f32[1024,1536]{1,0:T(8,128)}, bf16[1024,48]{1,0:T(8,128)(2,1)}, bf16[1024,96]{1,0:T(8,128)(2,1)}, /*index=5*/bf16[1056,768]{1,0:T(8,128)(2,1)}) custom-call(bf16[1024,768]{1,0:T(8,128)(2,1)} %copy-done.1, bf16[32,768]{1,0:T(8,128)(2,1)} %copy-done.6, ...), custom_call_target="tpu_custom_call" | custom-call | tf_op jit(solution)/shard_map/front/pallas_call | solution.py:591
  79.3 66.6 %forward_scan.1 = (f32[1024,1536]{1,0:T(8,128)}, f32[1024,1536]{1,0:T(8,128)}, bf16[1024,1536]{1,0:T(8,128)(2,1)}, f32[12,16,8,128]{3,2,1,0:T(8,128)}, f32[12,8,...) custom-call(bf16[1024,48]{1,0:T(8,128)(2,1)} %get-tuple-element.73.rate_ref, bf16[48,1536]{1,0:T(8,128)(2,1)} %slice.108.wdt_ref, ...), custom_call_target="tpu_custom_call" | custom-call | tf_op jit(solution)/shard_map/forward_scan/pallas_call | solution.py:450
  147.2 36.0 %routed.1 = (f32[1024,768]{1,0:T(8,128)}, f32[1024,128]{1,0:T(8,128)}, bf16[4,320,768]{2,1,0:T(8,128)(2,1)}) custom-call(bf16[1024,1536]{1,0:T(8,128)(2,1)} %get-tuple-element.78.mixed_ref, bf16[1536,768]{1,0:T(8,128)(2,1)} %all-gather.4.cloned.1.call-done.wout_ref, bf16[1024,768]{1,0:T(8,128)(2,1)} %copy-done.1, f32[1,768]{1,0:T(1,128)} %reshape.194.gain_ref, ...), custom_call_target="tpu_custom_call" | custom-call | tf_op jit(solution)/shard_map/routed/pallas_call | solution.py:825
  183.2 60.4 %one_expert.1 = (bf16[1280,768]{1,0:T(8,128)(2,1)}, bf16[1280,768]{1,0:T(8,128)(2,1)}, bf16[768,3072]{1,0:T(8,128)(2,1)}, bf16[3072,768]{1,0:T(8,128)(2,1)}, f32[128,768]{1,0:T(8,128)}) custom-call(bf16[1280,768]{1,0:T(8,128)(2,1)} %bitcast.71, bf16[1280,768]{1,0:T(8,128)(2,1)} %bitcast.70, bf16[768,3072]{1,0:T(8,128)(2,1)} %bitcast.66, ...), custom_call_target="tpu_custom_call" | custom-call | tf_op jit(solution)/shard_map/one_expert/pallas_call | solution.py:738
  245.6 32.0 %collect.1 = (f32[1024,768]{1,0:T(8,128)}, bf16[1024,768]{1,0:T(8,128)(2,1)}, f32[1,768]{1,0:T(1,128)}) custom-call(bf16[4,320,768]{2,1,0:T(8,128)(2,1)} %bitcast.69, s32[1024,1]{1,0:T(8,128)} %add_select_fusion.target_ref, f32[1024,768]{1,0:T(8,128)} %get-tuple-element.85.hidden_ref, bf16[1024,768]{1,0:T(8,128)(2,1)} %copy-done.2, f32[1,768]{1,0:T(1,128)} %reshape.194.gain_ref), custom_call_target="tpu_custom_call" | custom-call | tf_op jit(solution)/shard_map/collect/pallas_call | solution.py:894
  277.7 6.1 fusion.12.mg_ref
  283.8 3.9 convolution_convert_fusion.outg_ref
  287.7 17.8 %reduce-scatter.5.cloned.1.call-done = bf16[384,768]{1,0:T(8,128)(2,1)} async-done(((bf16[3072,768]{1,0:T(8,128)(2,1)}), bf16[384,768]{1,0:T(8,128)(2,1)}) %reduce-scatter.5.cloned.1.call-update) | async-done | bytes 589840 | tf_op jit(solution)/shard_map/reduce_scatter | solution.py:1513
  305.6 145.3 %backward_scan.1 = (bf16[1024,3072]{1,0:T(8,128)(2,1)}, bf16[1024,1536]{1,0:T(8,128)(2,1)}, f32[1024,1536]{1,0:T(8,128)}, bf16[80,1536]{1,0:T(8,128)(2,1)}, bf16...) custom-call(f32[1024,1536]{1,0:T(8,128)} %fusion.12.mg_ref, ...), custom_call_target="tpu_custom_call" | custom-call | tf_op jit(solution)/shard_map/backward_scan/pallas_call | solution.py:489
  452.6 13.4 %conv_back.1 = (bf16[1024,3072]{1,0:T(8,128)(2,1)}, f32[64,1536]{1,0:T(8,128)}, bf16[96,1536]{1,0:T(8,128)(2,1)}) custom-call(f32[1024,1536]{1,0:T(8,128)} %get-tuple-element.95.cg_ref, bf16[1024,1536]{1,0:T(8,128)(2,1)} %get-tuple-element.74.conv_ref.low_ref, bf16[1024,80]{1,0:T(8,128)(2,1)} %get-tuple-element.96.mpg_ref, ...), custom_call_target="tpu_custom_call", output_to_operand_aliasing={{0}: (8, {})} | custom-call | tf_op jit(solution)/shard_map/conv_back/pallas_call | solution.py:650
  467.0 1.5 collective-permute-start
  468.5 1.8 pad_maximum_fusion.small_ref
  470.3 5.3 collective-permute-done
  475.6 1.6 fusion.proj_ref
  477.2 99.0 %finish.1 = (f32[768,768]{1,0:T(8,128)}, f32[384,768]{1,0:T(8,128)}, f32[192,384]{1,0:T(8,128)}, f32[8,128,768]{2,1,0:T(8,128)}, bf16[8,128,768]{2,1,0:T(8,128)(2,1)}, /*index=5*/f32[3072,768]{1,0:T(8,128)}) custom-call(bf16[1024,3072]{1,0:T(8,128)(2,1)} %fusion.proj_ref, bf16[1056,768]{1,0:T(8,128)(2,1)} %get-tuple-element.101.normed_ref, ...), custom_call_target="tpu_custom_call" | custom-call | tf_op jit(solution)/shard_map/finish/pallas_call | solution.py:1228
  576.2 1.3 slice.119
  577.5 1.5 slice.122
  579.1 1.4 slice_reduce_fusion
  580.4 1.3 fusion.11
  581.8 1.3 slice_bitcast_fusion.3
  583.1 1.3 slice_bitcast_fusion.2
  584.4 1.6 slice_bitcast_fusion.1
  586.0 7.5 %bitcast_convert_fusion = f32[1,768,3072]{2,1,0:T(8,128)} fusion(bf16[768,3072]{1,0:T(8,128)(2,1)} %all-gather.8.cloned.1.call-done), kind=kLoop, calls=%fused_computation | loop fusion | flops 2359296 | bytes 14155776 | tf_op jit(solution)/shard_map/broadcast_in_dim | solution.py:1573
  594.7 1.3 copy-done.9
  596.0 1.7 copy.85
  598.8 1.4 copy.86
  601.9 3.7 copy.88
  (103 shorter events, 28.5 us)
Async XLA Ops:
  7.2 140.0 %all-gather.4.cloned.1.call-start = ((), (), s32[]{:S(2)}) async-start(), calls=%async_computation.2 | async-start | bytes 2949120 | tf_op jit(solution)/shard_map/all_gather | solution.py:1463
  15.6 1.4 copy-start.3
  17.0 1.4 copy-start.4
  18.4 1.3 copy-start.5
  19.6 35.5 %copy-start.15 = (s32[8,128]{1,0:T(8,128)S(1)}, s32[8,128]{1,0:T(8,128)}, u32[]{:S(2)}) copy-start(s32[8,128]{1,0:T(8,128)} %param.21) | copy-start | bytes 12292
  19.6 35.5 %copy-start.16 = (s32[8,128]{1,0:T(8,128)S(1)}, s32[8,128]{1,0:T(8,128)}, u32[]{:S(2)}) copy-start(s32[8,128]{1,0:T(8,128)} %param.22) | copy-start | bytes 12292
  48.9 2.2 copy-start
  51.2 1.1 copy-start.1
  52.3 1.1 copy-start.2
  53.4 0.6 copy-start.6
  54.1 251.4 %reduce-scatter.5.cloned.1.call-start = ((), (), s32[]{:S(2)}) async-start(), calls=%async_computation.4 | async-start | bytes 5308416 | tf_op jit(solution)/shard_map/reduce_scatter | solution.py:1513
  243.7 1.1 copy-start.7
  243.7 207.3 %reduce-scatter.3.cloned.1.call-start = ((), (), s32[]{:S(2)}) async-start(), calls=%async_computation.3 | async-start | bytes 5308416 | tf_op jit(solution)/shard_map/reduce_scatter | solution.py:1513
  244.4 232.8 %all-gather.6.cloned.1.call-start = ((), (), s32[]{:S(2)}) async-start(), calls=%async_computation.5 | async-start | bytes 5308416 | tf_op jit(solution)/shard_map/all_gather | solution.py:1516
  245.6 32.0 %copy-start.11 = (bf16[1536,768]{1,0:T(8,128)(2,1)S(1)}, bf16[1536,768]{1,0:T(8,128)(2,1)}, u32[]{:S(2)}) copy-start(bf16[1536,768]{1,0:T(8,128)(2,1)} %all-gather.4.cloned.1.call-done.wout_ref) | copy-start | bytes 7077892
  277.6 6.1 %copy-start.8 = (bf16[1024,1536]{1,0:T(8,128)(2,1)S(1)}, bf16[1024,1536]{1,0:T(8,128)(2,1)}, u32[]{:S(2)}) copy-start(bf16[1024,1536]{1,0:T(8,128)(2,1)} %get-tuple-element.78.mixed_ref) | copy-start | bytes 9437188
  277.7 6.1 %copy-start.17 = (bf16[1024,768]{1,0:T(8,128)(2,1)S(1)}, bf16[1024,768]{1,0:T(8,128)(2,1)}, u32[]{:S(2)}) copy-start(bf16[1024,768]{1,0:T(8,128)(2,1)} %get-tuple-element.86) | copy-start | bytes 4718596
  305.5 280.5 %all-gather.8.cloned.1.call-start = ((), (), s32[]{:S(2)}) async-start(), calls=%async_computation.6 | async-start | bytes 5308416 | tf_op jit(solution)/shard_map/all_gather | solution.py:1516
  452.6 15.9 %copy-start.14 = (bf16[80,1536]{1,0:T(8,128)(2,1)S(1)}, bf16[80,1536]{1,0:T(8,128)(2,1)}, u32[]{:S(2)}) copy-start(bf16[80,1536]{1,0:T(8,128)(2,1)} %get-tuple-element.103) | copy-start | bytes 737284
  467.0 8.6 %collective-permute-start = (bf16[32,1536]{1,0:T(8,128)(2,1)S(1)}, bf16[32,1536]{1,0:T(8,128)(2,1)S(1)}, u32[]{:S(2)}, u32[]{:S(2)}) collective-permute-start(bf16[32,1536]{1,0:T(8,128)(2,1)S(1)} %slice.185), channel_id=1, source_target_pairs={{4,0},{8,4},{12,8},{16,12},{20,16},{24,20},{28,24},{5,1},{9,5},{13... | collective-permute-start | bytes 294920 | tf_op jit(solution)/shard_map/ppermute | solution.py:1413
  586.0 7.5 %copy-start.12 = (bf16[8,128,768]{2,1,0:T(8,128)(2,1)S(1)}, bf16[8,128,768]{2,1,0:T(8,128)(2,1)}, u32[]{:S(2)}) copy-start(bf16[8,128,768]{2,1,0:T(8,128)(2,1)} %get-tuple-element.147) | copy-start | bytes 4718596
  586.0 15.9 %slice-start = ((s8[9437184]{0:T(1024)(128)(4,1)}), s8[4194304]{0:T(1024)(128)(4,1)S(1)}, s32[]{:S(2)}) async-start(s8[9437184]{0:T(1024)(128)(4,1)} %bitcast.63), calls=%async_computation.7 | async-start | bytes 8388608
  586.0 15.9 %slice-start.1 = ((s8[9437184]{0:T(1024)(128)(4,1)}), s8[4194304]{0:T(1024)(128)(4,1)S(1)}, s32[]{:S(2)}) async-start(s8[9437184]{0:T(1024)(128)(4,1)} %bitcast.63), calls=%async_computation.8 | async-start | bytes 8388608
  593.5 2.5 copy-start.9
  596.0 2.8 copy-start.10
  596.0 5.9 slice-start.2
  598.8 2.1 copy-start.13
Sparse Core Ops, SparseCore 0:
  54.2 23.4 all-gather.3
  243.8 61.6 reduce-scatter.4
  307.8 60.0 reduce-scatter.2
  369.2 55.9 all-gather.5
  451.1 62.2 all-gather.7
